TPU v7x, 32 devices: a whole 2x2x4 slice. The times are simulated.
32 devices in a mesh: row: 4 (over z), col: 4 (over y, core), occ: 2 (over x).
Axes of the slice: x: 2, y: 2, z: 4, core: 2. Of those that a mesh axis runs over, the one named last changes fastest.
Arguments:
- amplitudes: bfloat16 [2, 2048, 8192], P(None, ('row', 'occ'), 'col'), may hold values from -6 to 6
- integrals: bfloat16 [2, 8192, 8192], P(None, 'row', 'col'), may hold values from -0.09375 to 0.09375
- virtual_energy: float32 [256], replicated, may hold values from 0.4 to 3
- occupied_energy: float32 [128], replicated, may hold values from -2 to -0.4
- virtual_count: int32 [8], replicated, may hold values from 16 to 32, as said below
- occupied_count: int32 [8], replicated, may hold values from 8 to 16, as said below
Outputs:
- update: float32 [2, 2048, 8192], P(None, ('col', 'occ'), 'row')
Inputs may be any that keep to these rules, and one draw needn't show every extreme that they name: `virtual_count`: orbitals in each irrep block; some irrep fills all 32 slots. `occupied_count`: orbitals in each irrep block; some irrep fills all 16 slots.
All inputs are finite; a program needn't handle non-finite values.
Results may differ from a plain program's by a relative error of at most 0.0003.
Values may be sent and summed in bfloat16 or wider, within the bound.
No kernel may reach another device: no remote copies, remote signals or barrier semaphores. Data moves between devices by JAX's collectives and lax.ppermute only.
A program may use at most 128 MiB of HBM per device.

v0:
```python
import jax
import jax.numpy as jnp
from jax import lax
from jax.sharding import PartitionSpec as P


def table_value(values_table, positions):
    places = jnp.arange(values_table.shape[0], dtype=jnp.int32)
    matches = positions[..., None] == places
    return jnp.sum(jnp.where(matches, values_table, jnp.zeros((), values_table.dtype)), axis=-1)


def is_orbital(counts, orbital, capacity):
    return orbital % capacity < table_value(counts, orbital // capacity)


def pair_orbitals(slot, group_width, capacity, sym_count):
    symmetry = jnp.arange(sym_count, dtype=jnp.int32)[:, None]
    offset = slot // group_width
    first_orb = jnp.broadcast_to(slot % group_width, (sym_count, slot.shape[0]))
    second_orb = jnp.bitwise_xor(first_orb, symmetry * capacity + offset[None, :])
    mate = offset[None, :] * group_width + second_orb
    return (first_orb, second_orb, mate)


def mirror_block(block, row_index, col_index):
    return jnp.take(jnp.take(block, row_index, axis=0), col_index, axis=1)


def on_device(
    amplitudes, integrals, virtual_energy, occupied_energy, virtual_count, occupied_count
):
    row_number = lax.axis_index("row")
    col_number = lax.axis_index("col")
    occ_number = lax.axis_index("occ")
    sym_count = amplitudes.shape[0]
    share_rows = amplitudes.shape[1]
    tile_width = amplitudes.shape[2]
    virt_slots = virtual_energy.shape[0]
    occ_slots = occupied_energy.shape[0]
    virt_cap = virt_slots // 8
    occ_cap = occ_slots // 8
    gathered = lax.all_gather(amplitudes, "row", axis=1, tiled=True)
    gathered_row = jnp.arange(gathered.shape[1], dtype=jnp.int32)
    source_slot = (
        2 * (gathered_row // share_rows) + occ_number
    ) * share_rows + gathered_row % share_rows
    first_source, second_source, _ = pair_orbitals(source_slot, occ_slots, occ_cap, sym_count)
    source_ok = is_orbital(occupied_count, first_source, occ_cap) & is_orbital(
        occupied_count, second_source, occ_cap
    )
    contract_slot = col_number * tile_width + jnp.arange(tile_width, dtype=jnp.int32)
    first_contract, second_contract, _ = pair_orbitals(
        contract_slot, virt_slots, virt_cap, sym_count
    )
    contract_ok = is_orbital(virtual_count, first_contract, virt_cap) & is_orbital(
        virtual_count, second_contract, virt_cap
    )
    masked = jnp.where(
        source_ok[:, :, None] & contract_ok[:, None, :], gathered, jnp.zeros((), gathered.dtype)
    )
    summed = lax.psum_scatter(
        jnp.einsum("sqd,spd->qsp", masked, integrals, preferred_element_type=jnp.float32),
        "col",
        scatter_dimension=0,
        tiled=True,
    )
    ladder = summed.transpose(1, 0, 2)
    row_base = (2 * col_number + occ_number) * share_rows
    output_slot = row_base + jnp.arange(share_rows, dtype=jnp.int32)
    first_occupied, second_occupied, occupied_mate = pair_orbitals(
        output_slot, occ_slots, occ_cap, sym_count
    )
    col_base = row_number * tile_width
    output_pair = col_base + jnp.arange(tile_width, dtype=jnp.int32)
    first_virtual, second_virtual, virtual_mate = pair_orbitals(
        output_pair, virt_slots, virt_cap, sym_count
    )
    mirrored = jax.vmap(mirror_block)(ladder, occupied_mate - row_base, virtual_mate - col_base)
    symmetrized = ladder + mirrored
    hole_ok = is_orbital(occupied_count, first_occupied, occ_cap) & is_orbital(
        occupied_count, second_occupied, occ_cap
    )
    pair_ok = is_orbital(virtual_count, first_virtual, virt_cap) & is_orbital(
        virtual_count, second_virtual, virt_cap
    )
    pair_energy = table_value(virtual_energy, first_virtual) + table_value(
        virtual_energy, second_virtual
    )
    hole_energy = table_value(occupied_energy, first_occupied) + table_value(
        occupied_energy, second_occupied
    )
    denominator = pair_energy[:, None, :] - hole_energy[:, :, None]
    allowed = hole_ok[:, :, None] & pair_ok[:, None, :]
    return jnp.where(allowed, symmetrized / denominator, jnp.zeros((), jnp.float32))


def solution(mesh):
    placed = (P(None, ("row", "occ"), "col"), P(None, "row", "col"), P(), P(), P(), P())
    return jax.shard_map(
        on_device,
        mesh=mesh,
        in_specs=placed,
        out_specs=P(None, ("col", "occ"), "row"),
        check_vma=False,
    )
```

profile of v0, /device:TPU:5, one launch (start us, length us, event | category | flops | bytes accessed | tf_op | source)
XLA Modules:
  0.0 419.2 jit_solution(10658456871232354747)
XLA Ops:
  6.5 0.7 all-gather.2.cloned.1.call-update
  7.6 0.1 and_select_fusion.8
  7.8 0.8 select_reduce_fusion.9
  8.5 0.1 compare_and_fusion
  8.7 0.1 and_select_fusion.4
  8.9 0.9 select_reduce_fusion.7
  9.8 0.1 compare_and_fusion.3
  9.9 0.1 compare_and_fusion.1
  10.0 150.0 %all-gather.2.cloned.1.call-done = bf16[2,1024,2048]{2,1,0:T(8,128)(2,1)} async-done(((bf16[2,256,2048]{2,1,0:T(8,128)(2,1)}), bf16[2,1024,2048]{2,1,0:T(8,128)(2,1)}) %all-gather.2.cloned.1.call-update) | async-done | bytes 8388624 | tf_op jit(solution)/shard_map/all_gather | solution.py:43
  160.0 24.7 %fusion.3 = f32[1024,2,2048]{2,0,1:T(8,128)} fusion(bf16[2,2048,2048]{2,1,0:T(8,128)(2,1)} %param.7, bf16[2,1024,2048]{2,1,0:T(8,128)(2,1)} %all-gather.2.cloned.1.call-done, pred[2,2048]{1,0:T(4,128)(4,1)S(1)} %compare_and_fusion.1, pred[2,1024]{1,0:T(4,128)(4,1)S(1)} %compare_and_fusion.3), kind=kOutput, calls=%fused_computation.6 | convolution fusion | flops 17188257792 | bytes 41949184 | tf_op jit(solution)/shard_map/sqd,spd->qsp/dot_general | solution.py:63
  184.8 0.1 fusion.42
  184.9 0.1 fusion.10
  185.0 0.1 and_select_fusion.10
  185.1 0.3 copy-done.2
  185.4 0.3 select_reduce_fusion.2
  185.8 2.4 select_reduce_fusion
  188.3 0.1 select_reduce_fusion.11
  188.4 119.6 %reduce-scatter.2.cloned.1.call-done = f32[256,2,2048]{2,0,1:T(8,128)} async-done(((f32[1024,2,2048]{2,0,1:T(8,128)}), f32[256,2,2048]{2,0,1:T(8,128)}) %reduce-scatter.2.cloned.1.call-update) | async-done | bytes 4194320 | tf_op jit(solution)/shard_map/reduce_scatter | solution.py:62
  308.1 13.2 %gather_fusion = f32[512,2048]{1,0:T(8,128)} fusion(f32[2,256,2048]{2,1,0:T(8,128)} %bitcast.21, s32[512]{0:T(512)S(1)} %bitcast.23), kind=kCustom, calls=%fused_computation | custom fusion | bytes 8392704 | tf_op jit(solution)/shard_map/vmap(jit(_take))/gather | solution.py:27
  321.3 5.4 %copy.10 = f32[2,256,2048]{1,2,0:T(8,128)} copy(f32[2,256,2048]{2,1,0:T(8,128)} %bitcast.25) | data formatting | bytes 8388608 | tf_op jit(solution)/shard_map/vmap(jit(_take))/gather | solution.py:27
  326.6 4.5 %broadcast_select_fusion = f32[2,256,2048]{1,2,0:T(8,128)} fusion(f32[2,256,2048]{1,2,0:T(8,128)} %copy.10, pred[2,256]{1,0:T(4,128)(4,1)S(1)} %get-tuple-element.22), kind=kLoop, calls=%fused_computation.15 | loop fusion | flops 1048576 | bytes 8389120 | tf_op jit(solution)/shard_map/vmap(jit(_take))/select_n | solution.py:27
  331.2 68.9 %gather_fusion.1 = f32[4096,256]{1,0:T(8,128)} fusion(f32[2,256,2048]{1,2,0:T(8,128)} %broadcast_select_fusion, s32[4096]{0:T(1024)S(1)} %bitcast.22), kind=kCustom, calls=%fused_computation.1 | custom fusion | bytes 8421376 | tf_op jit(solution)/shard_map/vmap(jit(_take))/gather | solution.py:27
  400.1 5.3 %copy.11 = f32[2,2048,256]{1,2,0:T(8,128)} copy(f32[2,2048,256]{2,1,0:T(8,128)} %bitcast.24) | data formatting | bytes 8388608 | tf_op jit(solution)/shard_map/vmap(jit(_take))/gather | solution.py:27
  405.4 7.0 %fusion.5 = f32[2,256,2048]{2,1,0:T(8,128)} fusion(f32[2,2048,256]{1,2,0:T(8,128)} %copy.11, f32[2,256]{1,0:T(2,128)S(1)} %add.480, f32[2,2048]{1,0:T(2,128)S(1)} %add.479, pred[2,2048]{1,0:T(4,128)(4,1)S(1)} %get-tuple-element.19, pred[2,2048]{1,0:T(4,128)(4,1)S(1)} %compare_and_fusion.2, pred[2,256]{1,0:T(4,128)(4,1)S(1)} %get-tuple-element.21, ...), kind=kLoop, calls=%fused_computation.9 | loop fusion | flops 6291456 | bytes 12610048 | tf_op jit(solution)/shard_map/jit(_where)/select_n | solution.py:95
  (42 shorter events, 0.6 us)
Async XLA Ops:
  6.5 153.5 %all-gather.2.cloned.1.call-start = ((), (), s32[]{:S(2)}) async-start(), calls=%async_computation.1 | async-start | bytes 10485760 | tf_op jit(solution)/shard_map/all_gather | solution.py:43
  7.3 300.8 %reduce-scatter.2.cloned.1.call-start = ((), (), s32[]{:S(2)}) async-start(), calls=%async_computation.2 | async-start | bytes 20971520 | tf_op jit(solution)/shard_map/reduce_scatter | solution.py:62
  184.7 0.7 copy-start.2
  184.7 1.0 copy-start.1
  184.7 3.5 copy-start
Sparse Core Ops, SparseCore 0:
  8.9 151.0 all-gather.1
  184.9 123.1 reduce-scatter.1
where the time goes:
time: 423 us; the launch traced here: 419 us
  waiting for transfers between devices  270 us (64%)
  local copies, waits for them, and re-layouts  93.1 us (22%)
  matrix products  24.7 us (6%)
  other arithmetic  17.4 us (4%)
  between operations  13.6 us (3%)
    all_gather x1, waiting for transfers between devices, on_device(): gathered = lax.all_gather(amplitudes, 'row', axis=1, tiled=True)  150 us
    reduce_scatter x1, waiting for transfers between devices, on_device(): lax.psum_scatter(jnp.einsum('sqd,spd->qsp', masked, integrals, preferred_...  120 us
    gather x4, local copies, waits for them, and re-layouts, mirror_block(): return jnp.take(jnp.take(block, row_index, axis=0), col_index, axis=1)  92.8 us
    dot_general x1, matrix products, on_device(): jnp.einsum('sqd,spd->qsp', masked, integrals, preferred_element_type=jnp....  24.7 us
  transfers between devices with their start and end apart: 2, of which 2 were waited for; matrix products, arithmetic and copies ran while one was open for 1% of the time, Pallas kernels for 0%

commit v1 on v0

--- a/solution.py
+++ b/solution.py
@@ -1,7 +1,15 @@
+import functools
 import jax
 import jax.numpy as jnp
 from jax import lax
+from jax.experimental import pallas as pl
+from jax.experimental.pallas import tpu as pltpu
 from jax.sharding import PartitionSpec as P
+
+F32, BF16, I32, I16 = jnp.float32, jnp.bfloat16, jnp.int32, jnp.int16
+LANES = 128
+TILE_ROWS = 16
+ANY = pl.BlockSpec(memory_space=pl.ANY)
 
 
 def table_value(values_table, positions):
@@ -27,7 +35,7 @@
     return jnp.take(jnp.take(block, row_index, axis=0), col_index, axis=1)
 
 
-def on_device(
+def on_device_general(
     amplitudes, integrals, virtual_energy, occupied_energy, virtual_count, occupied_count
 ):
     row_number = lax.axis_index("row")
@@ -95,8 +103,483 @@
     return jnp.where(allowed, symmetrized / denominator, jnp.zeros((), jnp.float32))
 
 
+class Plan:
+    def __init__(self, amp_shape, int_shape, rows, virt_slots, occ_slots):
+        self.syms, self.share, self.width = amp_shape
+        self.pairs = int_shape[1]
+        self.rows = rows
+        self.virt_slots, self.occ_slots = virt_slots, occ_slots
+        self.virt_cap, self.occ_cap = virt_slots // 8, occ_slots // 8
+        self.tiles = self.width // LANES
+        self.row_tiles = self.share // TILE_ROWS
+        self.pay_tiles = self.syms * self.tiles * self.row_tiles
+        half = self.share // 2
+        self.rep_rows = [half + self.occ_slots // 2] + [half] * (self.syms - 1)
+        self.enc_tiles = sum(self.rep_rows) // TILE_ROWS
+        self.at_ndt = 2
+        self.at_first = self.at_ndt + self.syms
+        self.at_reps = self.at_first + self.syms * self.tiles
+        self.at_self = self.at_reps + self.syms * rows
+
+
+def scalars(plan, tab, sym, share):
+    reps = tab[plan.at_reps + sym * plan.rows + share]
+    selfs = tab[plan.at_self + sym * plan.rows + share]
+    return reps, selfs, tab[plan.at_ndt + sym]
+
+
+def band(rel_row):
+    return (lax.broadcasted_iota(I32, (2 * LANES, LANES), 0) == rel_row).astype(BF16)
+
+
+def pack_kernel(plan, tab, amp, dest, rel, pay, acc):
+    pay[...] = jnp.zeros_like(pay)
+    row = tab[0]
+    base = jnp.int32(0)
+    for sym in range(plan.syms):
+        reps, selfs, ndt = scalars(plan, tab, sym, row)
+        nrt = 2 * reps + selfs
+        pick = (
+            lax.broadcasted_iota(I32, (plan.share, plan.share), 0) == dest[sym : sym + 1, :]
+        ).astype(BF16)
+        compact = jnp.dot(pick, amp[sym], preferred_element_type=F32).astype(BF16)
+        acc[...] = jnp.zeros_like(acc)
+        for tile in range(plan.tiles):
+            at = sym * plan.tiles + tile
+            placed = lax.dot_general(
+                compact[:, tile * LANES : (tile + 1) * LANES],
+                band(rel[at : at + 1, :]),
+                (((1,), (1,)), ((), ())),
+                preferred_element_type=F32,
+            )
+            first = tab[plan.at_first + at]
+            acc[first] += placed[:, :LANES]
+            acc[first + 1] += placed[:, LANES:]
+
+        def put(tile, _, base=base, nrt=nrt):
+            start = pl.multiple_of((base + tile * nrt) * TILE_ROWS, TILE_ROWS)
+            pay[pl.ds(start, plan.share), :] = acc[tile].astype(BF16)
+            return 0
+
+        lax.fori_loop(0, ndt, put, 0)
+        base = base + nrt * ndt
+
+
+def pack(plan, tab, amp, dest, rel):
+    pay_rows = plan.pay_tiles * TILE_ROWS + plan.share
+    vm = pl.BlockSpec(memory_space=pltpu.VMEM)
+    return pl.pallas_call(
+        functools.partial(pack_kernel, plan),
+        out_shape=jax.ShapeDtypeStruct((pay_rows, LANES), BF16),
+        in_specs=[pl.BlockSpec(memory_space=pltpu.SMEM), vm, vm, vm],
+        out_specs=vm,
+        scratch_shapes=[pltpu.VMEM((plan.tiles + 1, plan.share, LANES), F32)],
+        compiler_params=pltpu.CompilerParams(vmem_limit_bytes=40 << 20),
+        name="pack",
+    )(tab, amp, dest, rel)
+
+
+def share_of(plan, row, kind):
+    step, side = kind
+    if step == 0:
+        return row, row >= 0
+    if side == "right":
+        return row - step, row >= step
+    if side == "left":
+        return row + step, row + step < plan.rows
+    share = jnp.where(row >= plan.rows // 2, row - step, row + step)
+    return share, (share >= 0) & (share < plan.rows)
+
+
+def lane_mates(plan, rows, sym, fbase, tile):
+    flip = sym * plan.virt_cap + fbase + (tile * LANES) // plan.virt_slots
+    return lax.broadcasted_iota(I32, (rows, LANES), 1) ^ flip
+
+
+def lane_take(x, index):
+    return jnp.take_along_axis(x, index, axis=1)
+
+
+def ladder_kernel(plan, kind, pay_rows, enc_rows, ptile, tab, rel, *refs):
+    pays, (ints, out, pay, dense, prod, enc, sem) = refs[:-7], refs[-7:]
+    sym, pt = pl.program_id(0), pl.program_id(1)
+    steps = plan.pairs // ptile
+    row = tab[0]
+    share, active = share_of(plan, row, kind)
+
+    @pl.when(active & (sym == 0) & (pt == 0))
+    def _():
+        if len(pays) == 1:
+            copy = pltpu.make_async_copy(pays[0], pay.at[pl.ds(0, pay_rows)], sem)
+            copy.start()
+            copy.wait()
+        else:
+            upper = row >= plan.rows // 2
+
+            @pl.when(upper)
+            def _():
+                copy = pltpu.make_async_copy(pays[0], pay.at[pl.ds(0, pay_rows)], sem)
+                copy.start()
+                copy.wait()
+
+            @pl.when(jnp.logical_not(upper))
+            def _():
+                copy = pltpu.make_async_copy(pays[1], pay.at[pl.ds(0, pay_rows)], sem)
+                copy.start()
+                copy.wait()
+
+    @pl.when(active)
+    def _():
+        reps, selfs, ndt = scalars(plan, tab, sym, share)
+        nrt = 2 * reps + selfs
+
+        @pl.when(pt == 0)
+        def _():
+            reps0, selfs0, ndt0 = scalars(plan, tab, 0, share)
+            base = jnp.where(sym == 0, 0, (2 * reps0 + selfs0) * ndt0)
+            for tile in range(plan.tiles):
+                at = sym * plan.tiles + tile
+                first = tab[plan.at_first + at]
+                parts = []
+                for step in range(2):
+                    use = jnp.maximum(jnp.minimum(first + step, ndt - 1), 0)
+                    start = pl.multiple_of((base + use * nrt) * TILE_ROWS, TILE_ROWS)
+                    parts.append(pay[pl.ds(start, plan.share), :])
+                dense[:, tile * LANES : (tile + 1) * LANES] = jnp.dot(
+                    jnp.concatenate(parts, axis=1),
+                    band(rel[pl.ds(at, 1), :]),
+                    preferred_element_type=F32,
+                ).astype(BF16)
+
+        product = lax.dot_general(
+            dense[...], ints[0], (((1,), (1,)), ((), ())), preferred_element_type=F32
+        )
+        prod[:, pl.ds(pl.multiple_of(pt * ptile, ptile), ptile)] = product
+
+        @pl.when(pt == steps - 1)
+        def _():
+            reps0, selfs0, _ = scalars(plan, tab, 0, share)
+            enc_base = jnp.where(sym == 0, 0, reps0 + selfs0)
+            fbase = row * (plan.pairs // plan.virt_slots)
+
+            def chunk(k, _):
+                mate_row = pl.multiple_of((k + reps) * TILE_ROWS, TILE_ROWS)
+                own_row = pl.multiple_of(
+                    jnp.where(k < reps, k, k + reps) * TILE_ROWS, TILE_ROWS
+                )
+                to_row = pl.multiple_of((enc_base + k) * TILE_ROWS, TILE_ROWS)
+                sums, top = [], None
+                for v in range(plan.pairs // LANES):
+                    lanes = slice(v * LANES, (v + 1) * LANES)
+                    mirrored = lane_take(
+                        prod[pl.ds(mate_row, TILE_ROWS), lanes],
+                        lane_mates(plan, TILE_ROWS, sym, fbase, v),
+                    )
+                    both = prod[pl.ds(own_row, TILE_ROWS), lanes] + mirrored
+                    sums.append(both)
+                    top = jnp.abs(both) if top is None else jnp.maximum(top, jnp.abs(both))
+                peak = jnp.maximum(jnp.max(top, axis=1, keepdims=True), 1e-30)
+                power = jnp.floor(jnp.log2(32000.0 / peak))
+                scale = jnp.exp2(power)
+                for v, both in enumerate(sums):
+                    enc[pl.ds(to_row, TILE_ROWS), v * LANES : (v + 1) * LANES] = (
+                        jnp.round(both * scale).astype(I32).astype(I16)
+                    )
+                enc[pl.ds(to_row, TILE_ROWS), plan.pairs :] = (
+                    jnp.broadcast_to(power, (TILE_ROWS, LANES)).astype(I32).astype(I16)
+                )
+                return 0
+
+            lax.fori_loop(0, reps + selfs, chunk, 0)
+
+    @pl.when(active & (sym == plan.syms - 1) & (pt == steps - 1))
+    def _():
+        copy = pltpu.make_async_copy(enc.at[pl.ds(0, enc_rows)], out, sem)
+        copy.start()
+        copy.wait()
+
+
+def ladder_call(plan, kind, tab, rel, pays, integrals, enc_rows):
+    ptile = min(512, plan.pairs)
+    pay_rows = pays[0].shape[0]
+
+    def int_block(sym, pt, tab):
+        _, active = share_of(plan, tab[0], kind)
+        use = active.astype(I32)
+        return (sym * use, pt * use, 0)
+
+    grid_spec = pltpu.PrefetchScalarGridSpec(
+        num_scalar_prefetch=1,
+        grid=(plan.syms, plan.pairs // ptile),
+        in_specs=[pl.BlockSpec(rel.shape, lambda sym, pt, tab: (0, 0))]
+        + [ANY] * len(pays)
+        + [pl.BlockSpec((1, ptile, plan.width), int_block)],
+        out_specs=ANY,
+        scratch_shapes=[
+            pltpu.VMEM((plan.pay_tiles * TILE_ROWS + plan.share, LANES), BF16),
+            pltpu.VMEM((plan.share, plan.width), BF16),
+            pltpu.VMEM((plan.share, plan.pairs), F32),
+            pltpu.VMEM((plan.enc_tiles * TILE_ROWS, plan.pairs + LANES), I16),
+            pltpu.SemaphoreType.DMA,
+        ],
+    )
+    return pl.pallas_call(
+        functools.partial(ladder_kernel, plan, kind, pay_rows, enc_rows, ptile),
+        out_shape=jax.ShapeDtypeStruct((enc_rows, plan.pairs + LANES), I16),
+        grid_spec=grid_spec,
+        compiler_params=pltpu.CompilerParams(
+            dimension_semantics=("arbitrary", "arbitrary"), vmem_limit_bytes=48 << 20
+        ),
+        cost_estimate=pl.CostEstimate(
+            flops=2 * plan.syms * plan.share * plan.width * plan.pairs,
+            bytes_accessed=2 * plan.syms * plan.width * plan.pairs,
+            transcendentals=0,
+        ),
+        name="ladder",
+    )(tab, rel, *pays, integrals)
+
+
+def finish_kernel(plan, enc_rows, wtile, tab, line, hole, pair, pair_ok, *refs):
+    sources, (out, held, sems) = refs[:-3], refs[-3:]
+    step = pl.program_id(0)
+    row, col = tab[0], tab[1]
+    away = jnp.abs(row - col)
+    which = jnp.where(away == 0, 0, jnp.where(away == 1, jnp.where(col < row, 1, 2), away + 1))
+
+    @pl.when(step == 0)
+    def _():
+        for number in range(len(sources) // 4):
+
+            @pl.when(which == number)
+            def _():
+                copies = [
+                    pltpu.make_async_copy(
+                        sources[4 * number + part],
+                        held.at[part, pl.ds(0, enc_rows)],
+                        sems.at[part],
+                    )
+                    for part in range(4)
+                ]
+                for copy in copies:
+                    copy.start()
+                for copy in copies:
+                    copy.wait()
+
+    fbase = row * (plan.pairs // plan.virt_slots) + step * (wtile // plan.virt_slots)
+    enc_base = jnp.int32(0)
+    for sym in range(plan.syms):
+        reps, selfs, _ = scalars(plan, tab, sym, col)
+        count = plan.rep_rows[sym]
+        rows = pl.ds(pl.multiple_of(enc_base * TILE_ROWS, TILE_ROWS), count)
+        enc_base = enc_base + reps + selfs
+        live = lax.broadcasted_iota(I32, (count, LANES), 0) < (reps + selfs) * TILE_ROWS
+        scales = [
+            jnp.exp2(-held[part, rows, pl.ds(plan.pairs, LANES)].astype(I32).astype(F32))
+            for part in range(4)
+        ]
+        own, mates = [], []
+        for v in range(wtile // LANES):
+            lanes = pl.ds(pl.multiple_of(step * wtile + v * LANES, LANES), LANES)
+            total = None
+            for part in range(4):
+                term = held[part, rows, lanes].astype(I32).astype(F32) * scales[part]
+                total = term if total is None else total + term
+            total = jnp.where(live, total, 0.0)
+            own.append(total)
+            mates.append(lane_take(total, lane_mates(plan, count, sym, fbase, v)))
+        both = jnp.concatenate(
+            [jnp.concatenate(own, axis=1), jnp.concatenate(mates, axis=1)], axis=0
+        )
+        pick = (
+            lax.broadcasted_iota(I32, (plan.share, 2 * count), 1) == line[sym]
+        ).astype(BF16)
+        result = None
+        rest = both
+        for _ in range(3):
+            term = rest.astype(BF16)
+            rest = rest - term.astype(F32)
+            part = jnp.dot(pick, term, preferred_element_type=F32)
+            result = part if result is None else result + part
+        allowed = (line[sym] >= 0) & (pair_ok[sym] > 0)
+        out[sym] = jnp.where(allowed, result / (pair[sym] - hole[sym]), 0.0)
+
+
+def finish(plan, tab, line, hole, pair, pair_ok, sources):
+    enc_rows = sources[0].shape[0]
+    wtile = min(256, plan.pairs)
+    whole = lambda shape: pl.BlockSpec(shape, lambda i, tab: (0,) * len(shape))
+    tiled = pl.BlockSpec((plan.syms, 1, wtile), lambda i, tab: (0, 0, i))
+    grid_spec = pltpu.PrefetchScalarGridSpec(
+        num_scalar_prefetch=1,
+        grid=(plan.pairs // wtile,),
+        in_specs=[whole(line.shape), whole(hole.shape), tiled, tiled] + [ANY] * len(sources),
+        out_specs=pl.BlockSpec((plan.syms, plan.share, wtile), lambda i, tab: (0, 0, i)),
+        scratch_shapes=[
+            pltpu.VMEM((4, plan.enc_tiles * TILE_ROWS, plan.pairs + LANES), I16),
+            pltpu.SemaphoreType.DMA((4,)),
+        ],
+    )
+    return pl.pallas_call(
+        functools.partial(finish_kernel, plan, enc_rows, wtile),
+        out_shape=jax.ShapeDtypeStruct((plan.syms, plan.share, plan.pairs), F32),
+        grid_spec=grid_spec,
+        compiler_params=pltpu.CompilerParams(
+            dimension_semantics=("arbitrary",), vmem_limit_bytes=48 << 20
+        ),
+        name="finish",
+    )(tab, line, hole, pair, pair_ok, *sources)
+
+
+def occupied_share(plan, counts, share_number):
+    slot = share_number * plan.share + jnp.arange(plan.share, dtype=I32)
+    first, second, mate = pair_orbitals(slot, plan.occ_slots, plan.occ_cap, plan.syms)
+    ok = is_orbital(counts, first, plan.occ_cap) & is_orbital(counts, second, plan.occ_cap)
+    lead = jnp.minimum(slot[None, :], mate)
+    is_rep = ok & (first < second)
+    is_self = ok & (first == second)
+    before = slot[None, None, :] < lead[:, :, None]
+    rank = jnp.sum((is_rep[:, None, :] & before).astype(I32), axis=-1)
+    self_rank = jnp.sum((is_self[:, None, :] & before).astype(I32), axis=-1)
+    return first, second, ok, is_rep, is_self, rank, self_rank
+
+
+def padded(count):
+    return (count + TILE_ROWS - 1) // TILE_ROWS
+
+
+def line_tables(plan, virtual_energy, occupied_energy, virtual_count, occupied_count):
+    row = lax.axis_index("row")
+    col = lax.axis_index("col")
+    occ = lax.axis_index("occ")
+    syms = plan.syms
+    slots = jnp.arange(2 * plan.rows * plan.share, dtype=I32)
+    first, second, _ = pair_orbitals(slots, plan.occ_slots, plan.occ_cap, syms)
+    ok = is_orbital(occupied_count, first, plan.occ_cap) & is_orbital(
+        occupied_count, second, plan.occ_cap
+    )
+    grouped = lambda x: jnp.sum(x.astype(I32).reshape(syms, plan.rows, 2, plan.share), axis=-1)
+    reps_all = padded(grouped(ok & (first < second)))
+    selfs_all = padded(grouped(ok & (first == second)))
+    reps = jnp.where(occ == 0, reps_all[:, :, 0], reps_all[:, :, 1])
+    selfs = jnp.where(occ == 0, selfs_all[:, :, 0], selfs_all[:, :, 1])
+    slot = col * plan.width + jnp.arange(plan.width, dtype=I32)
+    first, second, _ = pair_orbitals(slot, plan.virt_slots, plan.virt_cap, syms)
+    ok = is_orbital(virtual_count, first, plan.virt_cap) & is_orbital(
+        virtual_count, second, plan.virt_cap
+    )
+    ok = ok.reshape(syms, plan.tiles, LANES)
+    per_tile = jnp.sum(ok.astype(I32), axis=-1)
+    tile_ids = jnp.arange(plan.tiles, dtype=I32)
+    starts = jnp.sum(
+        jnp.where(tile_ids[None, None, :] < tile_ids[None, :, None], per_tile[:, None, :], 0), axis=-1
+    )
+    lane_ids = jnp.arange(LANES, dtype=I32)
+    within = jnp.sum(
+        (ok[:, :, None, :] & (lane_ids[None, :] < lane_ids[:, None])).astype(I32), axis=-1
+    )
+    firsts = starts // LANES
+    rel = jnp.where(ok, within + (starts % LANES)[:, :, None], -1)
+    ndt = (jnp.sum(per_tile, axis=-1) + LANES - 1) // LANES
+    tab = jnp.concatenate(
+        [jnp.stack([row, col]).astype(I32), ndt, firsts.reshape(-1), reps.reshape(-1), selfs.reshape(-1)]
+    )
+    _, _, ok, is_rep, is_self, rank, self_rank = occupied_share(
+        plan, occupied_count, 2 * row + occ
+    )
+    n_rep = padded(jnp.sum(is_rep.astype(I32), axis=-1, keepdims=True)) * TILE_ROWS
+    dest = jnp.where(is_self, 2 * n_rep + self_rank, jnp.where(is_rep, rank, n_rep + rank))
+    dest = jnp.where(ok, dest, -1)
+    first, second, ok, is_rep, is_self, rank, self_rank = occupied_share(
+        plan, occupied_count, 2 * col + occ
+    )
+    n_rep = padded(jnp.sum(is_rep.astype(I32), axis=-1, keepdims=True)) * TILE_ROWS
+    count = jnp.array(plan.rep_rows, I32)[:, None]
+    line = jnp.where(is_self, n_rep + self_rank, jnp.where(is_rep, rank, count + rank))
+    line = jnp.where(ok, line, -1)
+    hole = table_value(occupied_energy, first) + table_value(occupied_energy, second)
+    slot = row * plan.pairs + jnp.arange(plan.pairs, dtype=I32)
+    first, second, _ = pair_orbitals(slot, plan.virt_slots, plan.virt_cap, syms)
+    pair_ok = is_orbital(virtual_count, first, plan.virt_cap) & is_orbital(
+        virtual_count, second, plan.virt_cap
+    )
+    pair = table_value(virtual_energy, first) + table_value(virtual_energy, second)
+    return (
+        tab,
+        dest,
+        rel.reshape(syms * plan.tiles, LANES),
+        line[:, :, None],
+        hole[:, :, None],
+        pair[:, None, :],
+        pair_ok.astype(I32)[:, None, :],
+    )
+
+
+def send_to_roots(plan, enc, kind):
+    received = []
+    for flip in range(1, plan.rows):
+        pairs = []
+        for row in range(plan.rows):
+            step, side = kind
+            if side == "right":
+                root = row - step
+            elif side == "left":
+                root = row + step
+            else:
+                root = row - step if row >= plan.rows // 2 else row + step
+            if 0 <= root < plan.rows:
+                pairs.append((row * plan.rows + (root ^ flip), row * plan.rows + root))
+        received.append(lax.ppermute(enc, ("row", "col"), pairs))
+    return received
+
+
+def line_body(plan, pay_tiles, enc_tiles, tables, packed, integrals):
+    tab, rel, line, hole, pair, pair_ok = tables
+    enc_rows = enc_tiles * TILE_ROWS
+    pay = packed[: pay_tiles * TILE_ROWS]
+    n = plan.rows
+    sources = []
+
+    def work(kind, pays):
+        enc = ladder_call(plan, kind, tab, rel, pays, integrals, enc_rows)
+        sources.extend([enc] + send_to_roots(plan, enc, kind))
+
+    rights, lefts = [pay], [pay]
+    for step in range(1, n):
+        rights.append(
+            lax.ppermute(rights[-1], "row", [(i, i + 1) for i in range(step - 1, n - 1)])
+        )
+        lefts.append(
+            lax.ppermute(lefts[-1], "row", [(i + 1, i) for i in range(0, n - step)])
+        )
+    work((0, ""), [pay])
+    work((1, "right"), [rights[1]])
+    work((1, "left"), [lefts[1]])
+    for step in range(2, n):
+        work((step, ""), [rights[step], lefts[step]])
+    return finish(plan, tab, line, hole, pair, pair_ok, sources)
+
+
+def on_device_line(
+    rows, amplitudes, integrals, virtual_energy, occupied_energy, virtual_count, occupied_count
+):
+    plan = Plan(
+        amplitudes.shape, integrals.shape, rows, virtual_energy.shape[0], occupied_energy.shape[0]
+    )
+    tab, dest, rel, *rest = line_tables(
+        plan, virtual_energy, occupied_energy, virtual_count, occupied_count
+    )
+    packed = pack(plan, tab, amplitudes, dest, rel)
+    return line_body(
+        plan, plan.pay_tiles, plan.enc_tiles, (tab, rel, *rest), packed, integrals
+    )
+
+
 def solution(mesh):
+    rows, cols = mesh.shape["row"], mesh.shape["col"]
     placed = (P(None, ("row", "occ"), "col"), P(None, "row", "col"), P(), P(), P(), P())
+    on_device = on_device_general
+    if rows == 4 and cols == 4:
+        on_device = functools.partial(on_device_line, rows)
     return jax.shard_map(
         on_device,
         mesh=mesh,

time: 423 us -> 260 us (0.61)
  the two profiles are of different devices: /device:TPU:5 before, /device:TPU:16 now
where the time goes in v1:
time: 260 us
  waiting for transfers between devices  115 us (44%)
  Pallas kernels  76.3 us (29%)
  starting transfers between devices  45.3 us (17%)
  other arithmetic  13.3 us (5%)
  local copies, waits for them, and re-layouts  9.34 us (4%)
    ppermute x3, waiting for transfers between devices, line_body(): lax.ppermute(lefts[-1], 'row', [(i + 1, i) for i in range(0, n - step)])  63.4 us
    pallas_call x5, Pallas kernels, ladder_call(): pl.pallas_call(functools.partial(ladder_kernel, plan, kind, pay_rows, enc...  62.3 us
    ppermute x15, waiting for transfers between devices, send_to_roots(): received.append(lax.ppermute(enc, ('row', 'col'), pairs))  46.4 us
    ppermute x15, starting transfers between devices, send_to_roots(): received.append(lax.ppermute(enc, ('row', 'col'), pairs))  30.6 us
    pallas_call x1, Pallas kernels, finish(): pl.pallas_call(functools.partial(finish_kernel, plan, enc_rows, wtile), o...  10.6 us
    ppermute x3, starting transfers between devices, line_body(): lax.ppermute(rights[-1], 'row', [(i, i + 1) for i in range(step - 1, n -...  7.95 us
    ppermute x3, starting transfers between devices, line_body(): lax.ppermute(lefts[-1], 'row', [(i + 1, i) for i in range(0, n - step)])  6.81 us
    reduce_sum x5, other arithmetic, table_value(): jnp.sum(jnp.where(matches, values_table, jnp.zeros((), values_table.dtype...  6.38 us
  transfers between devices with their start and end apart: 21, of which 4 were waited for; matrix products, arithmetic and copies ran while one was open for 3% of the time, Pallas kernels for 24%

profile of v1, /device:TPU:16, one launch (start us, length us, event | category | flops | bytes accessed | tf_op | source)
XLA Modules:
  0.0 260.0 jit_solution(4659416424014801933)
XLA Ops:
  10.4 3.4 %pack.1 = bf16[8448,128]{1,0:T(8,128)(2,1)S(1)} custom-call(s32[52]{0:T(128)S(1)} %concatenate.3.tab, bf16[2,256,2048]{2,1,0:T(8,128)(2,1)S(1)} %copy-done.10, s32[2,256]{1,0:T(2,128)S(1)} %fusion.55.dest, s32[32,128]{1,0:T(8,128)S(1)} %fusion.16.rel), custom_call_target="tpu_custom_call" | custom-call | tf_op jit(solution)/shard_map/pack/pallas_call | solution.py:171
  14.0 2.4 collective-permute-start.7
  16.4 3.6 %collective-permute-start.3 = (bf16[8192,128]{1,0:T(8,128)(2,1)S(1)}, bf16[8192,128]{1,0:T(8,128)(2,1)S(1)}, u32[]{:S(2)}, u32[]{:S(2)}) collective-permute-start(bf16[8192,128]{1,0:T(8,128)(2,1)S(1)} %slice.24.refs_0_), channel_id=1, source_target_pairs={{0,8},{8,16},{16,24},{1,9},{9,17},{17,25},{2,10},{10,18},{18,26},{... | collective-permute-start | bytes 6291464 | tf_op jit(solution)/shard_map/ppermute | solution.py:549
  20.0 43.3 %collective-permute-done.7.refs_0_ = bf16[8192,128]{1,0:T(8,128)(2,1)S(1)} collective-permute-done((bf16[8192,128]{1,0:T(8,128)(2,1)S(1)}, bf16[8192,128]{1,0:T(8,128)(2,1)S(1)}, u32[]{:S(2)}, u32[]{:S(2)}) %collective-permute-start.7) | collective-permute-done | bytes 2097184 | tf_op jit(solution)/shard_map/ppermute | solution.py:552
  63.3 3.7 %collective-permute-start.12 = (bf16[8192,128]{1,0:T(8,128)(2,1)S(1)}, bf16[8192,128]{1,0:T(8,128)(2,1)}, u32[]{:S(2)}, u32[]{:S(2)}) collective-permute-start(bf16[8192,128]{1,0:T(8,128)(2,1)S(1)} %collective-permute-done.7.refs_0_), channel_id=1, source_target_pairs={{8,0},{16,8},{9,1},{17,9},{10,2},{18,10},{11,3},{19,11},{12,4},{20... | collective-permute-start | bytes 6291464 | tf_op jit(solution)/shard_map/ppermute | solution.py:552
  66.9 2.0 collective-permute-start.11
  69.0 14.5 %ladder.5.refs_0_ = s16[320,2176]{1,0:T(8,128)(2,1)S(1)} custom-call(s32[52]{0:T(128)S(1)} %concatenate.3.tab, s32[32,128]{1,0:T(8,128)S(1)} %fusion.16.rel, bf16[8192,128]{1,0:T(8,128)(2,1)S(1)} %slice.24.refs_0_, bf16[2,2048,2048]{2,1,0:T(8,128)(2,1)} %refs_2_.3), custom_call_target="tpu_custom_call" | custom-call | flops 4294967296 | bytes 16777216 | tf_op jit(solution)/shard_map/ladder/pallas_call | solution.py:326
  84.3 5.2 %collective-permute-start.1 = (s16[320,2176]{1,0:T(8,128)(2,1)S(1)}, s16[320,2176]{1,0:T(8,128)(2,1)}, u32[]{:S(2)}, u32[]{:S(2)}) collective-permute-start(s16[320,2176]{1,0:T(8,128)(2,1)S(1)} %ladder.5.refs_0_), channel_id=1, source_target_pairs={{4,0},{14,10},{16,20},{26,30},{5,1},{15,11},{17,21},{27,31}} | collective-permute-start | bytes 4177928 | tf_op jit(solution)/shard_map/ppermute | solution.py:531
  89.4 20.2 %collective-permute-done.12.refs_1_ = bf16[8192,128]{1,0:T(8,128)(2,1)} collective-permute-done((bf16[8192,128]{1,0:T(8,128)(2,1)S(1)}, bf16[8192,128]{1,0:T(8,128)(2,1)}, u32[]{:S(2)}, u32[]{:S(2)}) %collective-permute-start.12) | collective-permute-done | bytes 2097184 | tf_op jit(solution)/shard_map/ppermute | solution.py:552
  110.4 4.6 %collective-permute-done.11.refs_0_ = bf16[8192,128]{1,0:T(8,128)(2,1)S(1)} collective-permute-done((bf16[8192,128]{1,0:T(8,128)(2,1)S(1)}, bf16[8192,128]{1,0:T(8,128)(2,1)S(1)}, u32[]{:S(2)}, u32[]{:S(2)}) %collective-permute-start.11) | collective-permute-done | bytes 2097184 | tf_op jit(solution)/shard_map/ppermute | solution.py:549
  115.0 2.3 collective-permute-start.16
  117.4 1.8 collective-permute-start
  120.7 14.5 %ladder.7.refs_8_ = s16[320,2176]{1,0:T(8,128)(2,1)S(1)} custom-call(s32[52]{0:T(128)S(1)} %concatenate.3.tab, s32[32,128]{1,0:T(8,128)S(1)} %fusion.16.rel, bf16[8192,128]{1,0:T(8,128)(2,1)S(1)} %copy-done.9, bf16[2,2048,2048]{2,1,0:T(8,128)(2,1)} %refs_2_.3), custom_call_target="tpu_custom_call" | custom-call | flops 4294967296 | bytes 16777216 | tf_op jit(solution)/shard_map/ladder/pallas_call | solution.py:326
  136.4 4.9 %collective-permute-start.10 = (s16[320,2176]{1,0:T(8,128)(2,1)S(1)}, s16[320,2176]{1,0:T(8,128)(2,1)S(1)}, u32[]{:S(2)}, u32[]{:S(2)}) collective-permute-start(s16[320,2176]{1,0:T(8,128)(2,1)S(1)} %ladder.7.refs_8_), channel_id=1, source_target_pairs={{4,2},{10,12},{16,22},{5,3},{11,13},{17,23}} | collective-permute-start | bytes 4177928 | tf_op jit(solution)/shard_map/ppermute | solution.py:531
  141.2 1.8 collective-permute-start.9
  143.0 15.0 %ladder.6.refs_4_ = s16[320,2176]{1,0:T(8,128)(2,1)S(1)} custom-call(s32[52]{0:T(128)S(1)} %concatenate.3.tab, s32[32,128]{1,0:T(8,128)S(1)} %fusion.16.rel, bf16[8192,128]{1,0:T(8,128)(2,1)S(1)} %copy-done.7, bf16[2,2048,2048]{2,1,0:T(8,128)(2,1)} %refs_2_.3), custom_call_target="tpu_custom_call" | custom-call | flops 4294967296 | bytes 16777216 | tf_op jit(solution)/shard_map/ladder/pallas_call | solution.py:326
  158.1 16.2 %ladder.8.refs_12_ = s16[320,2176]{1,0:T(8,128)(2,1)S(1)} custom-call(s32[52]{0:T(128)S(1)} %concatenate.3.tab, s32[32,128]{1,0:T(8,128)S(1)} %fusion.16.rel, bf16[8192,128]{1,0:T(8,128)(2,1)S(1)} %collective-permute-done.11.refs_0_, bf16[8192,128]{1,0:T(8,128)(2,1)} %collective-permute-done.12.refs_1_, bf16[2,2048,2048]{2,1,0:T(8,128)(2,1)} %refs_2_.3), custom_call_target="tpu_custom_call" | custom-call | flops 4294967296 | bytes 16777216 | tf_op jit(solution)/shard_map/ladder/pallas_call | solution.py:326
  176.6 4.8 %collective-permute-start.4 = (s16[320,2176]{1,0:T(8,128)(2,1)S(1)}, s16[320,2176]{1,0:T(8,128)(2,1)}, u32[]{:S(2)}, u32[]{:S(2)}) collective-permute-start(s16[320,2176]{1,0:T(8,128)(2,1)S(1)} %ladder.6.refs_4_), channel_id=1, source_target_pairs={{10,8},{16,18},{30,28},{11,9},{17,19},{31,29}} | collective-permute-start | bytes 4177928 | tf_op jit(solution)/shard_map/ppermute | solution.py:531
  183.3 2.4 select_reduce_fusion
  185.7 2.2 ladder.9.refs_16_
  192.4 1.8 collective-permute-start.19
  194.2 46.4 %collective-permute-done.15.refs_15_ = s16[320,2176]{1,0:T(8,128)(2,1)} collective-permute-done((s16[320,2176]{1,0:T(8,128)(2,1)S(1)}, s16[320,2176]{1,0:T(8,128)(2,1)}, u32[]{:S(2)}, u32[]{:S(2)}) %collective-permute-start.15) | collective-permute-done | bytes 1392672 | tf_op jit(solution)/shard_map/ppermute | solution.py:531
  240.6 1.8 collective-permute-start.18
  249.2 10.6 %finish.1 = f32[2,256,2048]{2,1,0:T(8,128)} custom-call(s32[52]{0:T(128)S(1)} %concatenate.3.tab, s32[2,256,1]{2,1,0:T(8,128)S(1)} %fusion.3.line, f32[2,256,1]{2,1,0:T(8,128)S(1)} %copy.27.hole, f32[2,1,2048]{2,1,0:T(1,128)S(1)} %add.729.pair, s32[2,1,2048]{2,1,0:T(1,128)S(1)} %and_convert_fusion.pair_ok, s16[320,2176]{1,0:T(8,128)(2,1)S(1)} %copy-done.3, ...), custom_call_target="tpu_custom_call" | custom-call | tf_op jit(solution)/shard_map/finish/pallas_call | solution.py:422
  (190 shorter events, 29.7 us)
Async XLA Ops:
  14.0 49.3 %collective-permute-start.7 = (bf16[8192,128]{1,0:T(8,128)(2,1)S(1)}, bf16[8192,128]{1,0:T(8,128)(2,1)S(1)}, u32[]{:S(2)}, u32[]{:S(2)}) collective-permute-start(bf16[8192,128]{1,0:T(8,128)(2,1)S(1)} %slice.24.refs_0_), channel_id=1, source_target_pairs={{8,0},{16,8},{24,16},{9,1},{17,9},{25,17},{10,2},{18,10},{26,18},{... | collective-permute-start | bytes 6291464 | tf_op jit(solution)/shard_map/ppermute | solution.py:552
  16.4 50.6 %collective-permute-start.3 = (bf16[8192,128]{1,0:T(8,128)(2,1)S(1)}, bf16[8192,128]{1,0:T(8,128)(2,1)S(1)}, u32[]{:S(2)}, u32[]{:S(2)}) collective-permute-start(bf16[8192,128]{1,0:T(8,128)(2,1)S(1)} %slice.24.refs_0_), channel_id=1, source_target_pairs={{0,8},{8,16},{16,24},{1,9},{9,17},{17,25},{2,10},{10,18},{18,26},{... | collective-permute-start | bytes 6291464 | tf_op jit(solution)/shard_map/ppermute | solution.py:549
  63.3 46.3 %collective-permute-start.12 = (bf16[8192,128]{1,0:T(8,128)(2,1)S(1)}, bf16[8192,128]{1,0:T(8,128)(2,1)}, u32[]{:S(2)}, u32[]{:S(2)}) collective-permute-start(bf16[8192,128]{1,0:T(8,128)(2,1)S(1)} %collective-permute-done.7.refs_0_), channel_id=1, source_target_pairs={{8,0},{16,8},{9,1},{17,9},{10,2},{18,10},{11,3},{19,11},{12,4},{20... | collective-permute-start | bytes 6291464 | tf_op jit(solution)/shard_map/ppermute | solution.py:552
  66.9 48.1 %collective-permute-start.11 = (bf16[8192,128]{1,0:T(8,128)(2,1)S(1)}, bf16[8192,128]{1,0:T(8,128)(2,1)S(1)}, u32[]{:S(2)}, u32[]{:S(2)}) collective-permute-start(bf16[8192,128]{1,0:T(8,128)(2,1)S(1)} %collective-permute-done.3.refs_0_), channel_id=1, source_target_pairs={{8,16},{16,24},{9,17},{17,25},{10,18},{18,26},{11,19},{19,27},{12,... | collective-permute-start | bytes 6291464 | tf_op jit(solution)/shard_map/ppermute | solution.py:549
  83.5 51.8 %collective-permute-start.2 = (s16[320,2176]{1,0:T(8,128)(2,1)S(1)}, s16[320,2176]{1,0:T(8,128)(2,1)S(1)}, u32[]{:S(2)}, u32[]{:S(2)}) collective-permute-start(s16[320,2176]{1,0:T(8,128)(2,1)S(1)} %ladder.5.refs_0_), channel_id=1, source_target_pairs={{6,0},{12,10},{18,20},{24,30},{7,1},{13,11},{19,21},{25,31}} | collective-permute-start | bytes 4177928 | tf_op jit(solution)/shard_map/ppermute | solution.py:531
  84.3 57.0 %collective-permute-start.1 = (s16[320,2176]{1,0:T(8,128)(2,1)S(1)}, s16[320,2176]{1,0:T(8,128)(2,1)}, u32[]{:S(2)}, u32[]{:S(2)}) collective-permute-start(s16[320,2176]{1,0:T(8,128)(2,1)S(1)} %ladder.5.refs_0_), channel_id=1, source_target_pairs={{4,0},{14,10},{16,20},{26,30},{5,1},{15,11},{17,21},{27,31}} | collective-permute-start | bytes 4177928 | tf_op jit(solution)/shard_map/ppermute | solution.py:531
  109.6 67.0 %collective-permute-start.17 = (bf16[8192,128]{1,0:T(8,128)(2,1)}, bf16[8192,128]{1,0:T(8,128)(2,1)S(1)}, u32[]{:S(2)}, u32[]{:S(2)}) collective-permute-start(bf16[8192,128]{1,0:T(8,128)(2,1)} %collective-permute-done.12.refs_1_), channel_id=1, source_target_pairs={{8,0},{9,1},{10,2},{11,3},{12,4},{13,5},{14,6},{15,7}} | collective-permute-start | bytes 6291464 | tf_op jit(solution)/shard_map/ppermute | solution.py:552
  115.0 66.4 %collective-permute-start.16 = (bf16[8192,128]{1,0:T(8,128)(2,1)S(1)}, bf16[8192,128]{1,0:T(8,128)(2,1)S(1)}, u32[]{:S(2)}, u32[]{:S(2)}) collective-permute-start(bf16[8192,128]{1,0:T(8,128)(2,1)S(1)} %collective-permute-done.11.refs_0_), channel_id=1, source_target_pairs={{16,24},{17,25},{18,26},{19,27},{20,28},{21,29},{22,30},{23,31}} | collective-permute-start | bytes 6291464 | tf_op jit(solution)/shard_map/ppermute | solution.py:549
  117.4 56.9 %collective-permute-start = (s16[320,2176]{1,0:T(8,128)(2,1)S(1)}, s16[320,2176]{1,0:T(8,128)(2,1)}, u32[]{:S(2)}, u32[]{:S(2)}) collective-permute-start(s16[320,2176]{1,0:T(8,128)(2,1)S(1)} %ladder.5.refs_0_), channel_id=1, source_target_pairs={{2,0},{8,10},{22,20},{28,30},{3,1},{9,11},{23,21},{29,31}} | collective-permute-start | bytes 4177928 | tf_op jit(solution)/shard_map/ppermute | solution.py:531
  136.4 38.7 %collective-permute-start.10 = (s16[320,2176]{1,0:T(8,128)(2,1)S(1)}, s16[320,2176]{1,0:T(8,128)(2,1)S(1)}, u32[]{:S(2)}, u32[]{:S(2)}) collective-permute-start(s16[320,2176]{1,0:T(8,128)(2,1)S(1)} %ladder.7.refs_8_), channel_id=1, source_target_pairs={{4,2},{10,12},{16,22},{5,3},{11,13},{17,23}} | collective-permute-start | bytes 4177928 | tf_op jit(solution)/shard_map/ppermute | solution.py:531
  141.2 34.6 %collective-permute-start.9 = (s16[320,2176]{1,0:T(8,128)(2,1)S(1)}, s16[320,2176]{1,0:T(8,128)(2,1)}, u32[]{:S(2)}, u32[]{:S(2)}) collective-permute-start(s16[320,2176]{1,0:T(8,128)(2,1)S(1)} %ladder.7.refs_8_), channel_id=1, source_target_pairs={{6,2},{8,12},{18,22},{7,3},{9,13},{19,23}} | collective-permute-start | bytes 4177928 | tf_op jit(solution)/shard_map/ppermute | solution.py:531
  174.3 13.6 %collective-permute-start.8 = (s16[320,2176]{1,0:T(8,128)(2,1)S(1)}, s16[320,2176]{1,0:T(8,128)(2,1)S(1)}, u32[]{:S(2)}, u32[]{:S(2)}) collective-permute-start(s16[320,2176]{1,0:T(8,128)(2,1)S(1)} %ladder.7.refs_8_), channel_id=1, source_target_pairs={{0,2},{14,12},{20,22},{1,3},{15,13},{21,23}} | collective-permute-start | bytes 4177928 | tf_op jit(solution)/shard_map/ppermute | solution.py:531
  175.1 14.2 %collective-permute-start.6 = (s16[320,2176]{1,0:T(8,128)(2,1)S(1)}, s16[320,2176]{1,0:T(8,128)(2,1)S(1)}, u32[]{:S(2)}, u32[]{:S(2)}) collective-permute-start(s16[320,2176]{1,0:T(8,128)(2,1)S(1)} %ladder.6.refs_4_), channel_id=1, source_target_pairs={{14,8},{20,18},{26,28},{15,9},{21,19},{27,29}} | collective-permute-start | bytes 4177928 | tf_op jit(solution)/shard_map/ppermute | solution.py:531
  175.8 14.7 %collective-permute-start.5 = (s16[320,2176]{1,0:T(8,128)(2,1)S(1)}, s16[320,2176]{1,0:T(8,128)(2,1)S(1)}, u32[]{:S(2)}, u32[]{:S(2)}) collective-permute-start(s16[320,2176]{1,0:T(8,128)(2,1)S(1)} %ladder.6.refs_4_), channel_id=1, source_target_pairs={{12,8},{22,18},{24,28},{13,9},{23,19},{25,29}} | collective-permute-start | bytes 4177928 | tf_op jit(solution)/shard_map/ppermute | solution.py:531
  176.6 15.7 %collective-permute-start.4 = (s16[320,2176]{1,0:T(8,128)(2,1)S(1)}, s16[320,2176]{1,0:T(8,128)(2,1)}, u32[]{:S(2)}, u32[]{:S(2)}) collective-permute-start(s16[320,2176]{1,0:T(8,128)(2,1)S(1)} %ladder.6.refs_4_), channel_id=1, source_target_pairs={{10,8},{16,18},{30,28},{11,9},{17,19},{31,29}} | collective-permute-start | bytes 4177928 | tf_op jit(solution)/shard_map/ppermute | solution.py:531
  181.4 59.2 %collective-permute-start.15 = (s16[320,2176]{1,0:T(8,128)(2,1)S(1)}, s16[320,2176]{1,0:T(8,128)(2,1)}, u32[]{:S(2)}, u32[]{:S(2)}) collective-permute-start(s16[320,2176]{1,0:T(8,128)(2,1)S(1)} %ladder.8.refs_12_), channel_id=1, source_target_pairs={{2,4},{8,14},{22,16},{28,26},{3,5},{9,15},{23,17},{29,27}} | collective-permute-start | bytes 4177928 | tf_op jit(solution)/shard_map/ppermute | solution.py:531
  185.7 60.1 %copy-start.23 = (s32[256]{0:T(256)S(1)}, s32[256]{0:T(256)}, u32[]{:S(2)}) copy-start(s32[256]{0:T(256)} %copy-done.22) | copy-start | bytes 3076
  185.7 60.1 %copy-start.25 = (s32[256]{0:T(256)S(1)}, s32[256]{0:T(256)}, u32[]{:S(2)}) copy-start(s32[256]{0:T(256)} %copy-done.24) | copy-start | bytes 3076
  185.7 60.1 %copy-start.27 = (s32[256]{0:T(256)S(1)}, s32[256]{0:T(256)}, u32[]{:S(2)}) copy-start(s32[256]{0:T(256)} %copy-done.26) | copy-start | bytes 3076
  188.0 59.8 %collective-permute-start.14 = (s16[320,2176]{1,0:T(8,128)(2,1)S(1)}, s16[320,2176]{1,0:T(8,128)(2,1)}, u32[]{:S(2)}, u32[]{:S(2)}) collective-permute-start(s16[320,2176]{1,0:T(8,128)(2,1)S(1)} %ladder.8.refs_12_), channel_id=1, source_target_pairs={{0,4},{10,14},{20,16},{30,26},{1,5},{11,15},{21,17},{31,27}} | collective-permute-start | bytes 4177928 | tf_op jit(solution)/shard_map/ppermute | solution.py:531
  189.3 58.5 %collective-permute-start.13 = (s16[320,2176]{1,0:T(8,128)(2,1)S(1)}, s16[320,2176]{1,0:T(8,128)(2,1)}, u32[]{:S(2)}, u32[]{:S(2)}) collective-permute-start(s16[320,2176]{1,0:T(8,128)(2,1)S(1)} %ladder.8.refs_12_), channel_id=1, source_target_pairs={{6,4},{12,14},{18,16},{24,26},{7,5},{13,15},{19,17},{25,27}} | collective-permute-start | bytes 4177928 | tf_op jit(solution)/shard_map/ppermute | solution.py:531
  190.6 57.2 %collective-permute-start.20 = (s16[320,2176]{1,0:T(8,128)(2,1)S(1)}, s16[320,2176]{1,0:T(8,128)(2,1)}, u32[]{:S(2)}, u32[]{:S(2)}) collective-permute-start(s16[320,2176]{1,0:T(8,128)(2,1)S(1)} %ladder.9.refs_16_), channel_id=1, source_target_pairs={{0,6},{30,24},{1,7},{31,25}} | collective-permute-start | bytes 4177928 | tf_op jit(solution)/shard_map/ppermute | solution.py:531
  192.4 55.4 %collective-permute-start.19 = (s16[320,2176]{1,0:T(8,128)(2,1)S(1)}, s16[320,2176]{1,0:T(8,128)(2,1)}, u32[]{:S(2)}, u32[]{:S(2)}) collective-permute-start(s16[320,2176]{1,0:T(8,128)(2,1)S(1)} %ladder.9.refs_16_), channel_id=1, source_target_pairs={{2,6},{28,24},{3,7},{29,25}} | collective-permute-start | bytes 4177928 | tf_op jit(solution)/shard_map/ppermute | solution.py:531
  240.6 7.2 %collective-permute-start.18 = (s16[320,2176]{1,0:T(8,128)(2,1)S(1)}, s16[320,2176]{1,0:T(8,128)(2,1)}, u32[]{:S(2)}, u32[]{:S(2)}) collective-permute-start(s16[320,2176]{1,0:T(8,128)(2,1)S(1)} %ladder.9.refs_16_), channel_id=1, source_target_pairs={{4,6},{26,24},{5,7},{27,25}} | collective-permute-start | bytes 4177928 | tf_op jit(solution)/shard_map/ppermute | solution.py:531
  (33 other events, 1060.9 us)

commit v2 on v0

--- a/solution.py
+++ b/solution.py
@@ -1,7 +1,15 @@
+import functools
 import jax
 import jax.numpy as jnp
 from jax import lax
+from jax.experimental import pallas as pl
+from jax.experimental.pallas import tpu as pltpu
 from jax.sharding import PartitionSpec as P
+
+F32, BF16, I32, I16 = jnp.float32, jnp.bfloat16, jnp.int32, jnp.int16
+LANES = 128
+TILE_ROWS = 16
+ANY = pl.BlockSpec(memory_space=pltpu.HBM)
 
 
 def table_value(values_table, positions):
@@ -27,7 +35,7 @@
     return jnp.take(jnp.take(block, row_index, axis=0), col_index, axis=1)
 
 
-def on_device(
+def on_device_general(
     amplitudes, integrals, virtual_energy, occupied_energy, virtual_count, occupied_count
 ):
     row_number = lax.axis_index("row")
@@ -95,8 +103,565 @@
     return jnp.where(allowed, symmetrized / denominator, jnp.zeros((), jnp.float32))
 
 
+class Plan:
+    def __init__(self, amp_shape, int_shape, rows, virt_slots, occ_slots):
+        self.syms, self.share, self.width = amp_shape
+        self.pairs = int_shape[1]
+        self.rows = rows
+        self.virt_slots, self.occ_slots = virt_slots, occ_slots
+        self.virt_cap, self.occ_cap = virt_slots // 8, occ_slots // 8
+        self.tiles = self.width // LANES
+        self.row_tiles = self.share // TILE_ROWS
+        self.pay_tiles = self.syms * self.tiles * self.row_tiles
+        self.pay_room = self.pay_tiles * TILE_ROWS + self.share
+        self.enc_tiles = (self.share // 2 + self.occ_slots // 2) // TILE_ROWS
+        self.at_ndt = 2
+        self.at_first = self.at_ndt + 2 * self.syms
+        self.at_reps = self.at_first + 2 * self.syms * self.tiles
+        self.at_self = self.at_reps + self.syms * rows
+        self.at_more = self.at_self + self.syms * rows
+        self.base_tiles = self.pay_tiles * 43 // 64
+        self.enc_shape = (self.enc_tiles * TILE_ROWS, self.pairs + LANES)
+
+
+def row_counts(plan, tab, sym, share):
+    reps = tab[plan.at_reps + sym * plan.rows + share]
+    selfs = tab[plan.at_self + sym * plan.rows + share]
+    return reps, selfs, padded(2 * reps + selfs)
+
+
+def band(rel_row):
+    return (lax.broadcasted_iota(I32, (2 * LANES, LANES), 0) == rel_row).astype(BF16)
+
+
+def pack_kernel(plan, tab, amp, dest, rel, pay, acc):
+    pay[...] = jnp.zeros_like(pay)
+    row = tab[0]
+    base = jnp.int32(0)
+    for sym in range(plan.syms):
+        _, _, nrt = row_counts(plan, tab, sym, row)
+        ndt = tab[plan.at_ndt + sym]
+        pick = (
+            lax.broadcasted_iota(I32, (plan.share, plan.share), 0) == dest[sym : sym + 1, :]
+        ).astype(BF16)
+        compact = jnp.dot(pick, amp[sym], preferred_element_type=F32).astype(BF16)
+        acc[...] = jnp.zeros_like(acc)
+        for tile in range(plan.tiles):
+            at = sym * plan.tiles + tile
+            placed = lax.dot_general(
+                compact[:, tile * LANES : (tile + 1) * LANES],
+                band(rel[at : at + 1, :]),
+                (((1,), (1,)), ((), ())),
+                preferred_element_type=F32,
+            )
+            first = tab[plan.at_first + at]
+            acc[first] += placed[:, :LANES]
+            acc[first + 1] += placed[:, LANES:]
+
+        def put(tile, _, base=base, nrt=nrt):
+            start = pl.multiple_of((base + tile * nrt) * TILE_ROWS, TILE_ROWS)
+            pay[pl.ds(start, plan.share), :] = acc[tile].astype(BF16)
+            return 0
+
+        lax.fori_loop(0, ndt, put, 0)
+        base = base + nrt * ndt
+
+
+def pack(plan, tab, amp, dest, rel):
+    vm = pl.BlockSpec(memory_space=pltpu.VMEM)
+    return pl.pallas_call(
+        functools.partial(pack_kernel, plan),
+        out_shape=jax.ShapeDtypeStruct((plan.pay_room, LANES), BF16),
+        in_specs=[pl.BlockSpec(memory_space=pltpu.SMEM), vm, vm, vm],
+        out_specs=vm,
+        scratch_shapes=[pltpu.VMEM((plan.tiles + 1, plan.share, LANES), F32)],
+        compiler_params=pltpu.CompilerParams(vmem_limit_bytes=40 << 20),
+        name="pack",
+    )(tab, amp, dest, rel)
+
+
+def share_of(plan, row, kind):
+    step, side = kind
+    if step == 0:
+        return row, row >= 0
+    if side == "right":
+        return row - step, row >= step
+    if side == "left":
+        return row + step, row + step < plan.rows
+    share = jnp.where(row >= plan.rows // 2, row - step, row + step)
+    return share, (share >= 0) & (share < plan.rows)
+
+
+def lane_mates(plan, rows, sym, fbase, tile):
+    flip = sym * plan.virt_cap + fbase + (tile * LANES) // plan.virt_slots
+    return lax.broadcasted_iota(I32, (rows, LANES), 1) ^ flip
+
+
+def lane_take(x, index):
+    return jnp.take_along_axis(x, index, axis=1)
+
+
+def ladder_kernel(plan, kind, count, pay_rows, tab, rel, *refs):
+    pays, (rest, ints, sib_ints) = refs[:count], refs[count : count + 3]
+    outs, (pay, held, dense, prod, enc, sems, int_sems) = refs[-7 - plan.rows : -7], refs[-7:]
+    row, col = tab[0], tab[1]
+    sym = lax.rem(col, 2)
+    share, active = share_of(plan, row, kind)
+    steps = held.shape[1]
+    ptile = plan.pairs // steps
+
+    def int_copies(pt):
+        return [
+            pltpu.make_async_copy(
+                ref.at[sym, pl.ds(pt * ptile, ptile)], held.at[part, pt], int_sems.at[part, pt]
+            )
+            for part, ref in enumerate((ints, sib_ints))
+        ]
+
+    def pay_copies(pair):
+        return [
+            pltpu.make_async_copy(ref, pay.at[part, pl.ds(0, pay_rows)], sems.at[part])
+            for part, ref in enumerate(pair)
+        ]
+
+    @pl.when(active)
+    def _():
+        for start in (pay_rows, plan.pay_room - plan.share):
+            pay[:, start : start + plan.share, :] = jnp.zeros((2, plan.share, LANES), BF16)
+        if count == 2:
+            for copy in pay_copies(pays):
+                copy.start()
+        else:
+            upper = row >= plan.rows // 2
+
+            @pl.when(upper)
+            def _():
+                for copy in pay_copies(pays[:2]):
+                    copy.start()
+
+            @pl.when(jnp.logical_not(upper))
+            def _():
+                for copy in pay_copies(pays[2:]):
+                    copy.start()
+
+        for copy in pay_copies(pays[:2]):
+            copy.wait()
+        for pt in range(steps):
+            for copy in int_copies(pt):
+                copy.start()
+
+        @pl.when(tab[plan.at_more] > 0)
+        def _():
+            for part in range(2):
+                copy = pltpu.make_async_copy(
+                    rest.at[part, share], pay.at[part, pl.ds(pay_rows, rest.shape[2])], sems.at[part]
+                )
+                copy.start()
+                copy.wait()
+
+        reps, selfs, nrt = row_counts(plan, tab, sym, share)
+        _, _, nrt0 = row_counts(plan, tab, 0, share)
+        rep_room = padded(reps) * TILE_ROWS
+        lines = lax.broadcasted_iota(I32, (plan.share, plan.share), 1)
+        spread = lines + jnp.where(lines < reps, 0, jnp.where(lines < 2 * reps, 1, 2)) * (
+            rep_room - reps
+        )
+        spread = jnp.where(
+            spread == lax.broadcasted_iota(I32, (plan.share, plan.share), 0), 1.0, 0.0
+        ).astype(BF16)
+        group = 4
+        for part in range(2):
+            ndt0 = tab[plan.at_ndt + part * plan.syms]
+            ndt = tab[plan.at_ndt + part * plan.syms + sym]
+            base = jnp.where(sym == 0, 0, nrt0 * ndt0)
+            for at_tile in range(0, plan.tiles, group):
+                filled = []
+                for tile in range(at_tile, at_tile + group):
+                    at = (part * plan.syms + sym) * plan.tiles + tile
+                    first = tab[plan.at_first + at]
+                    pieces = []
+                    for step in range(2):
+                        use = jnp.maximum(jnp.minimum(first + step, ndt - 1), 0)
+                        start = pl.multiple_of((base + use * nrt) * TILE_ROWS, TILE_ROWS)
+                        pieces.append(pay[part, pl.ds(start, plan.share), :])
+                    filled.append(
+                        jnp.dot(
+                            jnp.concatenate(pieces, axis=1),
+                            band(rel[pl.ds(at, 1), :]),
+                            preferred_element_type=F32,
+                        ).astype(BF16)
+                    )
+                dense[part, :, at_tile * LANES : (at_tile + group) * LANES] = jnp.dot(
+                    spread, jnp.concatenate(filled, axis=1), preferred_element_type=F32
+                ).astype(BF16)
+
+        def multiply(pt, _):
+            for copy in int_copies(pt):
+                copy.wait()
+            prod[:, pl.ds(pl.multiple_of(pt * ptile, ptile), ptile)] = lax.dot_general(
+                dense[0], held[0, pt], (((1,), (1,)), ((), ())), preferred_element_type=F32
+            ) + lax.dot_general(
+                dense[1], held[1, pt], (((1,), (1,)), ((), ())), preferred_element_type=F32
+            )
+            return 0
+
+        lax.fori_loop(0, steps, multiply, 0)
+
+        fbase = row * (plan.pairs // plan.virt_slots)
+
+        def chunk(k, _):
+            to_row = pl.multiple_of(k * TILE_ROWS, TILE_ROWS)
+            mate_row = pl.multiple_of(to_row + rep_room, TILE_ROWS)
+            own_row = pl.multiple_of(jnp.where(to_row < rep_room, to_row, mate_row), TILE_ROWS)
+            sums, top = [], None
+            for v in range(plan.pairs // LANES):
+                lanes = slice(v * LANES, (v + 1) * LANES)
+                mirrored = lane_take(
+                    prod[pl.ds(mate_row, TILE_ROWS), lanes],
+                    lane_mates(plan, TILE_ROWS, sym, fbase, v),
+                )
+                both = prod[pl.ds(own_row, TILE_ROWS), lanes] + mirrored
+                sums.append(both)
+                top = jnp.abs(both) if top is None else jnp.maximum(top, jnp.abs(both))
+            peak = jnp.maximum(jnp.max(top, axis=1, keepdims=True), 1e-30)
+            power = jnp.floor(jnp.log2(32000.0 / peak))
+            scale = jnp.exp2(power)
+            for v, both in enumerate(sums):
+                enc[pl.ds(to_row, TILE_ROWS), v * LANES : (v + 1) * LANES] = (
+                    jnp.round(both * scale).astype(I32).astype(I16)
+                )
+            enc[pl.ds(to_row, TILE_ROWS), plan.pairs :] = (
+                jnp.broadcast_to(power, (TILE_ROWS, LANES)).astype(I32).astype(I16)
+            )
+            return 0
+
+        lax.fori_loop(0, padded(reps) + padded(selfs), chunk, 0)
+
+        for flip, out in enumerate(outs):
+
+            @pl.when((col ^ share) == flip)
+            def _():
+                copy = pltpu.make_async_copy(enc, out, sems.at[0])
+                copy.start()
+                copy.wait()
+
+
+def ladder_call(plan, kind, tab, rel, pays, rest, integrals, sib_integrals, encs):
+    steps = 4
+    n = plan.rows
+    smem, vmem = (pl.BlockSpec(memory_space=space) for space in (pltpu.SMEM, pltpu.VMEM))
+    first_enc = 5 + len(pays)
+    return pl.pallas_call(
+        functools.partial(ladder_kernel, plan, kind, len(pays), pays[0].shape[0]),
+        out_shape=[jax.ShapeDtypeStruct(plan.enc_shape, I16)] * n,
+        in_specs=[smem, vmem] + [ANY] * (len(pays) + 3 + len(encs)),
+        out_specs=[ANY] * n,
+        scratch_shapes=[
+            pltpu.VMEM((2, plan.pay_room, LANES), BF16),
+            pltpu.VMEM((2, steps, plan.pairs // steps, plan.width), BF16),
+            pltpu.VMEM((2, plan.share, plan.width), BF16),
+            pltpu.VMEM((plan.share, plan.pairs), F32),
+            pltpu.VMEM(plan.enc_shape, I16),
+            pltpu.SemaphoreType.DMA((2,)),
+            pltpu.SemaphoreType.DMA((2, steps)),
+        ],
+        input_output_aliases={first_enc + i: i for i in range(len(encs))},
+        compiler_params=pltpu.CompilerParams(vmem_limit_bytes=48 << 20),
+        cost_estimate=pl.CostEstimate(
+            flops=2 * plan.syms * plan.share * plan.width * plan.pairs,
+            bytes_accessed=2 * plan.syms * plan.width * plan.pairs,
+            transcendentals=0,
+        ),
+        name="ladder",
+    )(tab, rel, *pays, rest, integrals, sib_integrals, *encs)
+
+
+def finish_kernel(plan, wtile, tab, line, hole, pair, pair_ok, *refs):
+    n = plan.rows
+    out, held, pick, sems = refs[-4:]
+    away_sets = [refs[n * i : n * (i + 1)] for i in range(n - 1)]
+    step = pl.program_id(0)
+    row, col = tab[0], tab[1]
+    core = lax.rem(col, 2)
+
+    def fetch(sources):
+        parts = [(core, 0), (1 - core, 0), (core, 1), (1 - core, 1)]
+        copies = [
+            pltpu.make_async_copy(ref, held.at[sym, side], sems.at[number])
+            for number, (ref, (sym, side)) in enumerate(zip(sources, parts))
+        ]
+        for copy in copies:
+            copy.start()
+        places = lax.broadcasted_iota(I32, pick.shape[2:], 1)
+        for sym in range(plan.syms):
+            for half in range(2):
+                pick[sym, half] = (places + half * pick.shape[3] == line[sym]).astype(BF16)
+        for copy in copies:
+            copy.wait()
+
+    which = jnp.maximum(jnp.abs(row - col) - 1, 0)
+    for number, sources in enumerate(away_sets):
+
+        @pl.when((step == 0) & (which == number))
+        def _(sources=sources):
+            fetch(sources)
+
+    fbase = row * (plan.pairs // plan.virt_slots) + step * (wtile // plan.virt_slots)
+    for sym in range(plan.syms):
+        count = plan.enc_shape[0] if sym == 0 else plan.share // 2
+        reps, selfs, _ = row_counts(plan, tab, sym, col)
+        live = lax.broadcasted_iota(I32, (count, LANES), 0) < (
+            padded(reps) + padded(selfs)
+        ) * TILE_ROWS
+        scales = [
+            jnp.exp2(
+                -held[sym, side, pl.ds(0, count), pl.ds(plan.pairs, LANES)].astype(I32).astype(F32)
+            )
+            for side in range(2)
+        ]
+        terms = [[], []]
+        for v in range(wtile // LANES):
+            lanes = pl.ds(pl.multiple_of(step * wtile + v * LANES, LANES), LANES)
+            left = jnp.where(
+                live,
+                held[sym, 0, pl.ds(0, count), lanes].astype(I32).astype(F32) * scales[0]
+                + held[sym, 1, pl.ds(0, count), lanes].astype(I32).astype(F32) * scales[1],
+                0.0,
+            )
+            for term in terms:
+                term.append(left.astype(BF16))
+                left = left - term[-1].astype(F32)
+        terms = [jnp.concatenate(term, axis=1) for term in terms]
+        halves = []
+        for half in range(2):
+            total = None
+            for term in terms:
+                part = jnp.dot(pick[sym, half, :, :count], term, preferred_element_type=F32)
+                total = part if total is None else total + part
+            halves.append(total)
+        for v in range(wtile // LANES):
+            lanes = slice(v * LANES, (v + 1) * LANES)
+            result = halves[0][:, lanes] + lane_take(
+                halves[1][:, lanes], lane_mates(plan, plan.share, sym, fbase, v)
+            )
+            allowed = (line[sym] >= 0) & (pair_ok[sym, :, lanes] > 0)
+            out[sym, :, lanes] = jnp.where(
+                allowed, result / (pair[sym, :, lanes] - hole[sym]), 0.0
+            )
+
+
+def finish(plan, tab, line, hole, pair, pair_ok, sources):
+    wtile = min(256, plan.pairs)
+    whole = lambda shape: pl.BlockSpec(shape, lambda i, tab: (0,) * len(shape))
+    tiled = pl.BlockSpec((plan.syms, 1, wtile), lambda i, tab: (0, 0, i))
+    grid_spec = pltpu.PrefetchScalarGridSpec(
+        num_scalar_prefetch=1,
+        grid=(plan.pairs // wtile,),
+        in_specs=[whole(line.shape), whole(hole.shape), tiled, tiled] + [ANY] * len(sources),
+        out_specs=pl.BlockSpec((plan.syms, plan.share, wtile), lambda i, tab: (0, 0, i)),
+        scratch_shapes=[
+            pltpu.VMEM((plan.syms, 2) + plan.enc_shape, I16),
+            pltpu.VMEM((plan.syms, 2, plan.share, plan.enc_shape[0]), BF16),
+            pltpu.SemaphoreType.DMA((4,)),
+        ],
+    )
+    return pl.pallas_call(
+        functools.partial(finish_kernel, plan, wtile),
+        out_shape=jax.ShapeDtypeStruct((plan.syms, plan.share, plan.pairs), F32),
+        grid_spec=grid_spec,
+        compiler_params=pltpu.CompilerParams(
+            dimension_semantics=("arbitrary",), vmem_limit_bytes=48 << 20
+        ),
+        name="finish",
+    )(tab, line, hole, pair, pair_ok, *sources)
+
+
+def occupied_share(plan, counts, share_number):
+    slot = share_number * plan.share + jnp.arange(plan.share, dtype=I32)
+    first, second, mate = pair_orbitals(slot, plan.occ_slots, plan.occ_cap, plan.syms)
+    ok = is_orbital(counts, first, plan.occ_cap) & is_orbital(counts, second, plan.occ_cap)
+    lead = jnp.minimum(slot[None, :], mate)
+    is_rep = ok & (first < second)
+    is_self = ok & (first == second)
+    before = slot[None, None, :] < lead[:, :, None]
+    rank = jnp.sum((is_rep[:, None, :] & before).astype(I32), axis=-1)
+    self_rank = jnp.sum((is_self[:, None, :] & before).astype(I32), axis=-1)
+    return first, second, ok, is_rep, is_self, rank, self_rank
+
+
+def padded(count):
+    return (count + TILE_ROWS - 1) // TILE_ROWS
+
+
+def line_tables(plan, virtual_energy, occupied_energy, virtual_count, occupied_count):
+    row = lax.axis_index("row")
+    col = lax.axis_index("col")
+    occ = lax.axis_index("occ")
+    syms = plan.syms
+    slots = jnp.arange(2 * plan.rows * plan.share, dtype=I32)
+    first, second, _ = pair_orbitals(slots, plan.occ_slots, plan.occ_cap, syms)
+    ok = is_orbital(occupied_count, first, plan.occ_cap) & is_orbital(
+        occupied_count, second, plan.occ_cap
+    )
+    grouped = lambda x: jnp.sum(x.astype(I32).reshape(syms, plan.rows, 2, plan.share), axis=-1)
+    reps_all = grouped(ok & (first < second))
+    selfs_all = grouped(ok & (first == second))
+    reps = jnp.where(occ == 0, reps_all[:, :, 0], reps_all[:, :, 1])
+    selfs = jnp.where(occ == 0, selfs_all[:, :, 0], selfs_all[:, :, 1])
+    blocks = plan.rows
+    slots = jnp.arange(blocks * plan.width, dtype=I32)
+    first, second, _ = pair_orbitals(slots, plan.virt_slots, plan.virt_cap, syms)
+    ok = is_orbital(virtual_count, first, plan.virt_cap) & is_orbital(
+        virtual_count, second, plan.virt_cap
+    )
+    per_block = jnp.sum(ok.astype(I32).reshape(syms, blocks, plan.width), axis=-1)
+    ndt_all = (per_block + LANES - 1) // LANES
+    tiles_needed = jnp.max(
+        jnp.sum(padded(2 * reps_all + selfs_all)[:, :, :, None] * ndt_all[:, None, None, :], axis=0)
+    )
+    more = (tiles_needed > plan.base_tiles).astype(I32)
+    slot = (col ^ jnp.arange(2, dtype=I32))[:, None] * plan.width + jnp.arange(
+        plan.width, dtype=I32
+    )
+    first, second, _ = pair_orbitals(slot.reshape(-1), plan.virt_slots, plan.virt_cap, syms)
+    ok = is_orbital(virtual_count, first, plan.virt_cap) & is_orbital(
+        virtual_count, second, plan.virt_cap
+    )
+    ok = jnp.swapaxes(ok.reshape(syms, 2, plan.tiles, LANES), 0, 1)
+    per_tile = jnp.sum(ok.astype(I32), axis=-1)
+    tile_ids = jnp.arange(plan.tiles, dtype=I32)
+    starts = jnp.sum(
+        jnp.where(tile_ids[None, :] < tile_ids[:, None], per_tile[:, :, None, :], 0), axis=-1
+    )
+    lane_ids = jnp.arange(LANES, dtype=I32)
+    within = jnp.sum(
+        (ok[..., None, :] & (lane_ids[None, :] < lane_ids[:, None])).astype(I32), axis=-1
+    )
+    firsts = starts // LANES
+    rel = jnp.where(ok, within + (starts % LANES)[..., None], -1)
+    ndt = (jnp.sum(per_tile, axis=-1) + LANES - 1) // LANES
+    tab = jnp.concatenate(
+        [
+            jnp.stack([row, col]).astype(I32),
+            ndt.reshape(-1),
+            firsts.reshape(-1),
+            reps.reshape(-1),
+            selfs.reshape(-1),
+            more[None],
+        ]
+    )
+    _, _, ok, is_rep, is_self, rank, self_rank = occupied_share(
+        plan, occupied_count, 2 * row + occ
+    )
+    n_rep = jnp.sum(is_rep.astype(I32), axis=-1, keepdims=True)
+    dest = jnp.where(is_self, 2 * n_rep + self_rank, jnp.where(is_rep, rank, n_rep + rank))
+    dest = jnp.where(ok, dest, -1)
+    first, second, ok, is_rep, is_self, rank, self_rank = occupied_share(
+        plan, occupied_count, 2 * col + occ
+    )
+    n_rep = jnp.sum(is_rep.astype(I32), axis=-1, keepdims=True)
+    count = plan.enc_tiles * TILE_ROWS
+    rep_room = padded(n_rep) * TILE_ROWS
+    line = jnp.where(is_self, rep_room + self_rank, jnp.where(is_rep, rank, count + rank))
+    line = jnp.where(ok, line, -1)
+    hole = table_value(occupied_energy, first) + table_value(occupied_energy, second)
+    slot = row * plan.pairs + jnp.arange(plan.pairs, dtype=I32)
+    first, second, _ = pair_orbitals(slot, plan.virt_slots, plan.virt_cap, syms)
+    pair_ok = is_orbital(virtual_count, first, plan.virt_cap) & is_orbital(
+        virtual_count, second, plan.virt_cap
+    )
+    pair = table_value(virtual_energy, first) + table_value(virtual_energy, second)
+    return (
+        more,
+        tab,
+        dest,
+        rel.reshape(2 * syms * plan.tiles, LANES),
+        line[:, :, None],
+        hole[:, :, None],
+        pair[:, None, :],
+        pair_ok.astype(I32)[:, None, :],
+    )
+
+
+def to_roots(plan, encs, distances):
+    received = [encs[0]]
+    for flip in range(1, plan.rows):
+        pairs = [
+            (row * plan.rows + (root ^ flip), row * plan.rows + root)
+            for row in range(plan.rows)
+            for root in range(plan.rows)
+            if abs(row - root) in distances
+        ]
+        received.append(lax.ppermute(encs[flip], ("row", "col"), pairs))
+    return received
+
+
+def on_device_line(
+    rows, amplitudes, integrals, virtual_energy, occupied_energy, virtual_count, occupied_count
+):
+    n = rows
+    plan = Plan(
+        amplitudes.shape, integrals.shape, rows, virtual_energy.shape[0], occupied_energy.shape[0]
+    )
+    swap = [(i, i ^ 1) for i in range(n)]
+    sibling = lambda x: lax.ppermute(x, "col", swap)
+    sib_integrals = sibling(integrals)
+    more, tab, dest, rel, line, hole, pair, pair_ok = line_tables(
+        plan, virtual_energy, occupied_energy, virtual_count, occupied_count
+    )
+    packed = pack(plan, tab, amplitudes, dest, rel)
+    base_rows = plan.base_tiles * TILE_ROWS
+    all_rows = plan.pay_tiles * TILE_ROWS
+    pay = packed[:base_rows]
+
+    def send_rest(packed):
+        gathered = lax.all_gather(packed[base_rows:all_rows], "row")
+        return jnp.stack([gathered, sibling(gathered)])
+
+    def no_rest(packed):
+        return jnp.zeros((2, n, all_rows - base_rows, LANES), BF16)
+
+    rest = lax.cond(more > 0, send_rest, no_rest, packed)
+    row = lax.axis_index("row")
+
+    def work(kind, pays, encs):
+        both = [x for pay in pays for x in (pay, sibling(pay))]
+        return ladder_call(plan, kind, tab, rel, both, rest, integrals, sib_integrals, encs)
+
+    right = lax.ppermute(pay, "row", [(i, i + 1) for i in range(n - 1)])
+    left = lax.ppermute(pay, "row", [(i + 1, i) for i in range(n - 1)])
+    encs = work((0, ""), [pay], [])
+    sources = []
+    for step in range(2, n):
+        right, left, encs = lax.optimization_barrier((right, left, encs))
+        if step < n - 1:
+            ahead = (
+                lax.ppermute(right, "row", [(i, i + 1) for i in range(step - 1, n - 1)]),
+                lax.ppermute(left, "row", [(i + 1, i) for i in range(0, n - step)]),
+            )
+        else:
+            last = jnp.where(row >= n // 2, right, left)
+            last = lax.ppermute(last, "row", [(n - 2, n - 1), (1, 0)])
+        if step == 2:
+            encs = work((1, "right"), [right], encs)
+            encs = work((1, "left"), [left], encs)
+        else:
+            sources += to_roots(plan, encs, (0, 1) if step == 3 else (step - 2,))
+            encs = work((step - 1, ""), [right, left], [])
+        if step < n - 1:
+            right, left = ahead
+    sources += to_roots(plan, encs, (n - 2,))
+    last, sources = lax.optimization_barrier((last, sources))
+    sources += to_roots(plan, work((n - 1, ""), [last], []), (n - 1,))
+    return finish(plan, tab, line, hole, pair, pair_ok, sources)
+
+
 def solution(mesh):
+    rows, cols = mesh.shape["row"], mesh.shape["col"]
     placed = (P(None, ("row", "occ"), "col"), P(None, "row", "col"), P(), P(), P(), P())
+    on_device = on_device_general
+    if rows == 4 and cols == 4:
+        on_device = functools.partial(on_device_line, rows)
     return jax.shard_map(
         on_device,
         mesh=mesh,

time: 423 us -> 207 us (0.49)
  waiting for transfers between devices: 270 us -> 63 us
  local copies, waits for them, and re-layouts: 93.1 us -> 19.2 us
  Pallas kernels: 0 us -> 59.4 us
  starting transfers between devices: 0.04 us -> 33.6 us
  matrix products: 24.7 us -> 0 us
    all_gather x1 -> x0, waiting for transfers between devices: 150 us -> none  [on_device(): gathered = lax.all_gather(amplitudes, 'row', axis=1, tiled=True)]
    reduce_scatter x1 -> x0, waiting for transfers between devices: 120 us -> none  [on_device(): lax.psum_scatter(jnp.einsum('sqd,spd->qsp', masked, integrals, preferred_...]
    gather x4 -> x0, local copies, waits for them, and re-layouts: 92.8 us -> none  [mirror_block(): return jnp.take(jnp.take(block, row_index, axis=0), col_index, axis=1)]
    ppermute x0 -> x21, waiting for transfers between devices: none -> 63 us  [the longest x9 28.2 us: to_roots(): received.append(lax.ppermute(encs[flip], ('row', 'col'), pairs))]
    pallas_call x0 -> x7, Pallas kernels: none -> 59.4 us  [the longest x5 47 us: ladder_call(): pl.pallas_call(functools.partial(ladder_kernel, plan, kind, len(pays), pa...]
    ppermute x0 -> x21, starting transfers between devices: none -> 33.6 us  [the longest x9 13.7 us: to_roots(): received.append(lax.ppermute(encs[flip], ('row', 'col'), pairs))]
    dot_general x1 -> x0, matrix products: 24.7 us -> none  [on_device(): jnp.einsum('sqd,spd->qsp', masked, integrals, preferred_element_type=jnp....]
    unnamed x8 -> x48, local copies, waits for them, and re-layouts: 0.31 us -> 13.2 us
  transfers between devices with their start and end apart: 2 -> 21, of which waited for: 2 -> 10; matrix products, arithmetic and copies ran while one was open for 1% -> 11% of each run, Pallas kernels for 0% -> 20%
where the time goes in v2:
time: 207 us; the launch traced here: 206 us
  waiting for transfers between devices  63 us (30%)
  Pallas kernels  59.4 us (29%)
  starting transfers between devices  33.6 us (16%)
  local copies, waits for them, and re-layouts  19.2 us (9%)
  other arithmetic  15.9 us (8%)
  between operations  14.8 us (7%)
    pallas_call x5, Pallas kernels, ladder_call(): pl.pallas_call(functools.partial(ladder_kernel, plan, kind, len(pays), pa...  47 us
    ppermute x9, waiting for transfers between devices, to_roots(): received.append(lax.ppermute(encs[flip], ('row', 'col'), pairs))  28.2 us
    ppermute x1, waiting for transfers between devices, on_device_line(): lax.ppermute(left, 'row', [(i + 1, i) for i in range(0, n - step)])  17.7 us
    ppermute x9, starting transfers between devices, to_roots(): received.append(lax.ppermute(encs[flip], ('row', 'col'), pairs))  13.7 us
    unnamed x48, local copies, waits for them, and re-layouts  13.2 us
    ppermute x7, starting transfers between devices, on_device_line(): sibling = lambda x: lax.ppermute(x, 'col', swap)  11 us
    pallas_call x1, Pallas kernels, finish(): pl.pallas_call(functools.partial(finish_kernel, plan, wtile), out_shape=j...  9.07 us
    ppermute x1, waiting for transfers between devices, on_device_line(): right = lax.ppermute(pay, 'row', [(i, i + 1) for i in range(n - 1)])  7.99 us
  transfers between devices with their start and end apart: 21, of which 10 were waited for; matrix products, arithmetic and copies ran while one was open for 11% of the time, Pallas kernels for 20%

profile of v2, /device:TPU:5, one launch (start us, length us, event | category | flops | bytes accessed | tf_op | source)
XLA Modules:
  0.0 205.8 jit_solution(10344472728738542764)
XLA Ops:
  17.8 3.3 %pack.1 = bf16[8448,128]{1,0:T(8,128)(2,1)S(1)} custom-call(s32[87]{0:T(128)S(1)} %concatenate.3.tab, bf16[2,256,2048]{2,1,0:T(8,128)(2,1)S(1)} %copy-done.2, s32[2,256]{1,0:T(2,128)S(1)} %fusion.63.dest, s32[64,128]{1,0:T(8,128)S(1)} %bitcast.25), custom_call_target="tpu_custom_call" | custom-call | tf_op jit(solution)/shard_map/pack/pallas_call | solution.py:172
  22.4 4.3 %collective-permute-start.1 = (bf16[5504,128]{1,0:T(8,128)(2,1)S(1)}, bf16[5504,128]{1,0:T(8,128)(2,1)}, u32[]{:S(2)}, u32[]{:S(2)}) collective-permute-start(bf16[5504,128]{1,0:T(8,128)(2,1)S(1)} %slice.27.refs_0_), channel_id=1, source_target_pairs={{0,8},{8,16},{16,24},{1,9},{9,17},{17,25},{2,10},{10,18},{18,26},{... | collective-permute-start | bytes 4227080 | tf_op jit(solution)/shard_map/ppermute | solution.py:631
  28.0 3.1 %conditional.1 = (bf16[2,4,2688,128]{3,2,1,0:T(8,128)(2,1)}) conditional(s32[]{:T(128)} %convert_element_type.65, () %tuple.14, bf16[8448,128]{1,0:T(8,128)(2,1)} %copy-done.15), branch_computations={%region_31.32_spmd, %region_32.33_spmd} | conditional | flops 2752512 | bytes 33718360 | solution.py:624
  28.0 3.1 %broadcast.2247 = bf16[2,4,2688,128]{3,2,1,0:T(8,128)(2,1)} broadcast(bf16[]{:T(256)} %constant.410.clone), dimensions={} | broadcast | bytes 5505026 | tf_op jit(solution)/shard_map/broadcast.48
  31.1 3.0 %collective-permute-done.3.refs_1_ = bf16[5504,128]{1,0:T(8,128)(2,1)} collective-permute-done((bf16[5504,128]{1,0:T(8,128)(2,1)S(1)}, bf16[5504,128]{1,0:T(8,128)(2,1)}, u32[]{:S(2)}, u32[]{:S(2)}) %collective-permute-start.3) | collective-permute-done | bytes 1409056 | tf_op jit(solution)/shard_map/ppermute | solution.py:607
  34.1 12.7 %ladder.5 = (s16[192,2176]{1,0:T(8,128)(2,1)S(1)}, s16[192,2176]{1,0:T(8,128)(2,1)S(1)}, s16[192,2176]{1,0:T(8,128)(2,1)S(1)}, s16[192,2176]{1,0:T(8,128)(2,1)}) custom-call(s32[87]{0:T(128)S(1)} %concatenate.3.tab, s32[64,128]{1,0:T(8,128)S(1)} %bitcast.26, bf16[5504,128]{1,0:T(8,128)(2,1)S(1)} %slice.27.refs_0_, ...), custom_call_target="tpu_custom_call" | custom-call | flops 4294967296 | bytes 16777216 | tf_op jit(solution)/shard_map/ladder/pallas_call | solution.py:354
  47.7 8.0 %collective-permute-done.1.refs_0_ = bf16[5504,128]{1,0:T(8,128)(2,1)} collective-permute-done((bf16[5504,128]{1,0:T(8,128)(2,1)S(1)}, bf16[5504,128]{1,0:T(8,128)(2,1)}, u32[]{:S(2)}, u32[]{:S(2)}) %collective-permute-start.1) | collective-permute-done | bytes 1409056 | tf_op jit(solution)/shard_map/ppermute | solution.py:631
  55.7 5.0 %collective-permute-done.2.refs_0_ = bf16[5504,128]{1,0:T(8,128)(2,1)} collective-permute-done((bf16[5504,128]{1,0:T(8,128)(2,1)S(1)}, bf16[5504,128]{1,0:T(8,128)(2,1)}, u32[]{:S(2)}, u32[]{:S(2)}) %collective-permute-start.2) | collective-permute-done | bytes 1409056 | tf_op jit(solution)/shard_map/ppermute | solution.py:632
  67.2 1.7 copy-done.14
  68.9 11.6 %ladder.7 = (s16[192,2176]{1,0:T(8,128)(2,1)S(1)}, s16[192,2176]{1,0:T(8,128)(2,1)S(1)}, s16[192,2176]{1,0:T(8,128)(2,1)S(1)}, s16[192,2176]{1,0:T(8,128)(2,1)}) custom-call(s32[87]{0:T(128)S(1)} %concatenate.3.tab, s32[64,128]{1,0:T(8,128)S(1)} %bitcast.28, ...), custom_call_target="tpu_custom_call", output_to_operand_aliasing={{0}: (7, {}), {1}: (8, {}), {2}: (9, {}), {3}: (10, {})} | custom-call | flops 4294967296 | bytes 16777216 | tf_op jit(solution)/shard_map/ladder/pallas_call | solution.py:354
  80.5 17.7 %collective-permute-done.6.refs_2_ = bf16[5504,128]{1,0:T(8,128)(2,1)} collective-permute-done((bf16[5504,128]{1,0:T(8,128)(2,1)}, bf16[5504,128]{1,0:T(8,128)(2,1)}, u32[]{:S(2)}, u32[]{:S(2)}) %collective-permute-start.6) | collective-permute-done | bytes 1409056 | tf_op jit(solution)/shard_map/ppermute | solution.py:640
  100.3 3.9 %collective-permute-start.11 = (s16[192,2176]{1,0:T(8,128)(2,1)S(1)}, s16[192,2176]{1,0:T(8,128)(2,1)S(1)}, u32[]{:S(2)}, u32[]{:S(2)}) collective-permute-start(s16[192,2176]{1,0:T(8,128)(2,1)S(1)} %get-tuple-element.72), channel_id=1, source_target_pairs={{4,0},{6,2},{12,8},{14,10},{8,12},{22,18},{16,20},{18,22},{24,28},... | collective-permute-start | bytes 2506760 | tf_op jit(solution)/shard_map/ppermute | solution.py:595
  104.3 1.5 broadcast_select_fusion
  109.6 12.0 %ladder.8 = (s16[192,2176]{1,0:T(8,128)(2,1)S(1)}, s16[192,2176]{1,0:T(8,128)(2,1)S(1)}, s16[192,2176]{1,0:T(8,128)(2,1)S(1)}, s16[192,2176]{1,0:T(8,128)(2,1)S(1)}) custom-call(s32[87]{0:T(128)S(1)} %concatenate.3.tab, s32[64,128]{1,0:T(8,128)S(1)} %bitcast.29, bf16[5504,128]{1,0:T(8,128)(2,1)S(1)} %collective-permute-done.5.refs_0_, ...), custom_call_target="tpu_custom_call" | custom-call | flops 4294967296 | bytes 16777216 | tf_op jit(solution)/shard_map/ladder/pallas_call | solution.py:354
  122.5 2.3 %collective-permute-start.15 = (s16[192,2176]{1,0:T(8,128)(2,1)S(1)}, s16[192,2176]{1,0:T(8,128)(2,1)S(1)}, u32[]{:S(2)}, u32[]{:S(2)}) collective-permute-start(s16[192,2176]{1,0:T(8,128)(2,1)S(1)} %get-tuple-element.75), channel_id=1, source_target_pairs={{6,4},{12,14},{18,16},{24,26},{7,5},{13,15},{19,17},{25,27}} | collective-permute-start | bytes 2506760 | tf_op jit(solution)/shard_map/ppermute | solution.py:595
  127.7 12.5 %collective-permute-done.12.refs_3_ = s16[192,2176]{1,0:T(8,128)(2,1)S(1)} collective-permute-done((s16[192,2176]{1,0:T(8,128)(2,1)}, s16[192,2176]{1,0:T(8,128)(2,1)S(1)}, u32[]{:S(2)}, u32[]{:S(2)}) %collective-permute-start.12) | collective-permute-done | bytes 835616 | tf_op jit(solution)/shard_map/ppermute | solution.py:595
  141.3 7.4 %collective-permute-start.18 = (bf16[5504,128]{1,0:T(8,128)(2,1)S(1)}, bf16[5504,128]{1,0:T(8,128)(2,1)S(1)}, u32[]{:S(2)}, u32[]{:S(2)}) collective-permute-start(bf16[5504,128]{1,0:T(8,128)(2,1)S(1)} %collective-permute-done.9.refs_0_), channel_id=1, source_target_pairs={{0,2},{2,0},{4,6},{6,4},{1,3},{3,1},{5,7},{7,5},{8,10},{10,8},{12,... | collective-permute-start | bytes 4227080 | tf_op jit(solution)/shard_map/ppermute | solution.py:607
  148.8 2.4 %select_reduce_fusion = (f32[2,2048]{1,0:T(2,128)S(1)}, f32[2,2048]{1,0:T(2,128)S(1)}) fusion(s32[2,2048]{1,0:T(2,128)S(1)} %get-tuple-element.119, f32[256]{0:T(256)S(1)} %copy-done.20, s32[2048]{0:T(1024)S(1)} %get-tuple-element.172), kind=kLoop, calls=%fused_computation.2 | loop fusion | flops 6283264 | bytes 58368 | tf_op jit(solution)/shard_map/reduce_sum | solution.py:18
  151.5 10.1 %ladder.9 = (s16[192,2176]{1,0:T(8,128)(2,1)S(1)}, s16[192,2176]{1,0:T(8,128)(2,1)}, s16[192,2176]{1,0:T(8,128)(2,1)}, s16[192,2176]{1,0:T(8,128)(2,1)}) custom-call(s32[87]{0:T(128)S(1)} %concatenate.3.tab, s32[64,128]{1,0:T(8,128)S(1)} %bitcast.30, bf16[5504,128]{1,0:T(8,128)(2,1)S(1)} %collective-permute-done.9.refs_0_, ...), custom_call_target="tpu_custom_call" | custom-call | flops 4294967296 | bytes 16777216 | tf_op jit(solution)/shard_map/ladder/pallas_call | solution.py:354
  162.5 1.4 collective-permute-start.19
  169.0 1.6 fusion.3.line
  170.7 13.8 %collective-permute-done.20.refs_10_ = s16[192,2176]{1,0:T(8,128)(2,1)} collective-permute-done((s16[192,2176]{1,0:T(8,128)(2,1)}, s16[192,2176]{1,0:T(8,128)(2,1)}, u32[]{:S(2)}, u32[]{:S(2)}) %collective-permute-start.20) | collective-permute-done | bytes 835616 | tf_op jit(solution)/shard_map/ppermute | solution.py:595
  184.5 1.9 collective-permute-done.21.refs_11_
  189.9 9.1 %finish.1 = f32[2,256,2048]{2,1,0:T(8,128)} custom-call(s32[87]{0:T(128)S(1)} %concatenate.3.tab, s32[2,256,1]{2,1,0:T(8,128)S(1)} %fusion.3.line, f32[2,256,1]{2,1,0:T(8,128)S(1)} %copy.61.hole, f32[2,1,2048]{2,1,0:T(1,128)S(1)} %add.804.pair, s32[2,1,2048]{2,1,0:T(1,128)S(1)} %and_convert_fusion.pair_ok, s16[192,2176]{1,0:T(8,128)(2,1)S(1)} %get-tuple-element.78.refs_0_, ...), custom_call_target="tpu_custom_call" | custom-call | tf_op jit(solution)/shard_map/finish/pallas_call | solution.py:468
  (181 shorter events, 40.9 us)
Async XLA Ops:
  6.5 27.6 %collective-permute-start.4 = (bf16[2,2048,2048]{2,1,0:T(8,128)(2,1)}, bf16[2,2048,2048]{2,1,0:T(8,128)(2,1)}, u32[]{:S(2)}, u32[]{:S(2)}) collective-permute-start(bf16[2,2048,2048]{2,1,0:T(8,128)(2,1)} %refs_3_.7), channel_id=1, source_target_pairs={{0,2},{2,0},{4,6},{6,4},{1,3},{3,1},{5,7},{7,5},{8,10},{10,8},{12,... | collective-permute-start | bytes 50331656 | tf_op jit(solution)/shard_map/ppermute | solution.py:607
  21.2 12.9 %collective-permute-start.3 = (bf16[5504,128]{1,0:T(8,128)(2,1)S(1)}, bf16[5504,128]{1,0:T(8,128)(2,1)}, u32[]{:S(2)}, u32[]{:S(2)}) collective-permute-start(bf16[5504,128]{1,0:T(8,128)(2,1)S(1)} %slice.27.refs_0_), channel_id=1, source_target_pairs={{0,2},{2,0},{4,6},{6,4},{1,3},{3,1},{5,7},{7,5},{8,10},{10,8},{12,... | collective-permute-start | bytes 4227080 | tf_op jit(solution)/shard_map/ppermute | solution.py:607
  22.4 33.3 %collective-permute-start.1 = (bf16[5504,128]{1,0:T(8,128)(2,1)S(1)}, bf16[5504,128]{1,0:T(8,128)(2,1)}, u32[]{:S(2)}, u32[]{:S(2)}) collective-permute-start(bf16[5504,128]{1,0:T(8,128)(2,1)S(1)} %slice.27.refs_0_), channel_id=1, source_target_pairs={{0,8},{8,16},{16,24},{1,9},{9,17},{17,25},{2,10},{10,18},{18,26},{... | collective-permute-start | bytes 4227080 | tf_op jit(solution)/shard_map/ppermute | solution.py:631
  26.7 34.0 %collective-permute-start.2 = (bf16[5504,128]{1,0:T(8,128)(2,1)S(1)}, bf16[5504,128]{1,0:T(8,128)(2,1)}, u32[]{:S(2)}, u32[]{:S(2)}) collective-permute-start(bf16[5504,128]{1,0:T(8,128)(2,1)S(1)} %slice.27.refs_0_), channel_id=1, source_target_pairs={{8,0},{16,8},{24,16},{9,1},{17,9},{25,17},{10,2},{18,10},{26,18},{... | collective-permute-start | bytes 4227080 | tf_op jit(solution)/shard_map/ppermute | solution.py:632
  31.1 33.0 %copy-start.21 = (f32[128]{0:T(128)S(1)}, f32[128]{0:T(128)}, u32[]{:S(2)}) copy-start(f32[128]{0:T(128)} %param.11) | copy-start | bytes 1540
  60.7 4.5 %collective-permute-start.8 = (bf16[5504,128]{1,0:T(8,128)(2,1)}, bf16[5504,128]{1,0:T(8,128)(2,1)}, u32[]{:S(2)}, u32[]{:S(2)}) collective-permute-start(bf16[5504,128]{1,0:T(8,128)(2,1)} %collective-permute-done.1.refs_0_), channel_id=1, source_target_pairs={{0,2},{2,0},{4,6},{6,4},{1,3},{3,1},{5,7},{7,5},{8,10},{10,8},{12,... | collective-permute-start | bytes 4227080 | tf_op jit(solution)/shard_map/ppermute | solution.py:607
  62.0 5.2 %collective-permute-start.7 = (bf16[5504,128]{1,0:T(8,128)(2,1)}, bf16[5504,128]{1,0:T(8,128)(2,1)}, u32[]{:S(2)}, u32[]{:S(2)}) collective-permute-start(bf16[5504,128]{1,0:T(8,128)(2,1)} %collective-permute-done.2.refs_0_), channel_id=1, source_target_pairs={{0,2},{2,0},{4,6},{6,4},{1,3},{3,1},{5,7},{7,5},{8,10},{10,8},{12,... | collective-permute-start | bytes 4227080 | tf_op jit(solution)/shard_map/ppermute | solution.py:607
  62.0 18.5 %collective-permute-start.5 = (bf16[5504,128]{1,0:T(8,128)(2,1)}, bf16[5504,128]{1,0:T(8,128)(2,1)S(1)}, u32[]{:S(2)}, u32[]{:S(2)}) collective-permute-start(bf16[5504,128]{1,0:T(8,128)(2,1)} %collective-permute-done.1.refs_0_), channel_id=1, source_target_pairs={{8,16},{16,24},{9,17},{17,25},{10,18},{18,26},{11,19},{19,27},{12,... | collective-permute-start | bytes 4227080 | tf_op jit(solution)/shard_map/ppermute | solution.py:639
  62.8 35.4 %collective-permute-start.6 = (bf16[5504,128]{1,0:T(8,128)(2,1)}, bf16[5504,128]{1,0:T(8,128)(2,1)}, u32[]{:S(2)}, u32[]{:S(2)}) collective-permute-start(bf16[5504,128]{1,0:T(8,128)(2,1)} %collective-permute-done.2.refs_0_), channel_id=1, source_target_pairs={{8,0},{16,8},{9,1},{17,9},{10,2},{18,10},{11,3},{19,11},{12,4},{20... | collective-permute-start | bytes 4227080 | tf_op jit(solution)/shard_map/ppermute | solution.py:640
  98.2 8.9 %collective-permute-start.13 = (bf16[5504,128]{1,0:T(8,128)(2,1)S(1)}, bf16[5504,128]{1,0:T(8,128)(2,1)S(1)}, u32[]{:S(2)}, u32[]{:S(2)}) collective-permute-start(bf16[5504,128]{1,0:T(8,128)(2,1)S(1)} %collective-permute-done.5.refs_0_), channel_id=1, source_target_pairs={{0,2},{2,0},{4,6},{6,4},{1,3},{3,1},{5,7},{7,5},{8,10},{10,8},{12,... | collective-permute-start | bytes 4227080 | tf_op jit(solution)/shard_map/ppermute | solution.py:607
  99.6 8.9 %collective-permute-start.14 = (bf16[5504,128]{1,0:T(8,128)(2,1)}, bf16[5504,128]{1,0:T(8,128)(2,1)S(1)}, u32[]{:S(2)}, u32[]{:S(2)}) collective-permute-start(bf16[5504,128]{1,0:T(8,128)(2,1)} %collective-permute-done.6.refs_2_), channel_id=1, source_target_pairs={{0,2},{2,0},{4,6},{6,4},{1,3},{3,1},{5,7},{7,5},{8,10},{10,8},{12,... | collective-permute-start | bytes 4227080 | tf_op jit(solution)/shard_map/ppermute | solution.py:607
  99.6 25.2 %collective-permute-start.10 = (s16[192,2176]{1,0:T(8,128)(2,1)S(1)}, s16[192,2176]{1,0:T(8,128)(2,1)S(1)}, u32[]{:S(2)}, u32[]{:S(2)}) collective-permute-start(s16[192,2176]{1,0:T(8,128)(2,1)S(1)} %get-tuple-element.71), channel_id=1, source_target_pairs={{2,0},{0,2},{10,8},{8,10},{14,12},{16,18},{22,20},{20,22},{30,28},... | collective-permute-start | bytes 2506760 | tf_op jit(solution)/shard_map/ppermute | solution.py:595
  100.3 26.1 %collective-permute-start.11 = (s16[192,2176]{1,0:T(8,128)(2,1)S(1)}, s16[192,2176]{1,0:T(8,128)(2,1)S(1)}, u32[]{:S(2)}, u32[]{:S(2)}) collective-permute-start(s16[192,2176]{1,0:T(8,128)(2,1)S(1)} %get-tuple-element.72), channel_id=1, source_target_pairs={{4,0},{6,2},{12,8},{14,10},{8,12},{22,18},{16,20},{18,22},{24,28},... | collective-permute-start | bytes 2506760 | tf_op jit(solution)/shard_map/ppermute | solution.py:595
  105.8 34.5 %collective-permute-start.9 = (bf16[5504,128]{1,0:T(8,128)(2,1)S(1)}, bf16[5504,128]{1,0:T(8,128)(2,1)S(1)}, u32[]{:S(2)}, u32[]{:S(2)}) collective-permute-start(bf16[5504,128]{1,0:T(8,128)(2,1)S(1)} %broadcast_select_fusion), channel_id=1, source_target_pairs={{16,24},{8,0},{17,25},{9,1},{18,26},{10,2},{19,27},{11,3},{20,28},... | collective-permute-start | bytes 4227080 | tf_op jit(solution)/shard_map/ppermute | solution.py:644
  107.1 41.7 %copy-start.20 = (f32[256]{0:T(256)S(1)}, f32[256]{0:T(256)}, u32[]{:S(2)}) copy-start(f32[256]{0:T(256)} %param.10) | copy-start | bytes 3076
  107.1 33.1 %collective-permute-start.12 = (s16[192,2176]{1,0:T(8,128)(2,1)}, s16[192,2176]{1,0:T(8,128)(2,1)S(1)}, u32[]{:S(2)}, u32[]{:S(2)}) collective-permute-start(s16[192,2176]{1,0:T(8,128)(2,1)} %get-tuple-element.73), channel_id=1, source_target_pairs={{6,0},{4,2},{14,8},{12,10},{10,12},{20,18},{18,20},{16,22},{26,28}... | collective-permute-start | bytes 2506760 | tf_op jit(solution)/shard_map/ppermute | solution.py:595
  122.5 17.7 %collective-permute-start.15 = (s16[192,2176]{1,0:T(8,128)(2,1)S(1)}, s16[192,2176]{1,0:T(8,128)(2,1)S(1)}, u32[]{:S(2)}, u32[]{:S(2)}) collective-permute-start(s16[192,2176]{1,0:T(8,128)(2,1)S(1)} %get-tuple-element.75), channel_id=1, source_target_pairs={{6,4},{12,14},{18,16},{24,26},{7,5},{13,15},{19,17},{25,27}} | collective-permute-start | bytes 2506760 | tf_op jit(solution)/shard_map/ppermute | solution.py:595
  125.7 14.6 %collective-permute-start.16 = (s16[192,2176]{1,0:T(8,128)(2,1)S(1)}, s16[192,2176]{1,0:T(8,128)(2,1)S(1)}, u32[]{:S(2)}, u32[]{:S(2)}) collective-permute-start(s16[192,2176]{1,0:T(8,128)(2,1)S(1)} %get-tuple-element.76), channel_id=1, source_target_pairs={{0,4},{10,14},{20,16},{30,26},{1,5},{11,15},{21,17},{31,27}} | collective-permute-start | bytes 2506760 | tf_op jit(solution)/shard_map/ppermute | solution.py:595
  126.4 35.2 %copy-start.5 = (s16[192,2176]{1,0:T(8,128)(2,1)}, s16[192,2176]{1,0:T(8,128)(2,1)S(1)}, u32[]{:S(2)}) copy-start(s16[192,2176]{1,0:T(8,128)(2,1)S(1)} %collective-permute-done.11.refs_2_) | copy-start | bytes 2506756
  126.4 13.8 %collective-permute-start.17 = (s16[192,2176]{1,0:T(8,128)(2,1)S(1)}, s16[192,2176]{1,0:T(8,128)(2,1)S(1)}, u32[]{:S(2)}, u32[]{:S(2)}) collective-permute-start(s16[192,2176]{1,0:T(8,128)(2,1)S(1)} %get-tuple-element.77), channel_id=1, source_target_pairs={{2,4},{8,14},{22,16},{28,26},{3,5},{9,15},{23,17},{29,27}} | collective-permute-start | bytes 2506760 | tf_op jit(solution)/shard_map/ppermute | solution.py:595
  141.3 10.2 %collective-permute-start.18 = (bf16[5504,128]{1,0:T(8,128)(2,1)S(1)}, bf16[5504,128]{1,0:T(8,128)(2,1)S(1)}, u32[]{:S(2)}, u32[]{:S(2)}) collective-permute-start(bf16[5504,128]{1,0:T(8,128)(2,1)S(1)} %collective-permute-done.9.refs_0_), channel_id=1, source_target_pairs={{0,2},{2,0},{4,6},{6,4},{1,3},{3,1},{5,7},{7,5},{8,10},{10,8},{12,... | collective-permute-start | bytes 4227080 | tf_op jit(solution)/shard_map/ppermute | solution.py:607
  162.5 8.2 %collective-permute-start.19 = (s16[192,2176]{1,0:T(8,128)(2,1)}, s16[192,2176]{1,0:T(8,128)(2,1)}, u32[]{:S(2)}, u32[]{:S(2)}) collective-permute-start(s16[192,2176]{1,0:T(8,128)(2,1)} %get-tuple-element.88), channel_id=1, source_target_pairs={{4,6},{26,24},{5,7},{27,25}} | collective-permute-start | bytes 2506760 | tf_op jit(solution)/shard_map/ppermute | solution.py:595
  163.9 20.6 %collective-permute-start.20 = (s16[192,2176]{1,0:T(8,128)(2,1)}, s16[192,2176]{1,0:T(8,128)(2,1)}, u32[]{:S(2)}, u32[]{:S(2)}) collective-permute-start(s16[192,2176]{1,0:T(8,128)(2,1)} %get-tuple-element.89), channel_id=1, source_target_pairs={{2,6},{28,24},{3,7},{29,25}} | collective-permute-start | bytes 2506760 | tf_op jit(solution)/shard_map/ppermute | solution.py:595
  165.2 21.2 %collective-permute-start.21 = (s16[192,2176]{1,0:T(8,128)(2,1)}, s16[192,2176]{1,0:T(8,128)(2,1)}, u32[]{:S(2)}, u32[]{:S(2)}) collective-permute-start(s16[192,2176]{1,0:T(8,128)(2,1)} %get-tuple-element.90), channel_id=1, source_target_pairs={{0,6},{30,24},{1,7},{31,25}} | collective-permute-start | bytes 2506760 | tf_op jit(solution)/shard_map/ppermute | solution.py:595
  (19 other events, 143.7 us)

commit v3 on v2

--- a/solution.py
+++ b/solution.py
@@ -9,7 +9,7 @@
 F32, BF16, I32, I16 = jnp.float32, jnp.bfloat16, jnp.int32, jnp.int16
 LANES = 128
 TILE_ROWS = 16
-ANY = pl.BlockSpec(memory_space=pltpu.HBM)
+ANY = pl.BlockSpec(memory_space=pl.ANY)
 
 
 def table_value(values_table, positions):
@@ -121,7 +121,9 @@
         self.at_self = self.at_reps + self.syms * rows
         self.at_more = self.at_self + self.syms * rows
         self.base_tiles = self.pay_tiles * 43 // 64
-        self.enc_shape = (self.enc_tiles * TILE_ROWS, self.pairs + LANES)
+        enc_rows = self.enc_tiles * TILE_ROWS
+        self.enc_shapes = [(enc_rows, self.pairs + LANES)] * rows
+        self.far_shapes = self.enc_shapes[:-1] + [(self.share // 2, self.pairs + LANES)]
 
 
 def row_counts(plan, tab, sym, share):
@@ -136,11 +138,9 @@
 
 def pack_kernel(plan, tab, amp, dest, rel, pay, acc):
     pay[...] = jnp.zeros_like(pay)
-    row = tab[0]
     base = jnp.int32(0)
     for sym in range(plan.syms):
-        _, _, nrt = row_counts(plan, tab, sym, row)
-        ndt = tab[plan.at_ndt + sym]
+        ndt, nrt = tab[sym], tab[plan.syms + sym]
         pick = (
             lax.broadcasted_iota(I32, (plan.share, plan.share), 0) == dest[sym : sym + 1, :]
         ).astype(BF16)
@@ -154,7 +154,7 @@
                 (((1,), (1,)), ((), ())),
                 preferred_element_type=F32,
             )
-            first = tab[plan.at_first + at]
+            first = tab[2 * plan.syms + at]
             acc[first] += placed[:, :LANES]
             acc[first + 1] += placed[:, LANES:]
 
@@ -337,11 +337,13 @@
 
         lax.fori_loop(0, padded(reps) + padded(selfs), chunk, 0)
 
-        for flip, out in enumerate(outs):
-
-            @pl.when((col ^ share) == flip)
-            def _():
-                copy = pltpu.make_async_copy(enc, out, sems.at[0])
+        flip = col ^ share
+        slot = flip if kind[0] < 2 else jnp.where(flip < 2, flip, 2 + sym)
+        for number, out in enumerate(outs):
+
+            @pl.when(slot == number)
+            def _(out=out):
+                copy = pltpu.make_async_copy(enc.at[pl.ds(0, out.shape[0])], out, sems.at[0])
                 copy.start()
                 copy.wait()
 
@@ -353,7 +355,10 @@
     first_enc = 5 + len(pays)
     return pl.pallas_call(
         functools.partial(ladder_kernel, plan, kind, len(pays), pays[0].shape[0]),
-        out_shape=[jax.ShapeDtypeStruct(plan.enc_shape, I16)] * n,
+        out_shape=[
+            jax.ShapeDtypeStruct(shape, I16)
+            for shape in (plan.enc_shapes if kind[0] < 2 else plan.far_shapes)
+        ],
         in_specs=[smem, vmem] + [ANY] * (len(pays) + 3 + len(encs)),
         out_specs=[ANY] * n,
         scratch_shapes=[
@@ -361,12 +366,12 @@
             pltpu.VMEM((2, steps, plan.pairs // steps, plan.width), BF16),
             pltpu.VMEM((2, plan.share, plan.width), BF16),
             pltpu.VMEM((plan.share, plan.pairs), F32),
-            pltpu.VMEM(plan.enc_shape, I16),
+            pltpu.VMEM(plan.enc_shapes[0], I16),
             pltpu.SemaphoreType.DMA((2,)),
             pltpu.SemaphoreType.DMA((2, steps)),
         ],
         input_output_aliases={first_enc + i: i for i in range(len(encs))},
-        compiler_params=pltpu.CompilerParams(vmem_limit_bytes=48 << 20),
+        compiler_params=pltpu.CompilerParams(vmem_limit_bytes=34 << 20),
         cost_estimate=pl.CostEstimate(
             flops=2 * plan.syms * plan.share * plan.width * plan.pairs,
             bytes_accessed=2 * plan.syms * plan.width * plan.pairs,
@@ -376,18 +381,20 @@
     )(tab, rel, *pays, rest, integrals, sib_integrals, *encs)
 
 
-def finish_kernel(plan, wtile, tab, line, hole, pair, pair_ok, *refs):
+def finish_kernel(plan, numbers, wtile, tab, line, hole, pair, pair_ok, *refs):
     n = plan.rows
-    out, held, pick, sems = refs[-4:]
-    away_sets = [refs[n * i : n * (i + 1)] for i in range(n - 1)]
-    step = pl.program_id(0)
+    out, held, pick, whole, sems, out_sems = refs[-6:]
     row, col = tab[0], tab[1]
     core = lax.rem(col, 2)
-
-    def fetch(sources):
-        parts = [(core, 0), (1 - core, 0), (core, 1), (1 - core, 1)]
+    which = jnp.maximum(jnp.abs(row - col) - 1, 0)
+    steps = plan.pairs // wtile
+
+    def fetch(sources, by_sym):
+        parts = [(core, 0), (1 - core, 0)] + ([(0, 1), (1, 1)] if by_sym else [(core, 1), (1 - core, 1)])
         copies = [
-            pltpu.make_async_copy(ref, held.at[sym, side], sems.at[number])
+            pltpu.make_async_copy(
+                ref, held.at[sym, side, pl.ds(0, ref.shape[0])], sems.at[number]
+            )
             for number, (ref, (sym, side)) in enumerate(zip(sources, parts))
         ]
         for copy in copies:
@@ -395,85 +402,101 @@
         places = lax.broadcasted_iota(I32, pick.shape[2:], 1)
         for sym in range(plan.syms):
             for half in range(2):
-                pick[sym, half] = (places + half * pick.shape[3] == line[sym]).astype(BF16)
+                pick[sym, half] = (places + half * pick.shape[3] == line[sym, :, 0:1]).astype(BF16)
         for copy in copies:
             copy.wait()
 
-    which = jnp.maximum(jnp.abs(row - col) - 1, 0)
-    for number, sources in enumerate(away_sets):
-
-        @pl.when((step == 0) & (which == number))
-        def _(sources=sources):
-            fetch(sources)
-
-    fbase = row * (plan.pairs // plan.virt_slots) + step * (wtile // plan.virt_slots)
-    for sym in range(plan.syms):
-        count = plan.enc_shape[0] if sym == 0 else plan.share // 2
-        reps, selfs, _ = row_counts(plan, tab, sym, col)
-        live = lax.broadcasted_iota(I32, (count, LANES), 0) < (
-            padded(reps) + padded(selfs)
-        ) * TILE_ROWS
-        scales = [
-            jnp.exp2(
-                -held[sym, side, pl.ds(0, count), pl.ds(plan.pairs, LANES)].astype(I32).astype(F32)
-            )
-            for side in range(2)
-        ]
-        terms = [[], []]
-        for v in range(wtile // LANES):
-            lanes = pl.ds(pl.multiple_of(step * wtile + v * LANES, LANES), LANES)
-            left = jnp.where(
-                live,
-                held[sym, 0, pl.ds(0, count), lanes].astype(I32).astype(F32) * scales[0]
-                + held[sym, 1, pl.ds(0, count), lanes].astype(I32).astype(F32) * scales[1],
-                0.0,
-            )
-            for term in terms:
-                term.append(left.astype(BF16))
-                left = left - term[-1].astype(F32)
-        terms = [jnp.concatenate(term, axis=1) for term in terms]
-        halves = []
-        for half in range(2):
-            total = None
-            for term in terms:
-                part = jnp.dot(pick[sym, half, :, :count], term, preferred_element_type=F32)
-                total = part if total is None else total + part
-            halves.append(total)
-        for v in range(wtile // LANES):
-            lanes = slice(v * LANES, (v + 1) * LANES)
-            result = halves[0][:, lanes] + lane_take(
-                halves[1][:, lanes], lane_mates(plan, plan.share, sym, fbase, v)
-            )
-            allowed = (line[sym] >= 0) & (pair_ok[sym, :, lanes] > 0)
-            out[sym, :, lanes] = jnp.where(
-                allowed, result / (pair[sym, :, lanes] - hole[sym]), 0.0
-            )
-
-
-def finish(plan, tab, line, hole, pair, pair_ok, sources):
+    for place, number in enumerate(numbers):
+
+        @pl.when(which == number)
+        def _(sources=refs[n * place : n * (place + 1)], by_sym=number > 0):
+            fetch(sources, by_sym)
+
+    def put(step):
+        lanes = pl.ds(pl.multiple_of(step * wtile, wtile), wtile)
+        return pltpu.make_async_copy(whole.at[:, :, lanes], out.at[:, :, lanes], out_sems.at[step])
+
+    def tile(step, _):
+        fbase = row * (plan.pairs // plan.virt_slots) + step * (wtile // plan.virt_slots)
+        for sym in range(plan.syms):
+            count = plan.enc_shapes[0][0] if sym == 0 else plan.share // 2
+            reps, selfs, _ = row_counts(plan, tab, sym, col)
+            live = lax.broadcasted_iota(I32, (count, LANES), 0) < (
+                padded(reps) + padded(selfs)
+            ) * TILE_ROWS
+            scales = [
+                jnp.exp2(
+                    -held[sym, side, pl.ds(0, count), pl.ds(plan.pairs, LANES)]
+                    .astype(I32)
+                    .astype(F32)
+                )
+                for side in range(2)
+            ]
+            spans = [
+                pl.ds(pl.multiple_of(step * wtile + v * LANES, LANES), LANES)
+                for v in range(wtile // LANES)
+            ]
+            terms = [[], []]
+            for lanes in spans:
+                left = jnp.where(
+                    live,
+                    held[sym, 0, pl.ds(0, count), lanes].astype(I32).astype(F32) * scales[0]
+                    + held[sym, 1, pl.ds(0, count), lanes].astype(I32).astype(F32) * scales[1],
+                    0.0,
+                )
+                for term in terms:
+                    term.append(left.astype(BF16))
+                    left = left - term[-1].astype(F32)
+            terms = [jnp.concatenate(term, axis=1) for term in terms]
+            halves = []
+            for half in range(2):
+                total = None
+                for term in terms:
+                    part = jnp.dot(pick[sym, half, :, :count], term, preferred_element_type=F32)
+                    total = part if total is None else total + part
+                halves.append(total)
+            for v, lanes in enumerate(spans):
+                cut = slice(v * LANES, (v + 1) * LANES)
+                result = halves[0][:, cut] + lane_take(
+                    halves[1][:, cut], lane_mates(plan, plan.share, sym, fbase, v)
+                )
+                allowed = (line[sym] >= 0) & (pair_ok[sym, :, lanes] > 0)
+                whole[sym, :, lanes] = jnp.where(
+                    allowed, result / (pair[sym, :, lanes] - hole[sym]), 0.0
+                )
+        put(step).start()
+        return 0
+
+    def drain(step, _):
+        put(step).wait()
+        return 0
+
+    @pl.when((which >= numbers[0]) & (which <= numbers[-1]))
+    def _():
+        lax.fori_loop(0, steps, tile, 0)
+        lax.fori_loop(0, steps, drain, 0)
+
+
+def finish(plan, numbers, tab, line, hole, pair, pair_ok, sources, before):
     wtile = min(256, plan.pairs)
-    whole = lambda shape: pl.BlockSpec(shape, lambda i, tab: (0,) * len(shape))
-    tiled = pl.BlockSpec((plan.syms, 1, wtile), lambda i, tab: (0, 0, i))
-    grid_spec = pltpu.PrefetchScalarGridSpec(
-        num_scalar_prefetch=1,
-        grid=(plan.pairs // wtile,),
-        in_specs=[whole(line.shape), whole(hole.shape), tiled, tiled] + [ANY] * len(sources),
-        out_specs=pl.BlockSpec((plan.syms, plan.share, wtile), lambda i, tab: (0, 0, i)),
+    smem, vmem = (pl.BlockSpec(memory_space=space) for space in (pltpu.SMEM, pltpu.VMEM))
+    out = jax.ShapeDtypeStruct((plan.syms, plan.share, plan.pairs), F32)
+    return pl.pallas_call(
+        functools.partial(finish_kernel, plan, numbers, wtile),
+        out_shape=out,
+        in_specs=[smem] + [vmem] * 4 + [ANY] * (len(sources) + len(before)),
+        out_specs=ANY,
         scratch_shapes=[
-            pltpu.VMEM((plan.syms, 2) + plan.enc_shape, I16),
-            pltpu.VMEM((plan.syms, 2, plan.share, plan.enc_shape[0]), BF16),
+            pltpu.VMEM((plan.syms, 2) + plan.enc_shapes[0], I16),
+            pltpu.VMEM((plan.syms, 2, plan.share, plan.enc_shapes[0][0]), BF16),
+            pltpu.VMEM(out.shape, F32),
             pltpu.SemaphoreType.DMA((4,)),
+            pltpu.SemaphoreType.DMA((plan.pairs // wtile,)),
         ],
-    )
-    return pl.pallas_call(
-        functools.partial(finish_kernel, plan, wtile),
-        out_shape=jax.ShapeDtypeStruct((plan.syms, plan.share, plan.pairs), F32),
-        grid_spec=grid_spec,
-        compiler_params=pltpu.CompilerParams(
-            dimension_semantics=("arbitrary",), vmem_limit_bytes=48 << 20
-        ),
+        input_output_aliases={5 + len(sources): 0} if before else {},
+        compiler_params=pltpu.CompilerParams(vmem_limit_bytes=30 << 20),
         name="finish",
-    )(tab, line, hole, pair, pair_ok, *sources)
+    )(tab, line, hole, pair, pair_ok, *sources, *before)
 
 
 def occupied_share(plan, counts, share_number):
@@ -556,6 +579,8 @@
     n_rep = jnp.sum(is_rep.astype(I32), axis=-1, keepdims=True)
     dest = jnp.where(is_self, 2 * n_rep + self_rank, jnp.where(is_rep, rank, n_rep + rank))
     dest = jnp.where(ok, dest, -1)
+    n_valid = jnp.sum(ok.astype(I32), axis=-1)
+    pack_tab = jnp.concatenate([ndt[0], padded(n_valid), firsts[0].reshape(-1)])
     first, second, ok, is_rep, is_self, rank, self_rank = occupied_share(
         plan, occupied_count, 2 * col + occ
     )
@@ -574,10 +599,11 @@
     return (
         more,
         tab,
+        pack_tab,
         dest,
         rel.reshape(2 * syms * plan.tiles, LANES),
-        line[:, :, None],
-        hole[:, :, None],
+        jnp.broadcast_to(line[:, :, None], line.shape + (LANES,)),
+        jnp.broadcast_to(hole[:, :, None], hole.shape + (LANES,)),
         pair[:, None, :],
         pair_ok.astype(I32)[:, None, :],
     )
@@ -585,14 +611,19 @@
 
 def to_roots(plan, encs, distances):
     received = [encs[0]]
-    for flip in range(1, plan.rows):
-        pairs = [
-            (row * plan.rows + (root ^ flip), row * plan.rows + root)
-            for row in range(plan.rows)
-            for root in range(plan.rows)
-            if abs(row - root) in distances
-        ]
-        received.append(lax.ppermute(encs[flip], ("row", "col"), pairs))
+    roots = [
+        (row, root)
+        for row in range(plan.rows)
+        for root in range(plan.rows)
+        if abs(row - root) in distances
+    ]
+    for slot in range(1, len(encs)):
+        if slot == 1 or 1 in distances:
+            source = lambda root: root ^ slot
+        else:
+            source = lambda root: (root ^ 2) // 2 * 2 + slot - 2
+        pairs = [(row * plan.rows + source(root), row * plan.rows + root) for row, root in roots]
+        received.append(lax.ppermute(encs[slot], ("row", "col"), pairs))
     return received
 
 
@@ -606,10 +637,10 @@
     swap = [(i, i ^ 1) for i in range(n)]
     sibling = lambda x: lax.ppermute(x, "col", swap)
     sib_integrals = sibling(integrals)
-    more, tab, dest, rel, line, hole, pair, pair_ok = line_tables(
+    more, tab, pack_tab, dest, rel, *tables = line_tables(
         plan, virtual_energy, occupied_energy, virtual_count, occupied_count
     )
-    packed = pack(plan, tab, amplitudes, dest, rel)
+    packed = pack(plan, pack_tab, amplitudes, dest, rel)
     base_rows = plan.base_tiles * TILE_ROWS
     all_rows = plan.pay_tiles * TILE_ROWS
     pay = packed[:base_rows]
@@ -633,7 +664,7 @@
     encs = work((0, ""), [pay], [])
     sources = []
     for step in range(2, n):
-        right, left, encs = lax.optimization_barrier((right, left, encs))
+        right, left, encs, tables = lax.optimization_barrier((right, left, encs, tables))
         if step < n - 1:
             ahead = (
                 lax.ppermute(right, "row", [(i, i + 1) for i in range(step - 1, n - 1)]),
@@ -652,8 +683,11 @@
             right, left = ahead
     sources += to_roots(plan, encs, (n - 2,))
     last, sources = lax.optimization_barrier((last, sources))
-    sources += to_roots(plan, work((n - 1, ""), [last], []), (n - 1,))
-    return finish(plan, tab, line, hole, pair, pair_ok, sources)
+    encs = work((n - 1, ""), [last], [])
+    near_tab, encs = lax.optimization_barrier((tab, encs))
+    far = to_roots(plan, encs, (n - 1,))
+    update = finish(plan, tuple(range(n - 2)), near_tab, *tables, sources, [])
+    return finish(plan, (n - 2,), tab, *tables, far, [update])
 
 
 def solution(mesh):

time: 207 us -> 190 us (0.918)
  local copies, waits for them, and re-layouts: 19.2 us -> 11.6 us
  starting transfers between devices: 33.6 us -> 26.5 us
  other arithmetic: 15.9 us -> 13.2 us
  waiting for transfers between devices: 63 us -> 65.5 us
    ppermute x9, waiting for transfers between devices: 28.2 us -> 35.8 us  [to_roots(): received.append(lax.ppermute(encs[slot], ('row', 'col'), pairs))]
    ppermute x7, starting transfers between devices: 11 us -> 4.07 us  [on_device_line(): sibling = lambda x: lax.ppermute(x, 'col', swap)]
    unnamed x48 -> x24, local copies, waits for them, and re-layouts: 13.2 us -> 6.58 us
    ppermute x1, waiting for transfers between devices: 7.99 us -> 3.08 us  [on_device_line(): right = lax.ppermute(pay, 'row', [(i, i + 1) for i in range(n - 1)])]
    pallas_call x1 -> x2, Pallas kernels: 9.07 us -> 7.71 us  [finish(): pl.pallas_call(functools.partial(finish_kernel, plan, numbers, wtile), ou...]
  transfers between devices with their start and end apart: 21 -> 21, of which waited for: 10 -> 10; matrix products, arithmetic and copies ran while one was open for 11% -> 9% of each run, Pallas kernels for 20% -> 21%
where the time goes in v3:
time: 190 us
  waiting for transfers between devices  65.5 us (34%)
  Pallas kernels  58 us (31%)
  starting transfers between devices  26.5 us (14%)
  between operations  14.8 us (8%)
  other arithmetic  13.2 us (7%)
  local copies, waits for them, and re-layouts  11.6 us (6%)
    pallas_call x5, Pallas kernels, ladder_call(): pl.pallas_call(functools.partial(ladder_kernel, plan, kind, len(pays), pa...  47 us
    ppermute x9, waiting for transfers between devices, to_roots(): received.append(lax.ppermute(encs[slot], ('row', 'col'), pairs))  35.8 us
    ppermute x1, waiting for transfers between devices, on_device_line(): lax.ppermute(left, 'row', [(i + 1, i) for i in range(0, n - step)])  17.4 us
    ppermute x9, starting transfers between devices, to_roots(): received.append(lax.ppermute(encs[slot], ('row', 'col'), pairs))  13.5 us
    pallas_call x2, Pallas kernels, finish(): pl.pallas_call(functools.partial(finish_kernel, plan, numbers, wtile), ou...  7.71 us
    unnamed x24, local copies, waits for them, and re-layouts  6.58 us
    reduce_sum x7, other arithmetic, table_value(): jnp.sum(jnp.where(matches, values_table, jnp.zeros((), values_table.dtype...  5.14 us
    ppermute x1, waiting for transfers between devices, on_device_line(): left = lax.ppermute(pay, 'row', [(i + 1, i) for i in range(n - 1)])  4.99 us
  transfers between devices with their start and end apart: 21, of which 10 were waited for; matrix products, arithmetic and copies ran while one was open for 9% of the time, Pallas kernels for 21%

profile of v3, /device:TPU:5, one launch (start us, length us, event | category | flops | bytes accessed | tf_op | source)
XLA Modules:
  0.0 189.6 jit_solution(9503440988300117715)
XLA Ops:
  12.8 1.6 copy-done.3
  14.4 3.3 %pack.1 = bf16[8448,128]{1,0:T(8,128)(2,1)S(1)} custom-call(s32[36]{0:T(128)S(1)} %pad_add_fusion.tab, bf16[2,256,2048]{2,1,0:T(8,128)(2,1)S(1)} %copy-done.3, s32[2,256]{1,0:T(2,128)S(1)} %get-tuple-element.159.dest, s32[64,128]{1,0:T(8,128)S(1)} %bitcast.19), custom_call_target="tpu_custom_call" | custom-call | tf_op jit(solution)/shard_map/pack/pallas_call | solution.py:172
  19.0 4.3 %collective-permute-start.1 = (bf16[5504,128]{1,0:T(8,128)(2,1)S(1)}, bf16[5504,128]{1,0:T(8,128)(2,1)}, u32[]{:S(2)}, u32[]{:S(2)}) collective-permute-start(bf16[5504,128]{1,0:T(8,128)(2,1)S(1)} %slice.39.refs_0_), channel_id=1, source_target_pairs={{0,8},{8,16},{16,24},{1,9},{9,17},{17,25},{2,10},{10,18},{18,26},{... | collective-permute-start | bytes 4227080 | tf_op jit(solution)/shard_map/ppermute | solution.py:662
  28.1 2.4 %select_reduce_fusion = (f32[2,2048]{1,0:T(2,128)S(1)}, f32[2,2048]{1,0:T(2,128)S(1)}) fusion(s32[2,2048]{1,0:T(2,128)S(1)} %get-tuple-element.142, f32[256]{0:T(256)S(1)} %copy-done.8, s32[2048]{0:T(1024)S(1)} %get-tuple-element.205), kind=kLoop, calls=%fused_computation.1 | loop fusion | flops 6283264 | bytes 58368 | tf_op jit(solution)/shard_map/reduce_sum | solution.py:18
  32.1 3.1 %conditional.1 = (bf16[2,4,2688,128]{3,2,1,0:T(8,128)(2,1)}) conditional(s32[]{:T(128)} %convert_element_type.65, () %tuple.15, bf16[8448,128]{1,0:T(8,128)(2,1)} %copy-done.5), branch_computations={%region_21.22_spmd, %region_22.23_spmd} | conditional | flops 2752512 | bytes 33718360 | solution.py:655
  32.1 3.1 %broadcast.2164 = bf16[2,4,2688,128]{3,2,1,0:T(8,128)(2,1)} broadcast(bf16[]{:T(256)} %constant.424.clone), dimensions={} | broadcast | bytes 5505026 | tf_op jit(solution)/shard_map/broadcast.54
  35.9 12.6 %ladder.5 = (s16[192,2176]{1,0:T(8,128)(2,1)S(1)}, s16[192,2176]{1,0:T(8,128)(2,1)S(1)}, s16[192,2176]{1,0:T(8,128)(2,1)S(1)}, s16[192,2176]{1,0:T(8,128)(2,1)}) custom-call(s32[87]{0:T(128)S(1)} %concatenate.6.tab, s32[64,128]{1,0:T(8,128)S(1)} %bitcast.20, bf16[5504,128]{1,0:T(8,128)(2,1)S(1)} %slice.39.refs_0_, ...), custom_call_target="tpu_custom_call" | custom-call | flops 4294967296 | bytes 16777216 | tf_op jit(solution)/shard_map/ladder/pallas_call | solution.py:356
  49.4 3.1 %collective-permute-done.1.refs_0_ = bf16[5504,128]{1,0:T(8,128)(2,1)} collective-permute-done((bf16[5504,128]{1,0:T(8,128)(2,1)S(1)}, bf16[5504,128]{1,0:T(8,128)(2,1)}, u32[]{:S(2)}, u32[]{:S(2)}) %collective-permute-start.1) | collective-permute-done | bytes 1409056 | tf_op jit(solution)/shard_map/ppermute | solution.py:662
  52.5 5.0 %collective-permute-done.2.refs_0_ = bf16[5504,128]{1,0:T(8,128)(2,1)} collective-permute-done((bf16[5504,128]{1,0:T(8,128)(2,1)S(1)}, bf16[5504,128]{1,0:T(8,128)(2,1)}, u32[]{:S(2)}, u32[]{:S(2)}) %collective-permute-start.2) | collective-permute-done | bytes 1409056 | tf_op jit(solution)/shard_map/ppermute | solution.py:663
  64.8 1.7 copy-done.4
  66.5 11.9 %ladder.7 = (s16[192,2176]{1,0:T(8,128)(2,1)S(1)}, s16[192,2176]{1,0:T(8,128)(2,1)S(1)}, s16[192,2176]{1,0:T(8,128)(2,1)S(1)}, s16[192,2176]{1,0:T(8,128)(2,1)}) custom-call(s32[87]{0:T(128)S(1)} %concatenate.6.tab, s32[64,128]{1,0:T(8,128)S(1)} %bitcast.22, ...), custom_call_target="tpu_custom_call", output_to_operand_aliasing={{0}: (7, {}), {1}: (8, {}), {2}: (9, {}), {3}: (10, {})} | custom-call | flops 4294967296 | bytes 16777216 | tf_op jit(solution)/shard_map/ladder/pallas_call | solution.py:356
  78.4 17.4 %collective-permute-done.6.refs_2_ = bf16[5504,128]{1,0:T(8,128)(2,1)} collective-permute-done((bf16[5504,128]{1,0:T(8,128)(2,1)}, bf16[5504,128]{1,0:T(8,128)(2,1)}, u32[]{:S(2)}, u32[]{:S(2)}) %collective-permute-start.6) | collective-permute-done | bytes 1409056 | tf_op jit(solution)/shard_map/ppermute | solution.py:671
  95.8 1.4 collective-permute-start.13
  97.9 1.5 broadcast_select_fusion
  100.7 3.9 %collective-permute-start.11 = (s16[192,2176]{1,0:T(8,128)(2,1)S(1)}, s16[192,2176]{1,0:T(8,128)(2,1)S(1)}, u32[]{:S(2)}, u32[]{:S(2)}) collective-permute-start(s16[192,2176]{1,0:T(8,128)(2,1)S(1)} %get-tuple-element.93), channel_id=1, source_target_pairs={{4,0},{6,2},{12,8},{14,10},{8,12},{22,18},{16,20},{18,22},{24,28},... | collective-permute-start | bytes 2506760 | tf_op jit(solution)/shard_map/ppermute | solution.py:626
  106.0 11.5 %ladder.8 = (s16[192,2176]{1,0:T(8,128)(2,1)S(1)}, s16[192,2176]{1,0:T(8,128)(2,1)S(1)}, s16[192,2176]{1,0:T(8,128)(2,1)S(1)}, s16[128,2176]{1,0:T(8,128)(2,1)S(1)}) custom-call(s32[87]{0:T(128)S(1)} %concatenate.6.tab, s32[64,128]{1,0:T(8,128)S(1)} %bitcast.23, bf16[5504,128]{1,0:T(8,128)(2,1)S(1)} %collective-permute-done.5.refs_0_, ...), custom_call_target="tpu_custom_call" | custom-call | flops 4294967296 | bytes 16777216 | tf_op jit(solution)/shard_map/ladder/pallas_call | solution.py:356
  117.5 2.3 %collective-permute-start.15 = (s16[192,2176]{1,0:T(8,128)(2,1)S(1)}, s16[192,2176]{1,0:T(8,128)(2,1)S(1)}, u32[]{:S(2)}, u32[]{:S(2)}) collective-permute-start(s16[192,2176]{1,0:T(8,128)(2,1)S(1)} %get-tuple-element.96), channel_id=1, source_target_pairs={{6,4},{12,14},{18,16},{24,26},{7,5},{13,15},{19,17},{25,27}} | collective-permute-start | bytes 2506760 | tf_op jit(solution)/shard_map/ppermute | solution.py:626
  120.6 2.0 %collective-permute-done.11.refs_2_ = s16[192,2176]{1,0:T(8,128)(2,1)S(1)} collective-permute-done((s16[192,2176]{1,0:T(8,128)(2,1)S(1)}, s16[192,2176]{1,0:T(8,128)(2,1)S(1)}, u32[]{:S(2)}, u32[]{:S(2)}) %collective-permute-start.11) | collective-permute-done | bytes 835616 | tf_op jit(solution)/shard_map/ppermute | solution.py:626
  123.3 17.3 %collective-permute-done.12.refs_3_ = s16[192,2176]{1,0:T(8,128)(2,1)S(1)} collective-permute-done((s16[192,2176]{1,0:T(8,128)(2,1)}, s16[192,2176]{1,0:T(8,128)(2,1)S(1)}, u32[]{:S(2)}, u32[]{:S(2)}) %collective-permute-start.12) | collective-permute-done | bytes 835616 | tf_op jit(solution)/shard_map/ppermute | solution.py:626
  141.5 2.8 %collective-permute-done.18.refs_1_ = bf16[5504,128]{1,0:T(8,128)(2,1)S(1)} collective-permute-done((bf16[5504,128]{1,0:T(8,128)(2,1)S(1)}, bf16[5504,128]{1,0:T(8,128)(2,1)S(1)}, u32[]{:S(2)}, u32[]{:S(2)}) %collective-permute-start.18) | collective-permute-done | bytes 1409056 | tf_op jit(solution)/shard_map/ppermute | solution.py:638
  144.3 10.3 %ladder.9 = (s16[192,2176]{1,0:T(8,128)(2,1)S(1)}, s16[192,2176]{1,0:T(8,128)(2,1)S(1)}, s16[192,2176]{1,0:T(8,128)(2,1)S(1)}, s16[128,2176]{1,0:T(8,128)(2,1)S(1)}) custom-call(s32[87]{0:T(128)S(1)} %concatenate.6.tab, s32[64,128]{1,0:T(8,128)S(1)} %bitcast.24, bf16[5504,128]{1,0:T(8,128)(2,1)S(1)} %collective-permute-done.9.refs_0_, ...), custom_call_target="tpu_custom_call" | custom-call | flops 4294967296 | bytes 16777216 | tf_op jit(solution)/shard_map/ladder/pallas_call | solution.py:356
  159.2 14.2 %collective-permute-done.21.refs_3_ = s16[128,2176]{1,0:T(8,128)(2,1)S(1)} collective-permute-done((s16[128,2176]{1,0:T(8,128)(2,1)S(1)}, s16[128,2176]{1,0:T(8,128)(2,1)S(1)}, u32[]{:S(2)}, u32[]{:S(2)}) %collective-permute-start.21) | collective-permute-done | bytes 557088 | tf_op jit(solution)/shard_map/ppermute | solution.py:626
  173.4 2.3 %collective-permute-done.20.refs_2_ = s16[192,2176]{1,0:T(8,128)(2,1)S(1)} collective-permute-done((s16[192,2176]{1,0:T(8,128)(2,1)S(1)}, s16[192,2176]{1,0:T(8,128)(2,1)S(1)}, u32[]{:S(2)}, u32[]{:S(2)}) %collective-permute-start.20) | collective-permute-done | bytes 835616 | tf_op jit(solution)/shard_map/ppermute | solution.py:626
  175.7 7.0 %finish.3 = f32[2,256,2048]{2,1,0:T(8,128)} custom-call(s32[87]{0:T(128)S(1)} %concatenate.6.tab, s32[2,256,128]{2,1,0:T(8,128)S(1)} %broadcast_in_dim.331.line, f32[2,256,128]{2,1,0:T(8,128)S(1)} %copy-done.2, f32[2,1,2048]{2,1,0:T(1,128)S(1)} %add.797.pair, s32[2,1,2048]{2,1,0:T(1,128)S(1)} %and_convert_fusion.pair_ok, ...), custom_call_target="tpu_custom_call", output_to_operand_aliasing={{}: (9, {})} | custom-call | tf_op jit(solution)/shard_map/finish/pallas_call | solution.py:484
  (162 shorter events, 31.9 us)
Async XLA Ops:
  6.5 29.4 %collective-permute-start.4 = (bf16[2,2048,2048]{2,1,0:T(8,128)(2,1)}, bf16[2,2048,2048]{2,1,0:T(8,128)(2,1)}, u32[]{:S(2)}, u32[]{:S(2)}) collective-permute-start(bf16[2,2048,2048]{2,1,0:T(8,128)(2,1)} %refs_3_.7), channel_id=1, source_target_pairs={{0,2},{2,0},{4,6},{6,4},{1,3},{3,1},{5,7},{7,5},{8,10},{10,8},{12,... | collective-permute-start | bytes 50331656 | tf_op jit(solution)/shard_map/ppermute | solution.py:638
  14.4 10.5 %copy-start.7 = (s32[8]{0:T(128)S(1)}, s32[8]{0:T(128)}, u32[]{:S(2)}) copy-start(s32[8]{0:T(128)} %param.13) | copy-start | bytes 100
  17.7 10.4 %copy-start.8 = (f32[256]{0:T(256)S(1)}, f32[256]{0:T(256)}, u32[]{:S(2)}) copy-start(f32[256]{0:T(256)} %param.10) | copy-start | bytes 3076
  17.8 18.1 %collective-permute-start.3 = (bf16[5504,128]{1,0:T(8,128)(2,1)S(1)}, bf16[5504,128]{1,0:T(8,128)(2,1)}, u32[]{:S(2)}, u32[]{:S(2)}) collective-permute-start(bf16[5504,128]{1,0:T(8,128)(2,1)S(1)} %slice.39.refs_0_), channel_id=1, source_target_pairs={{0,2},{2,0},{4,6},{6,4},{1,3},{3,1},{5,7},{7,5},{8,10},{10,8},{12,... | collective-permute-start | bytes 4227080 | tf_op jit(solution)/shard_map/ppermute | solution.py:638
  19.0 33.5 %collective-permute-start.1 = (bf16[5504,128]{1,0:T(8,128)(2,1)S(1)}, bf16[5504,128]{1,0:T(8,128)(2,1)}, u32[]{:S(2)}, u32[]{:S(2)}) collective-permute-start(bf16[5504,128]{1,0:T(8,128)(2,1)S(1)} %slice.39.refs_0_), channel_id=1, source_target_pairs={{0,8},{8,16},{16,24},{1,9},{9,17},{17,25},{2,10},{10,18},{18,26},{... | collective-permute-start | bytes 4227080 | tf_op jit(solution)/shard_map/ppermute | solution.py:662
  23.3 34.2 %collective-permute-start.2 = (bf16[5504,128]{1,0:T(8,128)(2,1)S(1)}, bf16[5504,128]{1,0:T(8,128)(2,1)}, u32[]{:S(2)}, u32[]{:S(2)}) collective-permute-start(bf16[5504,128]{1,0:T(8,128)(2,1)S(1)} %slice.39.refs_0_), channel_id=1, source_target_pairs={{8,0},{16,8},{24,16},{9,1},{17,9},{25,17},{10,2},{18,10},{26,18},{... | collective-permute-start | bytes 4227080 | tf_op jit(solution)/shard_map/ppermute | solution.py:663
  58.5 4.2 %collective-permute-start.8 = (bf16[5504,128]{1,0:T(8,128)(2,1)}, bf16[5504,128]{1,0:T(8,128)(2,1)}, u32[]{:S(2)}, u32[]{:S(2)}) collective-permute-start(bf16[5504,128]{1,0:T(8,128)(2,1)} %collective-permute-done.1.refs_0_), channel_id=1, source_target_pairs={{0,2},{2,0},{4,6},{6,4},{1,3},{3,1},{5,7},{7,5},{8,10},{10,8},{12,... | collective-permute-start | bytes 4227080 | tf_op jit(solution)/shard_map/ppermute | solution.py:638
  59.6 5.2 %collective-permute-start.7 = (bf16[5504,128]{1,0:T(8,128)(2,1)}, bf16[5504,128]{1,0:T(8,128)(2,1)}, u32[]{:S(2)}, u32[]{:S(2)}) collective-permute-start(bf16[5504,128]{1,0:T(8,128)(2,1)} %collective-permute-done.2.refs_0_), channel_id=1, source_target_pairs={{0,2},{2,0},{4,6},{6,4},{1,3},{3,1},{5,7},{7,5},{8,10},{10,8},{12,... | collective-permute-start | bytes 4227080 | tf_op jit(solution)/shard_map/ppermute | solution.py:638
  59.6 18.7 %collective-permute-start.5 = (bf16[5504,128]{1,0:T(8,128)(2,1)}, bf16[5504,128]{1,0:T(8,128)(2,1)S(1)}, u32[]{:S(2)}, u32[]{:S(2)}) collective-permute-start(bf16[5504,128]{1,0:T(8,128)(2,1)} %collective-permute-done.1.refs_0_), channel_id=1, source_target_pairs={{8,16},{16,24},{9,17},{17,25},{10,18},{18,26},{11,19},{19,27},{12,... | collective-permute-start | bytes 4227080 | tf_op jit(solution)/shard_map/ppermute | solution.py:670
  60.4 35.4 %collective-permute-start.6 = (bf16[5504,128]{1,0:T(8,128)(2,1)}, bf16[5504,128]{1,0:T(8,128)(2,1)}, u32[]{:S(2)}, u32[]{:S(2)}) collective-permute-start(bf16[5504,128]{1,0:T(8,128)(2,1)} %collective-permute-done.2.refs_0_), channel_id=1, source_target_pairs={{8,0},{16,8},{9,1},{17,9},{10,2},{18,10},{11,3},{19,11},{12,4},{20... | collective-permute-start | bytes 4227080 | tf_op jit(solution)/shard_map/ppermute | solution.py:671
  95.8 8.8 %collective-permute-start.13 = (bf16[5504,128]{1,0:T(8,128)(2,1)S(1)}, bf16[5504,128]{1,0:T(8,128)(2,1)S(1)}, u32[]{:S(2)}, u32[]{:S(2)}) collective-permute-start(bf16[5504,128]{1,0:T(8,128)(2,1)S(1)} %collective-permute-done.5.refs_0_), channel_id=1, source_target_pairs={{0,2},{2,0},{4,6},{6,4},{1,3},{3,1},{5,7},{7,5},{8,10},{10,8},{12,... | collective-permute-start | bytes 4227080 | tf_op jit(solution)/shard_map/ppermute | solution.py:638
  97.2 8.8 %collective-permute-start.14 = (bf16[5504,128]{1,0:T(8,128)(2,1)}, bf16[5504,128]{1,0:T(8,128)(2,1)S(1)}, u32[]{:S(2)}, u32[]{:S(2)}) collective-permute-start(bf16[5504,128]{1,0:T(8,128)(2,1)} %collective-permute-done.6.refs_2_), channel_id=1, source_target_pairs={{0,2},{2,0},{4,6},{6,4},{1,3},{3,1},{5,7},{7,5},{8,10},{10,8},{12,... | collective-permute-start | bytes 4227080 | tf_op jit(solution)/shard_map/ppermute | solution.py:638
  97.2 22.7 %collective-permute-start.10 = (s16[192,2176]{1,0:T(8,128)(2,1)S(1)}, s16[192,2176]{1,0:T(8,128)(2,1)S(1)}, u32[]{:S(2)}, u32[]{:S(2)}) collective-permute-start(s16[192,2176]{1,0:T(8,128)(2,1)S(1)} %get-tuple-element.92), channel_id=1, source_target_pairs={{2,0},{0,2},{10,8},{8,10},{14,12},{16,18},{22,20},{20,22},{30,28},... | collective-permute-start | bytes 2506760 | tf_op jit(solution)/shard_map/ppermute | solution.py:626
  99.4 41.2 %collective-permute-start.9 = (bf16[5504,128]{1,0:T(8,128)(2,1)S(1)}, bf16[5504,128]{1,0:T(8,128)(2,1)S(1)}, u32[]{:S(2)}, u32[]{:S(2)}) collective-permute-start(bf16[5504,128]{1,0:T(8,128)(2,1)S(1)} %broadcast_select_fusion), channel_id=1, source_target_pairs={{16,24},{8,0},{17,25},{9,1},{18,26},{10,2},{19,27},{11,3},{20,28},... | collective-permute-start | bytes 4227080 | tf_op jit(solution)/shard_map/ppermute | solution.py:675
  100.7 21.9 %collective-permute-start.11 = (s16[192,2176]{1,0:T(8,128)(2,1)S(1)}, s16[192,2176]{1,0:T(8,128)(2,1)S(1)}, u32[]{:S(2)}, u32[]{:S(2)}) collective-permute-start(s16[192,2176]{1,0:T(8,128)(2,1)S(1)} %get-tuple-element.93), channel_id=1, source_target_pairs={{4,0},{6,2},{12,8},{14,10},{8,12},{22,18},{16,20},{18,22},{24,28},... | collective-permute-start | bytes 2506760 | tf_op jit(solution)/shard_map/ppermute | solution.py:626
  104.6 35.9 %collective-permute-start.12 = (s16[192,2176]{1,0:T(8,128)(2,1)}, s16[192,2176]{1,0:T(8,128)(2,1)S(1)}, u32[]{:S(2)}, u32[]{:S(2)}) collective-permute-start(s16[192,2176]{1,0:T(8,128)(2,1)} %get-tuple-element.94), channel_id=1, source_target_pairs={{6,0},{4,2},{14,8},{12,10},{10,12},{20,18},{18,20},{16,22},{26,28}... | collective-permute-start | bytes 2506760 | tf_op jit(solution)/shard_map/ppermute | solution.py:626
  117.5 23.0 %collective-permute-start.15 = (s16[192,2176]{1,0:T(8,128)(2,1)S(1)}, s16[192,2176]{1,0:T(8,128)(2,1)S(1)}, u32[]{:S(2)}, u32[]{:S(2)}) collective-permute-start(s16[192,2176]{1,0:T(8,128)(2,1)S(1)} %get-tuple-element.96), channel_id=1, source_target_pairs={{6,4},{12,14},{18,16},{24,26},{7,5},{13,15},{19,17},{25,27}} | collective-permute-start | bytes 2506760 | tf_op jit(solution)/shard_map/ppermute | solution.py:626
  119.9 20.7 %collective-permute-start.16 = (s16[192,2176]{1,0:T(8,128)(2,1)S(1)}, s16[192,2176]{1,0:T(8,128)(2,1)S(1)}, u32[]{:S(2)}, u32[]{:S(2)}) collective-permute-start(s16[192,2176]{1,0:T(8,128)(2,1)S(1)} %get-tuple-element.97), channel_id=1, source_target_pairs={{0,4},{8,14},{20,16},{28,26},{1,5},{9,15},{21,17},{29,27}} | collective-permute-start | bytes 2506760 | tf_op jit(solution)/shard_map/ppermute | solution.py:626
  122.6 18.0 %collective-permute-start.17 = (s16[128,2176]{1,0:T(8,128)(2,1)S(1)}, s16[128,2176]{1,0:T(8,128)(2,1)S(1)}, u32[]{:S(2)}, u32[]{:S(2)}) collective-permute-start(s16[128,2176]{1,0:T(8,128)(2,1)S(1)} %get-tuple-element.98), channel_id=1, source_target_pairs={{2,4},{10,14},{22,16},{30,26},{3,5},{11,15},{23,17},{31,27}} | collective-permute-start | bytes 1671176 | tf_op jit(solution)/shard_map/ppermute | solution.py:626
  140.6 17.9 %copy-start.2 = (f32[2,256,128]{2,1,0:T(8,128)S(1)}, f32[2,256,128]{2,1,0:T(8,128)}, u32[]{:S(2)}) copy-start(f32[2,256,128]{2,1,0:T(8,128)} %broadcast_in_dim.334.hole) | copy-start | bytes 786436
  140.6 3.7 %collective-permute-start.18 = (bf16[5504,128]{1,0:T(8,128)(2,1)S(1)}, bf16[5504,128]{1,0:T(8,128)(2,1)S(1)}, u32[]{:S(2)}, u32[]{:S(2)}) collective-permute-start(bf16[5504,128]{1,0:T(8,128)(2,1)S(1)} %collective-permute-done.9.refs_0_), channel_id=1, source_target_pairs={{0,2},{2,0},{4,6},{6,4},{1,3},{3,1},{5,7},{7,5},{8,10},{10,8},{12,... | collective-permute-start | bytes 4227080 | tf_op jit(solution)/shard_map/ppermute | solution.py:638
  154.6 18.8 %collective-permute-start.19 = (s16[192,2176]{1,0:T(8,128)(2,1)S(1)}, s16[192,2176]{1,0:T(8,128)(2,1)S(1)}, u32[]{:S(2)}, u32[]{:S(2)}) collective-permute-start(s16[192,2176]{1,0:T(8,128)(2,1)S(1)} %get-tuple-element.105), channel_id=1, source_target_pairs={{4,6},{26,24},{5,7},{27,25}} | collective-permute-start | bytes 2506760 | tf_op jit(solution)/shard_map/ppermute | solution.py:626
  155.9 19.8 %collective-permute-start.20 = (s16[192,2176]{1,0:T(8,128)(2,1)S(1)}, s16[192,2176]{1,0:T(8,128)(2,1)S(1)}, u32[]{:S(2)}, u32[]{:S(2)}) collective-permute-start(s16[192,2176]{1,0:T(8,128)(2,1)S(1)} %get-tuple-element.106), channel_id=1, source_target_pairs={{0,6},{28,24},{1,7},{29,25}} | collective-permute-start | bytes 2506760 | tf_op jit(solution)/shard_map/ppermute | solution.py:626
  157.2 16.2 %collective-permute-start.21 = (s16[128,2176]{1,0:T(8,128)(2,1)S(1)}, s16[128,2176]{1,0:T(8,128)(2,1)S(1)}, u32[]{:S(2)}, u32[]{:S(2)}) collective-permute-start(s16[128,2176]{1,0:T(8,128)(2,1)S(1)} %get-tuple-element.107), channel_id=1, source_target_pairs={{2,6},{30,24},{3,7},{31,25}} | collective-permute-start | bytes 1671176 | tf_op jit(solution)/shard_map/ppermute | solution.py:626
  (7 other events, 25.2 us)

commit v4 on v3

--- a/solution.py
+++ b/solution.py
@@ -122,8 +122,9 @@
         self.at_more = self.at_self + self.syms * rows
         self.base_tiles = self.pay_tiles * 43 // 64
         enc_rows = self.enc_tiles * TILE_ROWS
-        self.enc_shapes = [(enc_rows, self.pairs + LANES)] * rows
-        self.far_shapes = self.enc_shapes[:-1] + [(self.share // 2, self.pairs + LANES)]
+        self.enc_shapes = [(enc_rows, self.pairs + LANES)] * (rows - 1) + [
+            (self.share // 2, self.pairs + LANES)
+        ]
 
 
 def row_counts(plan, tab, sym, share):
@@ -338,7 +339,7 @@
         lax.fori_loop(0, padded(reps) + padded(selfs), chunk, 0)
 
         flip = col ^ share
-        slot = flip if kind[0] < 2 else jnp.where(flip < 2, flip, 2 + sym)
+        slot = jnp.where(flip < 2, flip, 2 + sym)
         for number, out in enumerate(outs):
 
             @pl.when(slot == number)
@@ -355,10 +356,7 @@
     first_enc = 5 + len(pays)
     return pl.pallas_call(
         functools.partial(ladder_kernel, plan, kind, len(pays), pays[0].shape[0]),
-        out_shape=[
-            jax.ShapeDtypeStruct(shape, I16)
-            for shape in (plan.enc_shapes if kind[0] < 2 else plan.far_shapes)
-        ],
+        out_shape=[jax.ShapeDtypeStruct(shape, I16) for shape in plan.enc_shapes],
         in_specs=[smem, vmem] + [ANY] * (len(pays) + 3 + len(encs)),
         out_specs=[ANY] * n,
         scratch_shapes=[
@@ -386,11 +384,11 @@
     out, held, pick, whole, sems, out_sems = refs[-6:]
     row, col = tab[0], tab[1]
     core = lax.rem(col, 2)
-    which = jnp.maximum(jnp.abs(row - col) - 1, 0)
+    which = jnp.abs(row - col)
     steps = plan.pairs // wtile
 
-    def fetch(sources, by_sym):
-        parts = [(core, 0), (1 - core, 0)] + ([(0, 1), (1, 1)] if by_sym else [(core, 1), (1 - core, 1)])
+    def fetch(sources):
+        parts = [(core, 0), (1 - core, 0), (0, 1), (1, 1)]
         copies = [
             pltpu.make_async_copy(
                 ref, held.at[sym, side, pl.ds(0, ref.shape[0])], sems.at[number]
@@ -409,8 +407,8 @@
     for place, number in enumerate(numbers):
 
         @pl.when(which == number)
-        def _(sources=refs[n * place : n * (place + 1)], by_sym=number > 0):
-            fetch(sources, by_sym)
+        def _(sources=refs[n * place : n * (place + 1)]):
+            fetch(sources)
 
     def put(step):
         lanes = pl.ds(pl.multiple_of(step * wtile, wtile), wtile)
@@ -609,19 +607,16 @@
     )
 
 
-def to_roots(plan, encs, distances):
+def to_roots(plan, encs, distance):
     received = [encs[0]]
     roots = [
         (row, root)
         for row in range(plan.rows)
         for root in range(plan.rows)
-        if abs(row - root) in distances
+        if abs(row - root) == distance
     ]
     for slot in range(1, len(encs)):
-        if slot == 1 or 1 in distances:
-            source = lambda root: root ^ slot
-        else:
-            source = lambda root: (root ^ 2) // 2 * 2 + slot - 2
+        source = lambda root: root ^ 1 if slot == 1 else (root ^ 2) // 2 * 2 + slot - 2
         pairs = [(row * plan.rows + source(root), row * plan.rows + root) for row, root in roots]
         received.append(lax.ppermute(encs[slot], ("row", "col"), pairs))
     return received
@@ -671,23 +666,24 @@
                 lax.ppermute(left, "row", [(i + 1, i) for i in range(0, n - step)]),
             )
         else:
-            last = jnp.where(row >= n // 2, right, left)
+            sums, last = lax.optimization_barrier((sums, jnp.where(row >= n // 2, right, left)))
+            sources += sums
             last = lax.ppermute(last, "row", [(n - 2, n - 1), (1, 0)])
+        sums = to_roots(plan, encs, step - 2)
         if step == 2:
-            encs = work((1, "right"), [right], encs)
+            encs = work((1, "right"), [right], [])
             encs = work((1, "left"), [left], encs)
         else:
-            sources += to_roots(plan, encs, (0, 1) if step == 3 else (step - 2,))
             encs = work((step - 1, ""), [right, left], [])
         if step < n - 1:
             right, left = ahead
-    sources += to_roots(plan, encs, (n - 2,))
+    sources += sums + to_roots(plan, encs, n - 2)
     last, sources = lax.optimization_barrier((last, sources))
     encs = work((n - 1, ""), [last], [])
     near_tab, encs = lax.optimization_barrier((tab, encs))
-    far = to_roots(plan, encs, (n - 1,))
-    update = finish(plan, tuple(range(n - 2)), near_tab, *tables, sources, [])
-    return finish(plan, (n - 2,), tab, *tables, far, [update])
+    far = to_roots(plan, encs, n - 1)
+    update = finish(plan, tuple(range(n - 1)), near_tab, *tables, sources, [])
+    return finish(plan, (n - 1,), tab, *tables, far, [update])
 
 
 def solution(mesh):

time: 190 us -> 184 us (0.968)
  starting transfers between devices: 26.5 us -> 33.9 us
  waiting for transfers between devices: 65.5 us -> 58.9 us
  Pallas kernels: 58 us -> 54.6 us
  local copies, waits for them, and re-layouts: 11.6 us -> 8.86 us
    ppermute x9 -> x12, waiting for transfers between devices: 35.8 us -> 16.5 us  [to_roots(): received.append(lax.ppermute(encs[slot], ('row', 'col'), pairs))]
    ppermute x1, waiting for transfers between devices: 0.01 us -> 13.4 us  [on_device_line(): last = lax.ppermute(last, 'row', [(n - 2, n - 1), (1, 0)])]
    ppermute x7, starting transfers between devices: 4.07 us -> 8.09 us  [on_device_line(): sibling = lambda x: lax.ppermute(x, 'col', swap)]
    pallas_call x5, Pallas kernels: 47 us -> 43.5 us  [ladder_call(): pl.pallas_call(functools.partial(ladder_kernel, plan, kind, len(pays), pa...]
    ppermute x9 -> x12, starting transfers between devices: 13.5 us -> 16.9 us  [to_roots(): received.append(lax.ppermute(encs[slot], ('row', 'col'), pairs))]
    unnamed x24 -> x32, local copies, waits for them, and re-layouts: 6.58 us -> 4.55 us
  transfers between devices with their start and end apart: 21 -> 24, of which waited for: 10 -> 9; matrix products, arithmetic and copies ran while one was open for 9% -> 9% of each run, Pallas kernels for 21% -> 21%
where the time goes in v4:
time: 184 us; the launch traced here: 183 us
  waiting for transfers between devices  58.9 us (32%)
  Pallas kernels  54.6 us (30%)
  starting transfers between devices  33.9 us (18%)
  between operations  15 us (8%)
  other arithmetic  11.8 us (6%)
  local copies, waits for them, and re-layouts  8.86 us (5%)
    pallas_call x5, Pallas kernels, ladder_call(): pl.pallas_call(functools.partial(ladder_kernel, plan, kind, len(pays), pa...  43.5 us
    ppermute x12, starting transfers between devices, to_roots(): received.append(lax.ppermute(encs[slot], ('row', 'col'), pairs))  16.9 us
    ppermute x12, waiting for transfers between devices, to_roots(): received.append(lax.ppermute(encs[slot], ('row', 'col'), pairs))  16.5 us
    ppermute x1, waiting for transfers between devices, on_device_line(): lax.ppermute(left, 'row', [(i + 1, i) for i in range(0, n - step)])  16.2 us
    ppermute x1, waiting for transfers between devices, on_device_line(): last = lax.ppermute(last, 'row', [(n - 2, n - 1), (1, 0)])  13.4 us
    ppermute x7, starting transfers between devices, on_device_line(): sibling = lambda x: lax.ppermute(x, 'col', swap)  8.09 us
    pallas_call x2, Pallas kernels, finish(): pl.pallas_call(functools.partial(finish_kernel, plan, numbers, wtile), ou...  7.73 us
    reduce_sum x7, other arithmetic, table_value(): jnp.sum(jnp.where(matches, values_table, jnp.zeros((), values_table.dtype...  5.14 us
  transfers between devices with their start and end apart: 24, of which 9 were waited for; matrix products, arithmetic and copies ran while one was open for 9% of the time, Pallas kernels for 21%

profile of v4, /device:TPU:5, one launch (start us, length us, event | category | flops | bytes accessed | tf_op | source)
XLA Modules:
  0.0 183.0 jit_solution(855481494218377568)
XLA Ops:
  12.8 1.6 copy-done
  14.4 3.3 %pack.1 = bf16[8448,128]{1,0:T(8,128)(2,1)S(1)} custom-call(s32[36]{0:T(128)S(1)} %pad_add_fusion.tab, bf16[2,256,2048]{2,1,0:T(8,128)(2,1)S(1)} %copy-done, s32[2,256]{1,0:T(2,128)S(1)} %get-tuple-element.177.dest, s32[64,128]{1,0:T(8,128)S(1)} %bitcast.19), custom_call_target="tpu_custom_call" | custom-call | tf_op jit(solution)/shard_map/pack/pallas_call | solution.py:173
  19.1 4.3 %collective-permute-start.1 = (bf16[5504,128]{1,0:T(8,128)(2,1)S(1)}, bf16[5504,128]{1,0:T(8,128)(2,1)}, u32[]{:S(2)}, u32[]{:S(2)}) collective-permute-start(bf16[5504,128]{1,0:T(8,128)(2,1)S(1)} %slice.39.refs_0_), channel_id=1, source_target_pairs={{0,8},{8,16},{16,24},{1,9},{9,17},{17,25},{2,10},{10,18},{18,26},{... | collective-permute-start | bytes 4227080 | tf_op jit(solution)/shard_map/ppermute | solution.py:657
  28.2 2.4 %select_reduce_fusion = (f32[2,2048]{1,0:T(2,128)S(1)}, f32[2,2048]{1,0:T(2,128)S(1)}) fusion(s32[2,2048]{1,0:T(2,128)S(1)} %get-tuple-element.160, f32[256]{0:T(256)S(1)} %copy-done.10, s32[2048]{0:T(1024)S(1)} %get-tuple-element.223), kind=kLoop, calls=%fused_computation.1 | loop fusion | flops 6283264 | bytes 58368 | tf_op jit(solution)/shard_map/reduce_sum | solution.py:18
  32.1 3.1 %conditional.1 = (bf16[2,4,2688,128]{3,2,1,0:T(8,128)(2,1)}) conditional(s32[]{:T(128)} %convert_element_type.65, () %tuple.16, bf16[8448,128]{1,0:T(8,128)(2,1)} %copy-done.7), branch_computations={%region_21.22_spmd, %region_22.23_spmd} | conditional | flops 2752512 | bytes 33718360 | solution.py:650
  32.2 3.1 %broadcast.2164 = bf16[2,4,2688,128]{3,2,1,0:T(8,128)(2,1)} broadcast(bf16[]{:T(256)} %constant.424.clone), dimensions={} | broadcast | bytes 5505026 | tf_op jit(solution)/shard_map/broadcast.54
  36.0 10.7 %ladder.5 = (s16[192,2176]{1,0:T(8,128)(2,1)S(1)}, s16[192,2176]{1,0:T(8,128)(2,1)S(1)}, s16[192,2176]{1,0:T(8,128)(2,1)S(1)}, s16[128,2176]{1,0:T(8,128)(2,1)S(1)}) custom-call(s32[87]{0:T(128)S(1)} %concatenate.6.tab, s32[64,128]{1,0:T(8,128)S(1)} %bitcast.20, bf16[5504,128]{1,0:T(8,128)(2,1)S(1)} %slice.39.refs_0_, ...), custom_call_target="tpu_custom_call" | custom-call | flops 4294967296 | bytes 16777216 | tf_op jit(solution)/shard_map/ladder/pallas_call | solution.py:357
  48.4 4.2 %collective-permute-done.1.refs_0_ = bf16[5504,128]{1,0:T(8,128)(2,1)} collective-permute-done((bf16[5504,128]{1,0:T(8,128)(2,1)S(1)}, bf16[5504,128]{1,0:T(8,128)(2,1)}, u32[]{:S(2)}, u32[]{:S(2)}) %collective-permute-start.1) | collective-permute-done | bytes 1409056 | tf_op jit(solution)/shard_map/ppermute | solution.py:657
  52.6 5.0 %collective-permute-done.2.refs_0_ = bf16[5504,128]{1,0:T(8,128)(2,1)} collective-permute-done((bf16[5504,128]{1,0:T(8,128)(2,1)S(1)}, bf16[5504,128]{1,0:T(8,128)(2,1)}, u32[]{:S(2)}, u32[]{:S(2)}) %collective-permute-start.2) | collective-permute-done | bytes 1409056 | tf_op jit(solution)/shard_map/ppermute | solution.py:658
  59.8 1.3 collective-permute-start.6
  64.1 2.9 %collective-permute-start.11 = (s16[128,2176]{1,0:T(8,128)(2,1)S(1)}, s16[128,2176]{1,0:T(8,128)(2,1)S(1)}, u32[]{:S(2)}, u32[]{:S(2)}) collective-permute-start(s16[128,2176]{1,0:T(8,128)(2,1)S(1)} %copy-done.6), channel_id=1, source_target_pairs={{6,0},{14,10},{18,20},{26,30},{7,1},{15,11},{19,21},{27,31}} | collective-permute-start | bytes 1671176 | tf_op jit(solution)/shard_map/ppermute | solution.py:621
  67.1 11.9 %ladder.7 = (s16[192,2176]{1,0:T(8,128)(2,1)S(1)}, s16[192,2176]{1,0:T(8,128)(2,1)S(1)}, s16[192,2176]{1,0:T(8,128)(2,1)S(1)}, s16[128,2176]{1,0:T(8,128)(2,1)S(1)}) custom-call(s32[87]{0:T(128)S(1)} %concatenate.6.tab, s32[64,128]{1,0:T(8,128)S(1)} %bitcast.22, ...), custom_call_target="tpu_custom_call", output_to_operand_aliasing={{0}: (7, {}), {1}: (8, {}), {2}: (9, {}), {3}: (10, {})} | custom-call | flops 4294967296 | bytes 16777216 | tf_op jit(solution)/shard_map/ladder/pallas_call | solution.py:357
  79.0 16.2 %collective-permute-done.6.refs_2_ = bf16[5504,128]{1,0:T(8,128)(2,1)S(1)} collective-permute-done((bf16[5504,128]{1,0:T(8,128)(2,1)}, bf16[5504,128]{1,0:T(8,128)(2,1)S(1)}, u32[]{:S(2)}, u32[]{:S(2)}) %collective-permute-start.6) | collective-permute-done | bytes 1409056 | tf_op jit(solution)/shard_map/ppermute | solution.py:666
  96.7 1.3 collective-permute-start.12
  98.7 2.8 %collective-permute-start.15 = (s16[128,2176]{1,0:T(8,128)(2,1)S(1)}, s16[128,2176]{1,0:T(8,128)(2,1)S(1)}, u32[]{:S(2)}, u32[]{:S(2)}) collective-permute-start(s16[128,2176]{1,0:T(8,128)(2,1)S(1)} %get-tuple-element.108), channel_id=1, source_target_pairs={{6,2},{14,8},{10,12},{22,18},{18,22},{26,28},{7,3},{15,9},{11,13},... | collective-permute-start | bytes 1671176 | tf_op jit(solution)/shard_map/ppermute | solution.py:621
  102.3 10.4 %ladder.8 = (s16[192,2176]{1,0:T(8,128)(2,1)S(1)}, s16[192,2176]{1,0:T(8,128)(2,1)S(1)}, s16[192,2176]{1,0:T(8,128)(2,1)S(1)}, s16[128,2176]{1,0:T(8,128)(2,1)S(1)}) custom-call(s32[87]{0:T(128)S(1)} %concatenate.6.tab, s32[64,128]{1,0:T(8,128)S(1)} %bitcast.23, bf16[5504,128]{1,0:T(8,128)(2,1)S(1)} %collective-permute-done.5.refs_0_, ...), custom_call_target="tpu_custom_call" | custom-call | flops 4294967296 | bytes 16777216 | tf_op jit(solution)/shard_map/ladder/pallas_call | solution.py:357
  112.7 2.9 %collective-permute-start.18 = (s16[192,2176]{1,0:T(8,128)(2,1)S(1)}, s16[192,2176]{1,0:T(8,128)(2,1)S(1)}, u32[]{:S(2)}, u32[]{:S(2)}) collective-permute-start(s16[192,2176]{1,0:T(8,128)(2,1)S(1)} %get-tuple-element.110), channel_id=1, source_target_pairs={{6,4},{12,14},{18,16},{24,26},{7,5},{13,15},{19,17},{25,27}} | collective-permute-start | bytes 2506760 | tf_op jit(solution)/shard_map/ppermute | solution.py:621
  117.1 13.4 %collective-permute-done.12.refs_0_ = bf16[5504,128]{1,0:T(8,128)(2,1)S(1)} collective-permute-done((bf16[5504,128]{1,0:T(8,128)(2,1)S(1)}, bf16[5504,128]{1,0:T(8,128)(2,1)S(1)}, u32[]{:S(2)}, u32[]{:S(2)}) %collective-permute-start.12) | collective-permute-done | bytes 1409056 | tf_op jit(solution)/shard_map/ppermute | solution.py:671
  130.6 4.8 %collective-permute-start.21 = (bf16[5504,128]{1,0:T(8,128)(2,1)S(1)}, bf16[5504,128]{1,0:T(8,128)(2,1)S(1)}, u32[]{:S(2)}, u32[]{:S(2)}) collective-permute-start(bf16[5504,128]{1,0:T(8,128)(2,1)S(1)} %collective-permute-done.12.refs_0_), channel_id=1, source_target_pairs={{0,2},{2,0},{4,6},{6,4},{1,3},{3,1},{5,7},{7,5},{8,10},{10,8},{12,... | collective-permute-start | bytes 4227080 | tf_op jit(solution)/shard_map/ppermute | solution.py:633
  135.4 2.8 %collective-permute-done.21.refs_1_ = bf16[5504,128]{1,0:T(8,128)(2,1)S(1)} collective-permute-done((bf16[5504,128]{1,0:T(8,128)(2,1)S(1)}, bf16[5504,128]{1,0:T(8,128)(2,1)S(1)}, u32[]{:S(2)}, u32[]{:S(2)}) %collective-permute-start.21) | collective-permute-done | bytes 1409056 | tf_op jit(solution)/shard_map/ppermute | solution.py:633
  138.2 9.8 %ladder.9 = (s16[192,2176]{1,0:T(8,128)(2,1)S(1)}, s16[192,2176]{1,0:T(8,128)(2,1)S(1)}, s16[192,2176]{1,0:T(8,128)(2,1)S(1)}, s16[128,2176]{1,0:T(8,128)(2,1)S(1)}) custom-call(s32[87]{0:T(128)S(1)} %concatenate.6.tab, s32[64,128]{1,0:T(8,128)S(1)} %bitcast.24, bf16[5504,128]{1,0:T(8,128)(2,1)S(1)} %collective-permute-done.12.refs_0_, ...), custom_call_target="tpu_custom_call" | custom-call | flops 4294967296 | bytes 16777216 | tf_op jit(solution)/shard_map/ladder/pallas_call | solution.py:357
  152.6 14.2 %collective-permute-done.24.refs_3_ = s16[128,2176]{1,0:T(8,128)(2,1)S(1)} collective-permute-done((s16[128,2176]{1,0:T(8,128)(2,1)S(1)}, s16[128,2176]{1,0:T(8,128)(2,1)S(1)}, u32[]{:S(2)}, u32[]{:S(2)}) %collective-permute-start.24) | collective-permute-done | bytes 557088 | tf_op jit(solution)/shard_map/ppermute | solution.py:621
  166.8 2.3 %collective-permute-done.23.refs_2_ = s16[192,2176]{1,0:T(8,128)(2,1)S(1)} collective-permute-done((s16[192,2176]{1,0:T(8,128)(2,1)S(1)}, s16[192,2176]{1,0:T(8,128)(2,1)S(1)}, u32[]{:S(2)}, u32[]{:S(2)}) %collective-permute-start.23) | collective-permute-done | bytes 835616 | tf_op jit(solution)/shard_map/ppermute | solution.py:621
  169.1 7.0 %finish.3 = f32[2,256,2048]{2,1,0:T(8,128)} custom-call(s32[87]{0:T(128)S(1)} %concatenate.6.tab, s32[2,256,128]{2,1,0:T(8,128)S(1)} %broadcast_in_dim.331.line, f32[2,256,128]{2,1,0:T(8,128)S(1)} %broadcast_in_dim.334.hole, f32[2,1,2048]{2,1,0:T(1,128)S(1)} %add.797.pair, ...), custom_call_target="tpu_custom_call", output_to_operand_aliasing={{}: (9, {})} | custom-call | tf_op jit(solution)/shard_map/finish/pallas_call | solution.py:482
  (177 shorter events, 29.4 us)
Async XLA Ops:
  6.5 29.5 %collective-permute-start.4 = (bf16[2,2048,2048]{2,1,0:T(8,128)(2,1)}, bf16[2,2048,2048]{2,1,0:T(8,128)(2,1)}, u32[]{:S(2)}, u32[]{:S(2)}) collective-permute-start(bf16[2,2048,2048]{2,1,0:T(8,128)(2,1)} %refs_3_.7), channel_id=1, source_target_pairs={{0,2},{2,0},{4,6},{6,4},{1,3},{3,1},{5,7},{7,5},{8,10},{10,8},{12,... | collective-permute-start | bytes 50331656 | tf_op jit(solution)/shard_map/ppermute | solution.py:633
  17.9 18.1 %collective-permute-start.3 = (bf16[5504,128]{1,0:T(8,128)(2,1)S(1)}, bf16[5504,128]{1,0:T(8,128)(2,1)S(1)}, u32[]{:S(2)}, u32[]{:S(2)}) collective-permute-start(bf16[5504,128]{1,0:T(8,128)(2,1)S(1)} %slice.39.refs_0_), channel_id=1, source_target_pairs={{0,2},{2,0},{4,6},{6,4},{1,3},{3,1},{5,7},{7,5},{8,10},{10,8},{12,... | collective-permute-start | bytes 4227080 | tf_op jit(solution)/shard_map/ppermute | solution.py:633
  19.1 33.5 %collective-permute-start.1 = (bf16[5504,128]{1,0:T(8,128)(2,1)S(1)}, bf16[5504,128]{1,0:T(8,128)(2,1)}, u32[]{:S(2)}, u32[]{:S(2)}) collective-permute-start(bf16[5504,128]{1,0:T(8,128)(2,1)S(1)} %slice.39.refs_0_), channel_id=1, source_target_pairs={{0,8},{8,16},{16,24},{1,9},{9,17},{17,25},{2,10},{10,18},{18,26},{... | collective-permute-start | bytes 4227080 | tf_op jit(solution)/shard_map/ppermute | solution.py:657
  23.4 34.2 %collective-permute-start.2 = (bf16[5504,128]{1,0:T(8,128)(2,1)S(1)}, bf16[5504,128]{1,0:T(8,128)(2,1)}, u32[]{:S(2)}, u32[]{:S(2)}) collective-permute-start(bf16[5504,128]{1,0:T(8,128)(2,1)S(1)} %slice.39.refs_0_), channel_id=1, source_target_pairs={{8,0},{16,8},{24,16},{9,1},{17,9},{25,17},{10,2},{18,10},{26,18},{... | collective-permute-start | bytes 4227080 | tf_op jit(solution)/shard_map/ppermute | solution.py:658
  57.8 4.3 %collective-permute-start.8 = (bf16[5504,128]{1,0:T(8,128)(2,1)}, bf16[5504,128]{1,0:T(8,128)(2,1)}, u32[]{:S(2)}, u32[]{:S(2)}) collective-permute-start(bf16[5504,128]{1,0:T(8,128)(2,1)} %collective-permute-done.1.refs_0_), channel_id=1, source_target_pairs={{0,2},{2,0},{4,6},{6,4},{1,3},{3,1},{5,7},{7,5},{8,10},{10,8},{12,... | collective-permute-start | bytes 4227080 | tf_op jit(solution)/shard_map/ppermute | solution.py:633
  59.0 5.2 %collective-permute-start.7 = (bf16[5504,128]{1,0:T(8,128)(2,1)}, bf16[5504,128]{1,0:T(8,128)(2,1)}, u32[]{:S(2)}, u32[]{:S(2)}) collective-permute-start(bf16[5504,128]{1,0:T(8,128)(2,1)} %collective-permute-done.2.refs_0_), channel_id=1, source_target_pairs={{0,2},{2,0},{4,6},{6,4},{1,3},{3,1},{5,7},{7,5},{8,10},{10,8},{12,... | collective-permute-start | bytes 4227080 | tf_op jit(solution)/shard_map/ppermute | solution.py:633
  59.1 19.9 %collective-permute-start.5 = (bf16[5504,128]{1,0:T(8,128)(2,1)}, bf16[5504,128]{1,0:T(8,128)(2,1)S(1)}, u32[]{:S(2)}, u32[]{:S(2)}) collective-permute-start(bf16[5504,128]{1,0:T(8,128)(2,1)} %collective-permute-done.1.refs_0_), channel_id=1, source_target_pairs={{8,16},{16,24},{9,17},{17,25},{10,18},{18,26},{11,19},{19,27},{12,... | collective-permute-start | bytes 4227080 | tf_op jit(solution)/shard_map/ppermute | solution.py:665
  59.8 35.4 %collective-permute-start.6 = (bf16[5504,128]{1,0:T(8,128)(2,1)}, bf16[5504,128]{1,0:T(8,128)(2,1)S(1)}, u32[]{:S(2)}, u32[]{:S(2)}) collective-permute-start(bf16[5504,128]{1,0:T(8,128)(2,1)} %collective-permute-done.2.refs_0_), channel_id=1, source_target_pairs={{8,0},{16,8},{9,1},{17,9},{10,2},{18,10},{11,3},{19,11},{12,4},{20... | collective-permute-start | bytes 4227080 | tf_op jit(solution)/shard_map/ppermute | solution.py:666
  61.1 35.5 %collective-permute-start.10 = (s16[192,2176]{1,0:T(8,128)(2,1)}, s16[192,2176]{1,0:T(8,128)(2,1)S(1)}, u32[]{:S(2)}, u32[]{:S(2)}) collective-permute-start(s16[192,2176]{1,0:T(8,128)(2,1)} %copy-done.4), channel_id=1, source_target_pairs={{4,0},{12,10},{16,20},{24,30},{5,1},{13,11},{17,21},{25,31}} | collective-permute-start | bytes 2506760 | tf_op jit(solution)/shard_map/ppermute | solution.py:621
  62.1 34.6 %collective-permute-start.9 = (s16[192,2176]{1,0:T(8,128)(2,1)}, s16[192,2176]{1,0:T(8,128)(2,1)S(1)}, u32[]{:S(2)}, u32[]{:S(2)}) collective-permute-start(s16[192,2176]{1,0:T(8,128)(2,1)} %copy-done.3), channel_id=1, source_target_pairs={{2,0},{8,10},{22,20},{28,30},{3,1},{9,11},{23,21},{29,31}} | collective-permute-start | bytes 2506760 | tf_op jit(solution)/shard_map/ppermute | solution.py:621
  64.1 32.5 %collective-permute-start.11 = (s16[128,2176]{1,0:T(8,128)(2,1)S(1)}, s16[128,2176]{1,0:T(8,128)(2,1)S(1)}, u32[]{:S(2)}, u32[]{:S(2)}) collective-permute-start(s16[128,2176]{1,0:T(8,128)(2,1)S(1)} %copy-done.6), channel_id=1, source_target_pairs={{6,0},{14,10},{18,20},{26,30},{7,1},{15,11},{19,21},{27,31}} | collective-permute-start | bytes 1671176 | tf_op jit(solution)/shard_map/ppermute | solution.py:621
  95.2 6.3 %collective-permute-start.16 = (bf16[5504,128]{1,0:T(8,128)(2,1)S(1)}, bf16[5504,128]{1,0:T(8,128)(2,1)S(1)}, u32[]{:S(2)}, u32[]{:S(2)}) collective-permute-start(bf16[5504,128]{1,0:T(8,128)(2,1)S(1)} %collective-permute-done.5.refs_0_), channel_id=1, source_target_pairs={{0,2},{2,0},{4,6},{6,4},{1,3},{3,1},{5,7},{7,5},{8,10},{10,8},{12,... | collective-permute-start | bytes 4227080 | tf_op jit(solution)/shard_map/ppermute | solution.py:633
  96.5 5.7 %collective-permute-start.17 = (bf16[5504,128]{1,0:T(8,128)(2,1)S(1)}, bf16[5504,128]{1,0:T(8,128)(2,1)S(1)}, u32[]{:S(2)}, u32[]{:S(2)}) collective-permute-start(bf16[5504,128]{1,0:T(8,128)(2,1)S(1)} %collective-permute-done.6.refs_2_), channel_id=1, source_target_pairs={{0,2},{2,0},{4,6},{6,4},{1,3},{3,1},{5,7},{7,5},{8,10},{10,8},{12,... | collective-permute-start | bytes 4227080 | tf_op jit(solution)/shard_map/ppermute | solution.py:633
  96.7 33.8 %collective-permute-start.12 = (bf16[5504,128]{1,0:T(8,128)(2,1)S(1)}, bf16[5504,128]{1,0:T(8,128)(2,1)S(1)}, u32[]{:S(2)}, u32[]{:S(2)}) collective-permute-start(bf16[5504,128]{1,0:T(8,128)(2,1)S(1)} %broadcast_select_fusion), channel_id=1, source_target_pairs={{16,24},{8,0},{17,25},{9,1},{18,26},{10,2},{19,27},{11,3},{20,28},... | collective-permute-start | bytes 4227080 | tf_op jit(solution)/shard_map/ppermute | solution.py:671
  98.0 18.4 %collective-permute-start.13 = (s16[192,2176]{1,0:T(8,128)(2,1)S(1)}, s16[192,2176]{1,0:T(8,128)(2,1)S(1)}, u32[]{:S(2)}, u32[]{:S(2)}) collective-permute-start(s16[192,2176]{1,0:T(8,128)(2,1)S(1)} %get-tuple-element.106), channel_id=1, source_target_pairs={{0,2},{10,8},{14,12},{16,18},{20,22},{30,28},{1,3},{11,9},{15,13},... | collective-permute-start | bytes 2506760 | tf_op jit(solution)/shard_map/ppermute | solution.py:621
  98.7 16.9 %collective-permute-start.15 = (s16[128,2176]{1,0:T(8,128)(2,1)S(1)}, s16[128,2176]{1,0:T(8,128)(2,1)S(1)}, u32[]{:S(2)}, u32[]{:S(2)}) collective-permute-start(s16[128,2176]{1,0:T(8,128)(2,1)S(1)} %get-tuple-element.108), channel_id=1, source_target_pairs={{6,2},{14,8},{10,12},{22,18},{18,22},{26,28},{7,3},{15,9},{11,13},... | collective-permute-start | bytes 1671176 | tf_op jit(solution)/shard_map/ppermute | solution.py:621
  101.5 15.6 %collective-permute-start.14 = (s16[192,2176]{1,0:T(8,128)(2,1)S(1)}, s16[192,2176]{1,0:T(8,128)(2,1)S(1)}, u32[]{:S(2)}, u32[]{:S(2)}) collective-permute-start(s16[192,2176]{1,0:T(8,128)(2,1)S(1)} %get-tuple-element.107), channel_id=1, source_target_pairs={{4,2},{12,8},{8,12},{20,18},{16,22},{24,28},{5,3},{13,9},{9,13},{2... | collective-permute-start | bytes 2506760 | tf_op jit(solution)/shard_map/ppermute | solution.py:621
  112.7 17.8 %collective-permute-start.18 = (s16[192,2176]{1,0:T(8,128)(2,1)S(1)}, s16[192,2176]{1,0:T(8,128)(2,1)S(1)}, u32[]{:S(2)}, u32[]{:S(2)}) collective-permute-start(s16[192,2176]{1,0:T(8,128)(2,1)S(1)} %get-tuple-element.110), channel_id=1, source_target_pairs={{6,4},{12,14},{18,16},{24,26},{7,5},{13,15},{19,17},{25,27}} | collective-permute-start | bytes 2506760 | tf_op jit(solution)/shard_map/ppermute | solution.py:621
  115.7 14.9 %collective-permute-start.19 = (s16[192,2176]{1,0:T(8,128)(2,1)S(1)}, s16[192,2176]{1,0:T(8,128)(2,1)S(1)}, u32[]{:S(2)}, u32[]{:S(2)}) collective-permute-start(s16[192,2176]{1,0:T(8,128)(2,1)S(1)} %get-tuple-element.111), channel_id=1, source_target_pairs={{0,4},{8,14},{20,16},{28,26},{1,5},{9,15},{21,17},{29,27}} | collective-permute-start | bytes 2506760 | tf_op jit(solution)/shard_map/ppermute | solution.py:621
  116.4 14.1 %collective-permute-start.20 = (s16[128,2176]{1,0:T(8,128)(2,1)S(1)}, s16[128,2176]{1,0:T(8,128)(2,1)S(1)}, u32[]{:S(2)}, u32[]{:S(2)}) collective-permute-start(s16[128,2176]{1,0:T(8,128)(2,1)S(1)} %get-tuple-element.112), channel_id=1, source_target_pairs={{2,4},{10,14},{22,16},{30,26},{3,5},{11,15},{23,17},{31,27}} | collective-permute-start | bytes 1671176 | tf_op jit(solution)/shard_map/ppermute | solution.py:621
  130.6 7.6 %collective-permute-start.21 = (bf16[5504,128]{1,0:T(8,128)(2,1)S(1)}, bf16[5504,128]{1,0:T(8,128)(2,1)S(1)}, u32[]{:S(2)}, u32[]{:S(2)}) collective-permute-start(bf16[5504,128]{1,0:T(8,128)(2,1)S(1)} %collective-permute-done.12.refs_0_), channel_id=1, source_target_pairs={{0,2},{2,0},{4,6},{6,4},{1,3},{3,1},{5,7},{7,5},{8,10},{10,8},{12,... | collective-permute-start | bytes 4227080 | tf_op jit(solution)/shard_map/ppermute | solution.py:633
  148.0 18.8 %collective-permute-start.22 = (s16[192,2176]{1,0:T(8,128)(2,1)S(1)}, s16[192,2176]{1,0:T(8,128)(2,1)S(1)}, u32[]{:S(2)}, u32[]{:S(2)}) collective-permute-start(s16[192,2176]{1,0:T(8,128)(2,1)S(1)} %get-tuple-element.119), channel_id=1, source_target_pairs={{4,6},{26,24},{5,7},{27,25}} | collective-permute-start | bytes 2506760 | tf_op jit(solution)/shard_map/ppermute | solution.py:621
  149.3 19.8 %collective-permute-start.23 = (s16[192,2176]{1,0:T(8,128)(2,1)S(1)}, s16[192,2176]{1,0:T(8,128)(2,1)S(1)}, u32[]{:S(2)}, u32[]{:S(2)}) collective-permute-start(s16[192,2176]{1,0:T(8,128)(2,1)S(1)} %get-tuple-element.120), channel_id=1, source_target_pairs={{0,6},{28,24},{1,7},{29,25}} | collective-permute-start | bytes 2506760 | tf_op jit(solution)/shard_map/ppermute | solution.py:621
  150.6 16.2 %collective-permute-start.24 = (s16[128,2176]{1,0:T(8,128)(2,1)S(1)}, s16[128,2176]{1,0:T(8,128)(2,1)S(1)}, u32[]{:S(2)}, u32[]{:S(2)}) collective-permute-start(s16[128,2176]{1,0:T(8,128)(2,1)S(1)} %get-tuple-element.121), channel_id=1, source_target_pairs={{2,6},{30,24},{3,7},{31,25}} | collective-permute-start | bytes 1671176 | tf_op jit(solution)/shard_map/ppermute | solution.py:621
  (14 other events, 160.2 us)

commit v5 on v4

--- a/solution.py
+++ b/solution.py
@@ -245,9 +245,11 @@
                 for copy in pay_copies(pays[2:]):
                     copy.start()
 
+        for copy in int_copies(0):
+            copy.start()
         for copy in pay_copies(pays[:2]):
             copy.wait()
-        for pt in range(steps):
+        for pt in range(1, steps):
             for copy in int_copies(pt):
                 copy.start()
 
@@ -476,7 +478,7 @@
 
 
 def finish(plan, numbers, tab, line, hole, pair, pair_ok, sources, before):
-    wtile = min(256, plan.pairs)
+    wtile = min(512, plan.pairs)
     smem, vmem = (pl.BlockSpec(memory_space=space) for space in (pltpu.SMEM, pltpu.VMEM))
     out = jax.ShapeDtypeStruct((plan.syms, plan.share, plan.pairs), F32)
     return pl.pallas_call(

time: 184 us -> 184 us (level)
    pallas_call x5, Pallas kernels: 43.5 us -> 45.5 us  [ladder_call(): pl.pallas_call(functools.partial(ladder_kernel, plan, kind, len(pays), pa...]
where the time goes in v5:
time: 184 us
  waiting for transfers between devices  57.5 us (31%)
  Pallas kernels  56.3 us (31%)
  starting transfers between devices  34.3 us (19%)
  between operations  15 us (8%)
  other arithmetic  11.8 us (6%)
  local copies, waits for them, and re-layouts  8.86 us (5%)
    pallas_call x5, Pallas kernels, ladder_call(): pl.pallas_call(functools.partial(ladder_kernel, plan, kind, len(pays), pa...  45.5 us
    ppermute x12, starting transfers between devices, to_roots(): received.append(lax.ppermute(encs[slot], ('row', 'col'), pairs))  16.8 us
    ppermute x12, waiting for transfers between devices, to_roots(): received.append(lax.ppermute(encs[slot], ('row', 'col'), pairs))  16.6 us
    ppermute x1, waiting for transfers between devices, on_device_line(): lax.ppermute(left, 'row', [(i + 1, i) for i in range(0, n - step)])  15.4 us
    ppermute x1, waiting for transfers between devices, on_device_line(): last = lax.ppermute(last, 'row', [(n - 2, n - 1), (1, 0)])  13 us
    ppermute x7, starting transfers between devices, on_device_line(): sibling = lambda x: lax.ppermute(x, 'col', swap)  8.53 us
    pallas_call x2, Pallas kernels, finish(): pl.pallas_call(functools.partial(finish_kernel, plan, numbers, wtile), ou...  7.45 us
    reduce_sum x7, other arithmetic, table_value(): jnp.sum(jnp.where(matches, values_table, jnp.zeros((), values_table.dtype...  5.14 us
  transfers between devices with their start and end apart: 24, of which 9 were waited for; matrix products, arithmetic and copies ran while one was open for 9% of the time, Pallas kernels for 21%

profile of v5, /device:TPU:5, one launch (start us, length us, event | category | flops | bytes accessed | tf_op | source)
XLA Modules:
  0.0 183.7 jit_solution(11262670659007477340)
XLA Ops:
  12.8 1.6 copy-done
  14.4 3.3 %pack.1 = bf16[8448,128]{1,0:T(8,128)(2,1)S(1)} custom-call(s32[36]{0:T(128)S(1)} %pad_add_fusion.tab, bf16[2,256,2048]{2,1,0:T(8,128)(2,1)S(1)} %copy-done, s32[2,256]{1,0:T(2,128)S(1)} %get-tuple-element.177.dest, s32[64,128]{1,0:T(8,128)S(1)} %bitcast.19), custom_call_target="tpu_custom_call" | custom-call | tf_op jit(solution)/shard_map/pack/pallas_call | solution.py:173
  19.1 4.3 %collective-permute-start.1 = (bf16[5504,128]{1,0:T(8,128)(2,1)S(1)}, bf16[5504,128]{1,0:T(8,128)(2,1)}, u32[]{:S(2)}, u32[]{:S(2)}) collective-permute-start(bf16[5504,128]{1,0:T(8,128)(2,1)S(1)} %slice.39.refs_0_), channel_id=1, source_target_pairs={{0,8},{8,16},{16,24},{1,9},{9,17},{17,25},{2,10},{10,18},{18,26},{... | collective-permute-start | bytes 4227080 | tf_op jit(solution)/shard_map/ppermute | solution.py:659
  28.2 2.4 %select_reduce_fusion = (f32[2,2048]{1,0:T(2,128)S(1)}, f32[2,2048]{1,0:T(2,128)S(1)}) fusion(s32[2,2048]{1,0:T(2,128)S(1)} %get-tuple-element.160, f32[256]{0:T(256)S(1)} %copy-done.10, s32[2048]{0:T(1024)S(1)} %get-tuple-element.223), kind=kLoop, calls=%fused_computation.1 | loop fusion | flops 6283264 | bytes 58368 | tf_op jit(solution)/shard_map/reduce_sum | solution.py:18
  32.1 3.1 %conditional.1 = (bf16[2,4,2688,128]{3,2,1,0:T(8,128)(2,1)}) conditional(s32[]{:T(128)} %convert_element_type.65, () %tuple.16, bf16[8448,128]{1,0:T(8,128)(2,1)} %copy-done.7), branch_computations={%region_21.22_spmd, %region_22.23_spmd} | conditional | flops 2752512 | bytes 33718360 | solution.py:652
  32.2 3.1 %broadcast.2164 = bf16[2,4,2688,128]{3,2,1,0:T(8,128)(2,1)} broadcast(bf16[]{:T(256)} %constant.424.clone), dimensions={} | broadcast | bytes 5505026 | tf_op jit(solution)/shard_map/broadcast.54
  36.0 10.9 %ladder.5 = (s16[192,2176]{1,0:T(8,128)(2,1)S(1)}, s16[192,2176]{1,0:T(8,128)(2,1)S(1)}, s16[192,2176]{1,0:T(8,128)(2,1)S(1)}, s16[128,2176]{1,0:T(8,128)(2,1)S(1)}) custom-call(s32[87]{0:T(128)S(1)} %concatenate.6.tab, s32[64,128]{1,0:T(8,128)S(1)} %bitcast.20, bf16[5504,128]{1,0:T(8,128)(2,1)S(1)} %slice.39.refs_0_, ...), custom_call_target="tpu_custom_call" | custom-call | flops 4294967296 | bytes 16777216 | tf_op jit(solution)/shard_map/ladder/pallas_call | solution.py:359
  48.6 3.9 %collective-permute-done.1.refs_0_ = bf16[5504,128]{1,0:T(8,128)(2,1)} collective-permute-done((bf16[5504,128]{1,0:T(8,128)(2,1)S(1)}, bf16[5504,128]{1,0:T(8,128)(2,1)}, u32[]{:S(2)}, u32[]{:S(2)}) %collective-permute-start.1) | collective-permute-done | bytes 1409056 | tf_op jit(solution)/shard_map/ppermute | solution.py:659
  52.6 5.0 %collective-permute-done.2.refs_0_ = bf16[5504,128]{1,0:T(8,128)(2,1)} collective-permute-done((bf16[5504,128]{1,0:T(8,128)(2,1)S(1)}, bf16[5504,128]{1,0:T(8,128)(2,1)}, u32[]{:S(2)}, u32[]{:S(2)}) %collective-permute-start.2) | collective-permute-done | bytes 1409056 | tf_op jit(solution)/shard_map/ppermute | solution.py:660
  59.8 1.3 collective-permute-start.6
  64.1 2.9 %collective-permute-start.11 = (s16[128,2176]{1,0:T(8,128)(2,1)S(1)}, s16[128,2176]{1,0:T(8,128)(2,1)S(1)}, u32[]{:S(2)}, u32[]{:S(2)}) collective-permute-start(s16[128,2176]{1,0:T(8,128)(2,1)S(1)} %copy-done.6), channel_id=1, source_target_pairs={{6,0},{14,10},{18,20},{26,30},{7,1},{15,11},{19,21},{27,31}} | collective-permute-start | bytes 1671176 | tf_op jit(solution)/shard_map/ppermute | solution.py:623
  67.1 12.7 %ladder.7 = (s16[192,2176]{1,0:T(8,128)(2,1)S(1)}, s16[192,2176]{1,0:T(8,128)(2,1)S(1)}, s16[192,2176]{1,0:T(8,128)(2,1)S(1)}, s16[128,2176]{1,0:T(8,128)(2,1)S(1)}) custom-call(s32[87]{0:T(128)S(1)} %concatenate.6.tab, s32[64,128]{1,0:T(8,128)S(1)} %bitcast.22, ...), custom_call_target="tpu_custom_call", output_to_operand_aliasing={{0}: (7, {}), {1}: (8, {}), {2}: (9, {}), {3}: (10, {})} | custom-call | flops 4294967296 | bytes 16777216 | tf_op jit(solution)/shard_map/ladder/pallas_call | solution.py:359
  79.8 15.4 %collective-permute-done.6.refs_2_ = bf16[5504,128]{1,0:T(8,128)(2,1)S(1)} collective-permute-done((bf16[5504,128]{1,0:T(8,128)(2,1)}, bf16[5504,128]{1,0:T(8,128)(2,1)S(1)}, u32[]{:S(2)}, u32[]{:S(2)}) %collective-permute-start.6) | collective-permute-done | bytes 1409056 | tf_op jit(solution)/shard_map/ppermute | solution.py:668
  96.7 1.3 collective-permute-start.12
  98.7 2.7 %collective-permute-start.15 = (s16[128,2176]{1,0:T(8,128)(2,1)S(1)}, s16[128,2176]{1,0:T(8,128)(2,1)S(1)}, u32[]{:S(2)}, u32[]{:S(2)}) collective-permute-start(s16[128,2176]{1,0:T(8,128)(2,1)S(1)} %get-tuple-element.108), channel_id=1, source_target_pairs={{6,2},{14,8},{10,12},{22,18},{18,22},{26,28},{7,3},{15,9},{11,13},... | collective-permute-start | bytes 1671176 | tf_op jit(solution)/shard_map/ppermute | solution.py:623
  102.2 10.9 %ladder.8 = (s16[192,2176]{1,0:T(8,128)(2,1)S(1)}, s16[192,2176]{1,0:T(8,128)(2,1)S(1)}, s16[192,2176]{1,0:T(8,128)(2,1)S(1)}, s16[128,2176]{1,0:T(8,128)(2,1)S(1)}) custom-call(s32[87]{0:T(128)S(1)} %concatenate.6.tab, s32[64,128]{1,0:T(8,128)S(1)} %bitcast.23, bf16[5504,128]{1,0:T(8,128)(2,1)S(1)} %collective-permute-done.5.refs_0_, ...), custom_call_target="tpu_custom_call" | custom-call | flops 4294967296 | bytes 16777216 | tf_op jit(solution)/shard_map/ladder/pallas_call | solution.py:359
  113.1 2.9 %collective-permute-start.18 = (s16[192,2176]{1,0:T(8,128)(2,1)S(1)}, s16[192,2176]{1,0:T(8,128)(2,1)S(1)}, u32[]{:S(2)}, u32[]{:S(2)}) collective-permute-start(s16[192,2176]{1,0:T(8,128)(2,1)S(1)} %get-tuple-element.110), channel_id=1, source_target_pairs={{6,4},{12,14},{18,16},{24,26},{7,5},{13,15},{19,17},{25,27}} | collective-permute-start | bytes 2506760 | tf_op jit(solution)/shard_map/ppermute | solution.py:623
  117.6 13.0 %collective-permute-done.12.refs_0_ = bf16[5504,128]{1,0:T(8,128)(2,1)S(1)} collective-permute-done((bf16[5504,128]{1,0:T(8,128)(2,1)S(1)}, bf16[5504,128]{1,0:T(8,128)(2,1)S(1)}, u32[]{:S(2)}, u32[]{:S(2)}) %collective-permute-start.12) | collective-permute-done | bytes 1409056 | tf_op jit(solution)/shard_map/ppermute | solution.py:673
  130.6 5.3 %collective-permute-start.21 = (bf16[5504,128]{1,0:T(8,128)(2,1)S(1)}, bf16[5504,128]{1,0:T(8,128)(2,1)S(1)}, u32[]{:S(2)}, u32[]{:S(2)}) collective-permute-start(bf16[5504,128]{1,0:T(8,128)(2,1)S(1)} %collective-permute-done.12.refs_0_), channel_id=1, source_target_pairs={{0,2},{2,0},{4,6},{6,4},{1,3},{3,1},{5,7},{7,5},{8,10},{10,8},{12,... | collective-permute-start | bytes 4227080 | tf_op jit(solution)/shard_map/ppermute | solution.py:635
  135.8 2.8 %collective-permute-done.21.refs_1_ = bf16[5504,128]{1,0:T(8,128)(2,1)S(1)} collective-permute-done((bf16[5504,128]{1,0:T(8,128)(2,1)S(1)}, bf16[5504,128]{1,0:T(8,128)(2,1)S(1)}, u32[]{:S(2)}, u32[]{:S(2)}) %collective-permute-start.21) | collective-permute-done | bytes 1409056 | tf_op jit(solution)/shard_map/ppermute | solution.py:635
  138.6 10.3 %ladder.9 = (s16[192,2176]{1,0:T(8,128)(2,1)S(1)}, s16[192,2176]{1,0:T(8,128)(2,1)S(1)}, s16[192,2176]{1,0:T(8,128)(2,1)S(1)}, s16[128,2176]{1,0:T(8,128)(2,1)S(1)}) custom-call(s32[87]{0:T(128)S(1)} %concatenate.6.tab, s32[64,128]{1,0:T(8,128)S(1)} %bitcast.24, bf16[5504,128]{1,0:T(8,128)(2,1)S(1)} %collective-permute-done.12.refs_0_, ...), custom_call_target="tpu_custom_call" | custom-call | flops 4294967296 | bytes 16777216 | tf_op jit(solution)/shard_map/ladder/pallas_call | solution.py:359
  153.5 14.2 %collective-permute-done.24.refs_3_ = s16[128,2176]{1,0:T(8,128)(2,1)S(1)} collective-permute-done((s16[128,2176]{1,0:T(8,128)(2,1)S(1)}, s16[128,2176]{1,0:T(8,128)(2,1)S(1)}, u32[]{:S(2)}, u32[]{:S(2)}) %collective-permute-start.24) | collective-permute-done | bytes 557088 | tf_op jit(solution)/shard_map/ppermute | solution.py:623
  167.8 2.3 %collective-permute-done.23.refs_2_ = s16[192,2176]{1,0:T(8,128)(2,1)S(1)} collective-permute-done((s16[192,2176]{1,0:T(8,128)(2,1)S(1)}, s16[192,2176]{1,0:T(8,128)(2,1)S(1)}, u32[]{:S(2)}, u32[]{:S(2)}) %collective-permute-start.23) | collective-permute-done | bytes 835616 | tf_op jit(solution)/shard_map/ppermute | solution.py:623
  170.1 6.8 %finish.3 = f32[2,256,2048]{2,1,0:T(8,128)} custom-call(s32[87]{0:T(128)S(1)} %concatenate.6.tab, s32[2,256,128]{2,1,0:T(8,128)S(1)} %broadcast_in_dim.331.line, f32[2,256,128]{2,1,0:T(8,128)S(1)} %broadcast_in_dim.334.hole, f32[2,1,2048]{2,1,0:T(1,128)S(1)} %add.797.pair, ...), custom_call_target="tpu_custom_call", output_to_operand_aliasing={{}: (9, {})} | custom-call | tf_op jit(solution)/shard_map/finish/pallas_call | solution.py:484
  (177 shorter events, 29.3 us)
Async XLA Ops:
  6.5 29.5 %collective-permute-start.4 = (bf16[2,2048,2048]{2,1,0:T(8,128)(2,1)}, bf16[2,2048,2048]{2,1,0:T(8,128)(2,1)}, u32[]{:S(2)}, u32[]{:S(2)}) collective-permute-start(bf16[2,2048,2048]{2,1,0:T(8,128)(2,1)} %refs_3_.7), channel_id=1, source_target_pairs={{0,2},{2,0},{4,6},{6,4},{1,3},{3,1},{5,7},{7,5},{8,10},{10,8},{12,... | collective-permute-start | bytes 50331656 | tf_op jit(solution)/shard_map/ppermute | solution.py:635
  17.9 18.1 %collective-permute-start.3 = (bf16[5504,128]{1,0:T(8,128)(2,1)S(1)}, bf16[5504,128]{1,0:T(8,128)(2,1)S(1)}, u32[]{:S(2)}, u32[]{:S(2)}) collective-permute-start(bf16[5504,128]{1,0:T(8,128)(2,1)S(1)} %slice.39.refs_0_), channel_id=1, source_target_pairs={{0,2},{2,0},{4,6},{6,4},{1,3},{3,1},{5,7},{7,5},{8,10},{10,8},{12,... | collective-permute-start | bytes 4227080 | tf_op jit(solution)/shard_map/ppermute | solution.py:635
  19.1 33.5 %collective-permute-start.1 = (bf16[5504,128]{1,0:T(8,128)(2,1)S(1)}, bf16[5504,128]{1,0:T(8,128)(2,1)}, u32[]{:S(2)}, u32[]{:S(2)}) collective-permute-start(bf16[5504,128]{1,0:T(8,128)(2,1)S(1)} %slice.39.refs_0_), channel_id=1, source_target_pairs={{0,8},{8,16},{16,24},{1,9},{9,17},{17,25},{2,10},{10,18},{18,26},{... | collective-permute-start | bytes 4227080 | tf_op jit(solution)/shard_map/ppermute | solution.py:659
  23.4 34.2 %collective-permute-start.2 = (bf16[5504,128]{1,0:T(8,128)(2,1)S(1)}, bf16[5504,128]{1,0:T(8,128)(2,1)}, u32[]{:S(2)}, u32[]{:S(2)}) collective-permute-start(bf16[5504,128]{1,0:T(8,128)(2,1)S(1)} %slice.39.refs_0_), channel_id=1, source_target_pairs={{8,0},{16,8},{24,16},{9,1},{17,9},{25,17},{10,2},{18,10},{26,18},{... | collective-permute-start | bytes 4227080 | tf_op jit(solution)/shard_map/ppermute | solution.py:660
  57.8 4.3 %collective-permute-start.8 = (bf16[5504,128]{1,0:T(8,128)(2,1)}, bf16[5504,128]{1,0:T(8,128)(2,1)}, u32[]{:S(2)}, u32[]{:S(2)}) collective-permute-start(bf16[5504,128]{1,0:T(8,128)(2,1)} %collective-permute-done.1.refs_0_), channel_id=1, source_target_pairs={{0,2},{2,0},{4,6},{6,4},{1,3},{3,1},{5,7},{7,5},{8,10},{10,8},{12,... | collective-permute-start | bytes 4227080 | tf_op jit(solution)/shard_map/ppermute | solution.py:635
  59.0 5.2 %collective-permute-start.7 = (bf16[5504,128]{1,0:T(8,128)(2,1)}, bf16[5504,128]{1,0:T(8,128)(2,1)}, u32[]{:S(2)}, u32[]{:S(2)}) collective-permute-start(bf16[5504,128]{1,0:T(8,128)(2,1)} %collective-permute-done.2.refs_0_), channel_id=1, source_target_pairs={{0,2},{2,0},{4,6},{6,4},{1,3},{3,1},{5,7},{7,5},{8,10},{10,8},{12,... | collective-permute-start | bytes 4227080 | tf_op jit(solution)/shard_map/ppermute | solution.py:635
  59.1 20.7 %collective-permute-start.5 = (bf16[5504,128]{1,0:T(8,128)(2,1)}, bf16[5504,128]{1,0:T(8,128)(2,1)S(1)}, u32[]{:S(2)}, u32[]{:S(2)}) collective-permute-start(bf16[5504,128]{1,0:T(8,128)(2,1)} %collective-permute-done.1.refs_0_), channel_id=1, source_target_pairs={{8,16},{16,24},{9,17},{17,25},{10,18},{18,26},{11,19},{19,27},{12,... | collective-permute-start | bytes 4227080 | tf_op jit(solution)/shard_map/ppermute | solution.py:667
  59.8 35.4 %collective-permute-start.6 = (bf16[5504,128]{1,0:T(8,128)(2,1)}, bf16[5504,128]{1,0:T(8,128)(2,1)S(1)}, u32[]{:S(2)}, u32[]{:S(2)}) collective-permute-start(bf16[5504,128]{1,0:T(8,128)(2,1)} %collective-permute-done.2.refs_0_), channel_id=1, source_target_pairs={{8,0},{16,8},{9,1},{17,9},{10,2},{18,10},{11,3},{19,11},{12,4},{20... | collective-permute-start | bytes 4227080 | tf_op jit(solution)/shard_map/ppermute | solution.py:668
  61.1 35.5 %collective-permute-start.10 = (s16[192,2176]{1,0:T(8,128)(2,1)}, s16[192,2176]{1,0:T(8,128)(2,1)S(1)}, u32[]{:S(2)}, u32[]{:S(2)}) collective-permute-start(s16[192,2176]{1,0:T(8,128)(2,1)} %copy-done.4), channel_id=1, source_target_pairs={{4,0},{12,10},{16,20},{24,30},{5,1},{13,11},{17,21},{25,31}} | collective-permute-start | bytes 2506760 | tf_op jit(solution)/shard_map/ppermute | solution.py:623
  62.1 34.6 %collective-permute-start.9 = (s16[192,2176]{1,0:T(8,128)(2,1)}, s16[192,2176]{1,0:T(8,128)(2,1)S(1)}, u32[]{:S(2)}, u32[]{:S(2)}) collective-permute-start(s16[192,2176]{1,0:T(8,128)(2,1)} %copy-done.3), channel_id=1, source_target_pairs={{2,0},{8,10},{22,20},{28,30},{3,1},{9,11},{23,21},{29,31}} | collective-permute-start | bytes 2506760 | tf_op jit(solution)/shard_map/ppermute | solution.py:623
  64.1 32.5 %collective-permute-start.11 = (s16[128,2176]{1,0:T(8,128)(2,1)S(1)}, s16[128,2176]{1,0:T(8,128)(2,1)S(1)}, u32[]{:S(2)}, u32[]{:S(2)}) collective-permute-start(s16[128,2176]{1,0:T(8,128)(2,1)S(1)} %copy-done.6), channel_id=1, source_target_pairs={{6,0},{14,10},{18,20},{26,30},{7,1},{15,11},{19,21},{27,31}} | collective-permute-start | bytes 1671176 | tf_op jit(solution)/shard_map/ppermute | solution.py:623
  95.2 6.2 %collective-permute-start.16 = (bf16[5504,128]{1,0:T(8,128)(2,1)S(1)}, bf16[5504,128]{1,0:T(8,128)(2,1)S(1)}, u32[]{:S(2)}, u32[]{:S(2)}) collective-permute-start(bf16[5504,128]{1,0:T(8,128)(2,1)S(1)} %collective-permute-done.5.refs_0_), channel_id=1, source_target_pairs={{0,2},{2,0},{4,6},{6,4},{1,3},{3,1},{5,7},{7,5},{8,10},{10,8},{12,... | collective-permute-start | bytes 4227080 | tf_op jit(solution)/shard_map/ppermute | solution.py:635
  96.5 5.7 %collective-permute-start.17 = (bf16[5504,128]{1,0:T(8,128)(2,1)S(1)}, bf16[5504,128]{1,0:T(8,128)(2,1)S(1)}, u32[]{:S(2)}, u32[]{:S(2)}) collective-permute-start(bf16[5504,128]{1,0:T(8,128)(2,1)S(1)} %collective-permute-done.6.refs_2_), channel_id=1, source_target_pairs={{0,2},{2,0},{4,6},{6,4},{1,3},{3,1},{5,7},{7,5},{8,10},{10,8},{12,... | collective-permute-start | bytes 4227080 | tf_op jit(solution)/shard_map/ppermute | solution.py:635
  96.7 33.8 %collective-permute-start.12 = (bf16[5504,128]{1,0:T(8,128)(2,1)S(1)}, bf16[5504,128]{1,0:T(8,128)(2,1)S(1)}, u32[]{:S(2)}, u32[]{:S(2)}) collective-permute-start(bf16[5504,128]{1,0:T(8,128)(2,1)S(1)} %broadcast_select_fusion), channel_id=1, source_target_pairs={{16,24},{8,0},{17,25},{9,1},{18,26},{10,2},{19,27},{11,3},{20,28},... | collective-permute-start | bytes 4227080 | tf_op jit(solution)/shard_map/ppermute | solution.py:673
  98.0 18.8 %collective-permute-start.13 = (s16[192,2176]{1,0:T(8,128)(2,1)S(1)}, s16[192,2176]{1,0:T(8,128)(2,1)S(1)}, u32[]{:S(2)}, u32[]{:S(2)}) collective-permute-start(s16[192,2176]{1,0:T(8,128)(2,1)S(1)} %get-tuple-element.106), channel_id=1, source_target_pairs={{0,2},{10,8},{14,12},{16,18},{20,22},{30,28},{1,3},{11,9},{15,13},... | collective-permute-start | bytes 2506760 | tf_op jit(solution)/shard_map/ppermute | solution.py:623
  98.7 17.4 %collective-permute-start.15 = (s16[128,2176]{1,0:T(8,128)(2,1)S(1)}, s16[128,2176]{1,0:T(8,128)(2,1)S(1)}, u32[]{:S(2)}, u32[]{:S(2)}) collective-permute-start(s16[128,2176]{1,0:T(8,128)(2,1)S(1)} %get-tuple-element.108), channel_id=1, source_target_pairs={{6,2},{14,8},{10,12},{22,18},{18,22},{26,28},{7,3},{15,9},{11,13},... | collective-permute-start | bytes 1671176 | tf_op jit(solution)/shard_map/ppermute | solution.py:623
  101.5 16.1 %collective-permute-start.14 = (s16[192,2176]{1,0:T(8,128)(2,1)S(1)}, s16[192,2176]{1,0:T(8,128)(2,1)S(1)}, u32[]{:S(2)}, u32[]{:S(2)}) collective-permute-start(s16[192,2176]{1,0:T(8,128)(2,1)S(1)} %get-tuple-element.107), channel_id=1, source_target_pairs={{4,2},{12,8},{8,12},{20,18},{16,22},{24,28},{5,3},{13,9},{9,13},{2... | collective-permute-start | bytes 2506760 | tf_op jit(solution)/shard_map/ppermute | solution.py:623
  113.1 17.4 %collective-permute-start.18 = (s16[192,2176]{1,0:T(8,128)(2,1)S(1)}, s16[192,2176]{1,0:T(8,128)(2,1)S(1)}, u32[]{:S(2)}, u32[]{:S(2)}) collective-permute-start(s16[192,2176]{1,0:T(8,128)(2,1)S(1)} %get-tuple-element.110), channel_id=1, source_target_pairs={{6,4},{12,14},{18,16},{24,26},{7,5},{13,15},{19,17},{25,27}} | collective-permute-start | bytes 2506760 | tf_op jit(solution)/shard_map/ppermute | solution.py:623
  116.1 14.4 %collective-permute-start.19 = (s16[192,2176]{1,0:T(8,128)(2,1)S(1)}, s16[192,2176]{1,0:T(8,128)(2,1)S(1)}, u32[]{:S(2)}, u32[]{:S(2)}) collective-permute-start(s16[192,2176]{1,0:T(8,128)(2,1)S(1)} %get-tuple-element.111), channel_id=1, source_target_pairs={{0,4},{8,14},{20,16},{28,26},{1,5},{9,15},{21,17},{29,27}} | collective-permute-start | bytes 2506760 | tf_op jit(solution)/shard_map/ppermute | solution.py:623
  116.8 13.7 %collective-permute-start.20 = (s16[128,2176]{1,0:T(8,128)(2,1)S(1)}, s16[128,2176]{1,0:T(8,128)(2,1)S(1)}, u32[]{:S(2)}, u32[]{:S(2)}) collective-permute-start(s16[128,2176]{1,0:T(8,128)(2,1)S(1)} %get-tuple-element.112), channel_id=1, source_target_pairs={{2,4},{10,14},{22,16},{30,26},{3,5},{11,15},{23,17},{31,27}} | collective-permute-start | bytes 1671176 | tf_op jit(solution)/shard_map/ppermute | solution.py:623
  130.6 8.1 %collective-permute-start.21 = (bf16[5504,128]{1,0:T(8,128)(2,1)S(1)}, bf16[5504,128]{1,0:T(8,128)(2,1)S(1)}, u32[]{:S(2)}, u32[]{:S(2)}) collective-permute-start(bf16[5504,128]{1,0:T(8,128)(2,1)S(1)} %collective-permute-done.12.refs_0_), channel_id=1, source_target_pairs={{0,2},{2,0},{4,6},{6,4},{1,3},{3,1},{5,7},{7,5},{8,10},{10,8},{12,... | collective-permute-start | bytes 4227080 | tf_op jit(solution)/shard_map/ppermute | solution.py:635
  149.0 18.8 %collective-permute-start.22 = (s16[192,2176]{1,0:T(8,128)(2,1)S(1)}, s16[192,2176]{1,0:T(8,128)(2,1)S(1)}, u32[]{:S(2)}, u32[]{:S(2)}) collective-permute-start(s16[192,2176]{1,0:T(8,128)(2,1)S(1)} %get-tuple-element.119), channel_id=1, source_target_pairs={{4,6},{26,24},{5,7},{27,25}} | collective-permute-start | bytes 2506760 | tf_op jit(solution)/shard_map/ppermute | solution.py:623
  150.3 19.8 %collective-permute-start.23 = (s16[192,2176]{1,0:T(8,128)(2,1)S(1)}, s16[192,2176]{1,0:T(8,128)(2,1)S(1)}, u32[]{:S(2)}, u32[]{:S(2)}) collective-permute-start(s16[192,2176]{1,0:T(8,128)(2,1)S(1)} %get-tuple-element.120), channel_id=1, source_target_pairs={{0,6},{28,24},{1,7},{29,25}} | collective-permute-start | bytes 2506760 | tf_op jit(solution)/shard_map/ppermute | solution.py:623
  151.6 16.2 %collective-permute-start.24 = (s16[128,2176]{1,0:T(8,128)(2,1)S(1)}, s16[128,2176]{1,0:T(8,128)(2,1)S(1)}, u32[]{:S(2)}, u32[]{:S(2)}) collective-permute-start(s16[128,2176]{1,0:T(8,128)(2,1)S(1)} %get-tuple-element.121), channel_id=1, source_target_pairs={{2,6},{30,24},{3,7},{31,25}} | collective-permute-start | bytes 1671176 | tf_op jit(solution)/shard_map/ppermute | solution.py:623
  (14 other events, 160.6 us)
